TPU v7x, 32 devices: a whole 2x2x4 slice. The times are simulated.
32 devices in a mesh: tm: 4 (over z), space: 8 (over y, x, core).
Axes of the slice: x: 2, y: 2, z: 4, core: 2. Of those that a mesh axis runs over, the one named last changes fastest.
Arguments:
- c_state: float32 [4, 2, 64, 2048], P('tm', None, 'space'), may hold values from -4 to 4
Outputs:
- next_state: float32 [4, 2, 64, 2048], P('tm', None, 'space')
All inputs are finite; a program needn't handle non-finite values.
Results may differ from a plain program's by a relative error of at most 0.00002.
Values sent between devices are 32-bit elements; how exact they have to be, the bound alone decides.
No kernel may reach another device: no remote copies, remote signals or barrier semaphores. Data moves between devices by JAX's collectives and lax.ppermute only.
A program may use at most 64 MiB of HBM per device.

v0:
```python
import jax
import jax.numpy as jnp
from jax import lax
from jax.sharding import PartitionSpec as P

FSTEPS = 4
CF = 4


COURANT = 0.06
DIFFUSION = 0.04


def padded_2(block, sides, width):
    for axis, dim in sides:
        count = lax.axis_size(axis)
        forward = [(i, i + 1) for i in range(count - 1)]
        forward.append((count - 1, 0))
        backward = [(target, source) for source, target in forward]
        low = lax.ppermute(
            lax.slice_in_dim(block, block.shape[dim] - width, None, axis=dim), axis, forward
        )
        high = lax.ppermute(lax.slice_in_dim(block, 0, width, axis=dim), axis, backward)
        block = jnp.concatenate([low, block, high], axis=dim)
    return block


def advance(padded, courant, diffusion):
    center = padded[:, 1:-1]
    row_above = padded[:, :-2]
    row_below = padded[:, 2:]
    col_left = jnp.roll(center, 1, axis=2)
    col_right = jnp.roll(center, -1, axis=2)
    along_u = center[0:1]
    along_v = center[1:2]
    transport = jnp.maximum(along_u, 0.0) * (center - row_above) + jnp.minimum(along_u, 0.0) * (
        row_below - center
    )
    transport = (
        transport
        + jnp.maximum(along_v, 0.0) * (center - col_left)
        + jnp.minimum(along_v, 0.0) * (col_right - center)
    )
    spread = row_above + row_below + col_left + col_right - 4.0 * center
    return center - courant * transport + diffusion * spread


def restrict(field):
    blocks = field.reshape(field.shape[0], field.shape[1] // CF, CF, field.shape[2] // CF, CF)
    return jnp.mean(blocks, axis=(2, 4))


def prolong(field):
    return jnp.repeat(jnp.repeat(field, CF, axis=1), CF, axis=2)


def coarse_step(field):
    padded = padded_2(field, (("space", 1),), 1)
    return advance(padded, COURANT * FSTEPS / CF, DIFFUSION * FSTEPS / (CF * CF))


def body(c_state):
    field = c_state[0]
    for section_index in range(FSTEPS):
        padded = padded_2(field, (("space", 1),), 1)
        field = advance(padded, COURANT, DIFFUSION)
    start_coarse = restrict(c_state[0])
    end_coarse = restrict(field)
    defect = end_coarse - coarse_step(start_coarse)
    group_index = lax.axis_index("tm")
    all_start, all_defect = (
        lax.all_gather(start_coarse[None], "tm", axis=0, tiled=True),
        lax.all_gather(defect[None], "tm", axis=0, tiled=True),
    )

    def chain_step(carry, defect_term):
        advanced = coarse_step(carry) + defect_term
        return (advanced, advanced)

    unused, coarse_path = lax.scan(chain_step, all_start[0], all_defect)
    reached = lax.dynamic_index_in_dim(coarse_path, group_index, 0, keepdims=False)
    next_state = field + prolong(reached - end_coarse)
    return next_state[None]


def solution(mesh):
    placed = (P("tm", None, "space", None),)
    return jax.shard_map(
        body, mesh=mesh, in_specs=placed, out_specs=P("tm", None, "space", None), check_vma=False
    )
```

profile of v0, /device:TPU:0, one launch (start us, length us, event | category | flops | bytes accessed | tf_op | source)
XLA Modules:
  0.0 84.8 jit_solution(13688418001067768919)
XLA Ops:
  0.0 1.0 %fusion.74 = (f32[2,1,2048]{2,1,0:T(1,128)S(1)}, f32[2,1,2048]{2,1,0:T(1,128)S(1)}) fusion(f32[2,8,2048]{2,1,0:T(8,128)} %bitcast.68), kind=kLoop, calls=%fused_computation.128 | loop fusion | bytes 65536 | tf_op jit(solution)/shard_map/slice | solution.py:21
  1.0 0.5 collective-permute-start.2
  1.6 2.9 %collective-permute-start.3 = (f32[2,1,2048]{2,0,1:T(2,128)S(1)}, f32[2,1,2048]{2,0,1:T(2,128)S(1)}, u32[]{:S(2)}, u32[]{:S(2)}) collective-permute-start(f32[2,1,2048]{2,0,1:T(2,128)S(1)} %copy.154), channel_id=1, source_target_pairs={{1,0},{2,1},{3,2},{4,3},{5,4},{6,5},{7,6},{0,7},{9,8},{10,9},{11,1... | collective-permute-start | bytes 49160 | tf_op jit(solution)/shard_map/ppermute | solution.py:23
  4.5 6.5 %reshape_squeeze.3 = f32[2,2,4,512,4]{4,3,2,1,0:T(8,128)} reshape(f32[1,2,8,2048]{3,2,1,0:T(8,128)} %param.3) | data formatting | bytes 262144 | tf_op jit(solution)/shard_map/reshape;squeeze | solution.py:49
  11.0 2.5 %reduce_sum.18 = f32[2,2,512]{2,1,0:T(2,128)S(1)} reduce(f32[2,2,4,512,4]{4,3,2,1,0:T(8,128)} %reshape_squeeze.3, f32[]{:T(128)} %constant.9.clone.1), dimensions={2,4}, to_apply=%region_0.1 | reduce | flops 30720 | bytes 139268 | tf_op jit(solution)/shard_map/reduce_sum | solution.py:50
  13.6 0.1 collective-permute-start.10
  13.7 2.6 %collective-permute-start.11 = (f32[2,1,512]{2,1,0:T(1,128)S(1)}, f32[2,1,512]{2,1,0:T(1,128)S(1)}, u32[]{:S(2)}, u32[]{:S(2)}) collective-permute-start(f32[2,1,512]{2,1,0:T(1,128)S(1)} %get-tuple-element.93), channel_id=1, source_target_pairs={{1,0},{2,1},{3,2},{4,3},{5,4},{6,5},{7,6},{0,7},{9,8},{10,9},{11,1... | collective-permute-start | bytes 12296 | tf_op jit(solution)/shard_map/ppermute | solution.py:23
  16.3 0.1 fusion.73
  16.4 0.1 fusion.72
  16.5 0.1 fusion.77
  16.6 0.1 fusion.76
  16.7 14.1 %all-gather = f32[8,2,512]{2,1,0:T(2,128)S(1)} all-gather(f32[2,2,512]{2,1,0:T(2,128)S(1)} %broadcast_multiply_fusion), channel_id=2, replica_groups=mesh['tm'=4,'space'=8] {'tm'}, dimensions={0}, use_global_device_ids=true | all-gather | bytes 40960 | tf_op jit(solution)/shard_map/all_gather | solution.py:72
  30.8 0.2 fusion.51
  31.0 0.1 fusion.70
  31.3 2.7 %collective-permute-start.5 = (f32[2,1,2048]{2,0,1:T(2,128)S(1)}, f32[2,1,2048]{2,0,1:T(2,128)S(1)}, u32[]{:S(2)}, u32[]{:S(2)}) collective-permute-start(f32[2,1,2048]{2,0,1:T(2,128)S(1)} %copy.158), channel_id=1, source_target_pairs={{1,0},{2,1},{3,2},{4,3},{5,4},{6,5},{7,6},{0,7},{9,8},{10,9},{11,1... | collective-permute-start | bytes 49160 | tf_op jit(solution)/shard_map/ppermute | solution.py:23
  33.9 0.1 fusion.69
  34.0 1.3 %collective-permute-done.4 = f32[2,1,2048]{2,0,1:T(2,128)S(1)} collective-permute-done((f32[2,1,2048]{2,0,1:T(2,128)S(1)}, f32[2,1,2048]{2,0,1:T(2,128)S(1)}, u32[]{:S(2)}, u32[]{:S(2)}) %collective-permute-start.4) | collective-permute-done | bytes 16416 | tf_op jit(solution)/shard_map/ppermute | solution.py:20
  35.4 0.2 fusion.36
  35.6 0.1 fusion.67
  35.8 2.7 %collective-permute-start.7 = (f32[2,1,2048]{2,0,1:T(2,128)S(1)}, f32[2,1,2048]{2,0,1:T(2,128)S(1)}, u32[]{:S(2)}, u32[]{:S(2)}) collective-permute-start(f32[2,1,2048]{2,0,1:T(2,128)S(1)} %copy.162), channel_id=1, source_target_pairs={{1,0},{2,1},{3,2},{4,3},{5,4},{6,5},{7,6},{0,7},{9,8},{10,9},{11,1... | collective-permute-start | bytes 49160 | tf_op jit(solution)/shard_map/ppermute | solution.py:23
  38.5 0.1 fusion.66
  38.6 1.3 %collective-permute-done.6 = f32[2,1,2048]{2,0,1:T(2,128)S(1)} collective-permute-done((f32[2,1,2048]{2,0,1:T(2,128)S(1)}, f32[2,1,2048]{2,0,1:T(2,128)S(1)}, u32[]{:S(2)}, u32[]{:S(2)}) %collective-permute-start.6) | collective-permute-done | bytes 16416 | tf_op jit(solution)/shard_map/ppermute | solution.py:20
  39.9 0.1 collective-permute-done.7
  40.0 0.2 fusion.21
  40.2 0.1 fusion.64
  40.3 0.6 collective-permute-start.8
  40.9 2.1 %collective-permute-start.9 = (f32[2,1,2048]{2,0,1:T(2,128)S(1)}, f32[2,1,2048]{2,0,1:T(2,128)S(1)}, u32[]{:S(2)}, u32[]{:S(2)}) collective-permute-start(f32[2,1,2048]{2,0,1:T(2,128)S(1)} %copy.166), channel_id=1, source_target_pairs={{1,0},{2,1},{3,2},{4,3},{5,4},{6,5},{7,6},{0,7},{9,8},{10,9},{11,1... | collective-permute-start | bytes 49160 | tf_op jit(solution)/shard_map/ppermute | solution.py:23
  43.1 0.1 fusion.63
  43.1 1.3 %collective-permute-done.8 = f32[2,1,2048]{2,0,1:T(2,128)S(1)} collective-permute-done((f32[2,1,2048]{2,0,1:T(2,128)S(1)}, f32[2,1,2048]{2,0,1:T(2,128)S(1)}, u32[]{:S(2)}, u32[]{:S(2)}) %collective-permute-start.8) | collective-permute-done | bytes 16416 | tf_op jit(solution)/shard_map/ppermute | solution.py:20
  44.4 0.1 collective-permute-done.9
  44.5 0.2 fusion.6
  44.7 5.7 %reshape.56 = f32[2,2,4,512,4]{4,3,2,1,0:T(8,128)} reshape(f32[2,8,2048]{2,1,0:T(8,128)S(1)} %fusion.6) | data formatting | bytes 262144 | tf_op jit(solution)/shard_map/reshape | solution.py:49
  50.4 2.5 %reduce_sum.19 = f32[2,2,512]{2,1,0:T(2,128)S(1)} reduce(f32[2,2,4,512,4]{4,3,2,1,0:T(8,128)} %reshape.56, f32[]{:T(128)} %constant.9.clone.1), dimensions={2,4}, to_apply=%region_1.2 | reduce | flops 30720 | bytes 139268 | tf_op jit(solution)/shard_map/reduce_sum | solution.py:50
  52.9 0.1 add_subtract_fusion
  53.0 13.1 %all-gather.1 = f32[8,2,512]{2,1,0:T(2,128)S(1)} all-gather(f32[2,2,512]{2,1,0:T(2,128)S(1)} %add_subtract_fusion), channel_id=3, replica_groups=mesh['tm'=4,'space'=8] {'tm'}, dimensions={0}, use_global_device_ids=true | all-gather | bytes 40960 | tf_op jit(solution)/shard_map/all_gather | solution.py:73
  66.2 16.7 %while.12 = (s32[]{:T(128)}, f32[2,2,512]{2,1,0:T(2,128)S(1)}, f32[4,2,2,512]{3,2,1,0:T(2,128)S(1)}, f32[4,2,2,512]{3,2,1,0:T(2,128)S(1)}, s32[]{:T(128)}) while((s32[]{:T(128)}, f32[2,2,512]{2,1,0:T(2,128)S(1)}, f32[4,2,2,512]{3,2,1,0:T(2,128)S(1)}, f32[4,2,2,512]{3,2,1,0:T(2,128)S(1)}, s32[]{:T(128)}) %tuple.68), condition=%wide.region_3.4_spmd, body=%wide.region_2.3_spmd.sunk | while | flops 55298 | bytes 200857 | solution.py:80
  66.3 0.5 collective-permute-start.1
  66.8 0.1 fusion.82
  66.8 0.1 fusion.81
  66.9 0.7 collective-permute-done
  67.6 2.7 %collective-permute-done.1 = f32[2,1,512]{2,1,0:T(1,128)S(1)} collective-permute-done((f32[2,1,512]{2,1,0:T(1,128)S(1)}, f32[2,1,512]{2,1,0:T(1,128)S(1)}, u32[]{:S(2)}, u32[]{:S(2)}) %collective-permute-start.1) | collective-permute-done | bytes 4128 | tf_op jit(solution)/shard_map/while/body/eval_jaxpr/ppermute | solution.py:20
  70.2 0.1 bitcast_dynamic-update-slice_fusion.2
  70.4 0.5 collective-permute-start.1
  70.9 0.1 fusion.82
  71.0 0.1 fusion.81
  71.1 0.7 collective-permute-done
  71.8 2.7 %collective-permute-done.1 = f32[2,1,512]{2,1,0:T(1,128)S(1)} collective-permute-done((f32[2,1,512]{2,1,0:T(1,128)S(1)}, f32[2,1,512]{2,1,0:T(1,128)S(1)}, u32[]{:S(2)}, u32[]{:S(2)}) %collective-permute-start.1) | collective-permute-done | bytes 4128 | tf_op jit(solution)/shard_map/while/body/eval_jaxpr/ppermute | solution.py:20
  74.4 0.1 bitcast_dynamic-update-slice_fusion.2
  74.6 0.5 collective-permute-start.1
  75.1 0.1 fusion.82
  75.2 0.1 fusion.81
  75.3 0.7 collective-permute-done
  76.0 2.7 %collective-permute-done.1 = f32[2,1,512]{2,1,0:T(1,128)S(1)} collective-permute-done((f32[2,1,512]{2,1,0:T(1,128)S(1)}, f32[2,1,512]{2,1,0:T(1,128)S(1)}, u32[]{:S(2)}, u32[]{:S(2)}) %collective-permute-start.1) | collective-permute-done | bytes 4128 | tf_op jit(solution)/shard_map/while/body/eval_jaxpr/ppermute | solution.py:20
  78.6 0.1 bitcast_dynamic-update-slice_fusion.2
  78.8 0.5 collective-permute-start.1
  79.3 0.1 fusion.82
  79.4 0.1 fusion.81
  79.5 0.7 collective-permute-done
  80.1 2.7 %collective-permute-done.1 = f32[2,1,512]{2,1,0:T(1,128)S(1)} collective-permute-done((f32[2,1,512]{2,1,0:T(1,128)S(1)}, f32[2,1,512]{2,1,0:T(1,128)S(1)}, u32[]{:S(2)}, u32[]{:S(2)}) %collective-permute-start.1) | collective-permute-done | bytes 4128 | tf_op jit(solution)/shard_map/while/body/eval_jaxpr/ppermute | solution.py:20
  82.8 0.1 bitcast_dynamic-update-slice_fusion.2
  83.0 0.2 copy.169
  83.2 0.4 broadcast_in_dim.23
  83.5 0.6 copy.170
  84.1 0.7 add_bitcast_fusion
  (56 shorter events, 0.9 us)
Async XLA Ops:
  1.0 29.8 %collective-permute-start.2 = (f32[2,1,2048]{2,0,1:T(2,128)S(1)}, f32[2,1,2048]{2,0,1:T(2,128)S(1)}, u32[]{:S(2)}, u32[]{:S(2)}) collective-permute-start(f32[2,1,2048]{2,0,1:T(2,128)S(1)} %copy.152), channel_id=1, source_target_pairs={{0,1},{1,2},{2,3},{3,4},{4,5},{5,6},{6,7},{7,0},{8,9},{9,10},{10,1... | collective-permute-start | bytes 49160 | tf_op jit(solution)/shard_map/ppermute | solution.py:20
  1.6 14.7 %copy-start = (f32[1,2,8,2048]{3,2,1,0:T(8,128)S(1)}, f32[1,2,8,2048]{3,2,1,0:T(8,128)}, u32[]{:S(2)}) copy-start(f32[1,2,8,2048]{3,2,1,0:T(8,128)} %param.3) | copy-start | bytes 393220
  1.6 29.2 %collective-permute-start.3 = (f32[2,1,2048]{2,0,1:T(2,128)S(1)}, f32[2,1,2048]{2,0,1:T(2,128)S(1)}, u32[]{:S(2)}, u32[]{:S(2)}) collective-permute-start(f32[2,1,2048]{2,0,1:T(2,128)S(1)} %copy.154), channel_id=1, source_target_pairs={{1,0},{2,1},{3,2},{4,3},{5,4},{6,5},{7,6},{0,7},{9,8},{10,9},{11,1... | collective-permute-start | bytes 49160 | tf_op jit(solution)/shard_map/ppermute | solution.py:23
  13.6 39.3 %collective-permute-start.10 = (f32[2,1,512]{2,1,0:T(1,128)S(1)}, f32[2,1,512]{2,1,0:T(1,128)S(1)}, u32[]{:S(2)}, u32[]{:S(2)}) collective-permute-start(f32[2,1,512]{2,1,0:T(1,128)S(1)} %get-tuple-element.92), channel_id=1, source_target_pairs={{0,1},{1,2},{2,3},{3,4},{4,5},{5,6},{6,7},{7,0},{8,9},{9,10},{10,1... | collective-permute-start | bytes 12296 | tf_op jit(solution)/shard_map/ppermute | solution.py:20
  13.7 39.3 %collective-permute-start.11 = (f32[2,1,512]{2,1,0:T(1,128)S(1)}, f32[2,1,512]{2,1,0:T(1,128)S(1)}, u32[]{:S(2)}, u32[]{:S(2)}) collective-permute-start(f32[2,1,512]{2,1,0:T(1,128)S(1)} %get-tuple-element.93), channel_id=1, source_target_pairs={{1,0},{2,1},{3,2},{4,3},{5,4},{6,5},{7,6},{0,7},{9,8},{10,9},{11,1... | collective-permute-start | bytes 12296 | tf_op jit(solution)/shard_map/ppermute | solution.py:23
  31.2 4.2 %collective-permute-start.4 = (f32[2,1,2048]{2,0,1:T(2,128)S(1)}, f32[2,1,2048]{2,0,1:T(2,128)S(1)}, u32[]{:S(2)}, u32[]{:S(2)}) collective-permute-start(f32[2,1,2048]{2,0,1:T(2,128)S(1)} %copy.156), channel_id=1, source_target_pairs={{0,1},{1,2},{2,3},{3,4},{4,5},{5,6},{6,7},{7,0},{8,9},{9,10},{10,1... | collective-permute-start | bytes 49160 | tf_op jit(solution)/shard_map/ppermute | solution.py:20
  31.3 4.1 %collective-permute-start.5 = (f32[2,1,2048]{2,0,1:T(2,128)S(1)}, f32[2,1,2048]{2,0,1:T(2,128)S(1)}, u32[]{:S(2)}, u32[]{:S(2)}) collective-permute-start(f32[2,1,2048]{2,0,1:T(2,128)S(1)} %copy.158), channel_id=1, source_target_pairs={{1,0},{2,1},{3,2},{4,3},{5,4},{6,5},{7,6},{0,7},{9,8},{10,9},{11,1... | collective-permute-start | bytes 49160 | tf_op jit(solution)/shard_map/ppermute | solution.py:23
  35.7 4.1 %collective-permute-start.6 = (f32[2,1,2048]{2,0,1:T(2,128)S(1)}, f32[2,1,2048]{2,0,1:T(2,128)S(1)}, u32[]{:S(2)}, u32[]{:S(2)}) collective-permute-start(f32[2,1,2048]{2,0,1:T(2,128)S(1)} %copy.160), channel_id=1, source_target_pairs={{0,1},{1,2},{2,3},{3,4},{4,5},{5,6},{6,7},{7,0},{8,9},{9,10},{10,1... | collective-permute-start | bytes 49160 | tf_op jit(solution)/shard_map/ppermute | solution.py:20
  35.8 4.1 %collective-permute-start.7 = (f32[2,1,2048]{2,0,1:T(2,128)S(1)}, f32[2,1,2048]{2,0,1:T(2,128)S(1)}, u32[]{:S(2)}, u32[]{:S(2)}) collective-permute-start(f32[2,1,2048]{2,0,1:T(2,128)S(1)} %copy.162), channel_id=1, source_target_pairs={{1,0},{2,1},{3,2},{4,3},{5,4},{6,5},{7,6},{0,7},{9,8},{10,9},{11,1... | collective-permute-start | bytes 49160 | tf_op jit(solution)/shard_map/ppermute | solution.py:23
  40.3 4.1 %collective-permute-start.8 = (f32[2,1,2048]{2,0,1:T(2,128)S(1)}, f32[2,1,2048]{2,0,1:T(2,128)S(1)}, u32[]{:S(2)}, u32[]{:S(2)}) collective-permute-start(f32[2,1,2048]{2,0,1:T(2,128)S(1)} %copy.164), channel_id=1, source_target_pairs={{0,1},{1,2},{2,3},{3,4},{4,5},{5,6},{6,7},{7,0},{8,9},{9,10},{10,1... | collective-permute-start | bytes 49160 | tf_op jit(solution)/shard_map/ppermute | solution.py:20
  40.9 3.6 %collective-permute-start.9 = (f32[2,1,2048]{2,0,1:T(2,128)S(1)}, f32[2,1,2048]{2,0,1:T(2,128)S(1)}, u32[]{:S(2)}, u32[]{:S(2)}) collective-permute-start(f32[2,1,2048]{2,0,1:T(2,128)S(1)} %copy.166), channel_id=1, source_target_pairs={{1,0},{2,1},{3,2},{4,3},{5,4},{6,5},{7,6},{0,7},{9,8},{10,9},{11,1... | collective-permute-start | bytes 49160 | tf_op jit(solution)/shard_map/ppermute | solution.py:23
  66.2 1.4 %collective-permute-start = (f32[2,1,512]{2,1,0:T(1,128)S(1)}, f32[2,1,512]{2,1,0:T(1,128)S(1)}, u32[]{:S(2)}, u32[]{:S(2)}) collective-permute-start(f32[2,1,512]{2,1,0:T(1,128)S(1)} %get-tuple-element.141), channel_id=1, source_target_pairs={{1,0},{2,1},{3,2},{4,3},{5,4},{6,5},{7,6},{0,7},{9,8},{10,9},{11,1... | collective-permute-start | bytes 12296 | tf_op jit(solution)/shard_map/while/body/eval_jaxpr/ppermute | solution.py:23
  66.3 4.0 %collective-permute-start.1 = (f32[2,1,512]{2,1,0:T(1,128)S(1)}, f32[2,1,512]{2,1,0:T(1,128)S(1)}, u32[]{:S(2)}, u32[]{:S(2)}) collective-permute-start(f32[2,1,512]{2,1,0:T(1,128)S(1)} %get-tuple-element.143), channel_id=1, source_target_pairs={{0,1},{1,2},{2,3},{3,4},{4,5},{5,6},{6,7},{7,0},{8,9},{9,10},{10,1... | collective-permute-start | bytes 12296 | tf_op jit(solution)/shard_map/while/body/eval_jaxpr/ppermute | solution.py:20
  70.4 1.4 %collective-permute-start = (f32[2,1,512]{2,1,0:T(1,128)S(1)}, f32[2,1,512]{2,1,0:T(1,128)S(1)}, u32[]{:S(2)}, u32[]{:S(2)}) collective-permute-start(f32[2,1,512]{2,1,0:T(1,128)S(1)} %get-tuple-element.141), channel_id=1, source_target_pairs={{1,0},{2,1},{3,2},{4,3},{5,4},{6,5},{7,6},{0,7},{9,8},{10,9},{11,1... | collective-permute-start | bytes 12296 | tf_op jit(solution)/shard_map/while/body/eval_jaxpr/ppermute | solution.py:23
  70.4 4.0 %collective-permute-start.1 = (f32[2,1,512]{2,1,0:T(1,128)S(1)}, f32[2,1,512]{2,1,0:T(1,128)S(1)}, u32[]{:S(2)}, u32[]{:S(2)}) collective-permute-start(f32[2,1,512]{2,1,0:T(1,128)S(1)} %get-tuple-element.143), channel_id=1, source_target_pairs={{0,1},{1,2},{2,3},{3,4},{4,5},{5,6},{6,7},{7,0},{8,9},{9,10},{10,1... | collective-permute-start | bytes 12296 | tf_op jit(solution)/shard_map/while/body/eval_jaxpr/ppermute | solution.py:20
  74.6 1.4 %collective-permute-start = (f32[2,1,512]{2,1,0:T(1,128)S(1)}, f32[2,1,512]{2,1,0:T(1,128)S(1)}, u32[]{:S(2)}, u32[]{:S(2)}) collective-permute-start(f32[2,1,512]{2,1,0:T(1,128)S(1)} %get-tuple-element.141), channel_id=1, source_target_pairs={{1,0},{2,1},{3,2},{4,3},{5,4},{6,5},{7,6},{0,7},{9,8},{10,9},{11,1... | collective-permute-start | bytes 12296 | tf_op jit(solution)/shard_map/while/body/eval_jaxpr/ppermute | solution.py:23
  74.6 4.0 %collective-permute-start.1 = (f32[2,1,512]{2,1,0:T(1,128)S(1)}, f32[2,1,512]{2,1,0:T(1,128)S(1)}, u32[]{:S(2)}, u32[]{:S(2)}) collective-permute-start(f32[2,1,512]{2,1,0:T(1,128)S(1)} %get-tuple-element.143), channel_id=1, source_target_pairs={{0,1},{1,2},{2,3},{3,4},{4,5},{5,6},{6,7},{7,0},{8,9},{9,10},{10,1... | collective-permute-start | bytes 12296 | tf_op jit(solution)/shard_map/while/body/eval_jaxpr/ppermute | solution.py:20
  78.8 1.4 %collective-permute-start = (f32[2,1,512]{2,1,0:T(1,128)S(1)}, f32[2,1,512]{2,1,0:T(1,128)S(1)}, u32[]{:S(2)}, u32[]{:S(2)}) collective-permute-start(f32[2,1,512]{2,1,0:T(1,128)S(1)} %get-tuple-element.141), channel_id=1, source_target_pairs={{1,0},{2,1},{3,2},{4,3},{5,4},{6,5},{7,6},{0,7},{9,8},{10,9},{11,1... | collective-permute-start | bytes 12296 | tf_op jit(solution)/shard_map/while/body/eval_jaxpr/ppermute | solution.py:23
  78.8 4.0 %collective-permute-start.1 = (f32[2,1,512]{2,1,0:T(1,128)S(1)}, f32[2,1,512]{2,1,0:T(1,128)S(1)}, u32[]{:S(2)}, u32[]{:S(2)}) collective-permute-start(f32[2,1,512]{2,1,0:T(1,128)S(1)} %get-tuple-element.143), channel_id=1, source_target_pairs={{0,1},{1,2},{2,3},{3,4},{4,5},{5,6},{6,7},{7,0},{8,9},{9,10},{10,1... | collective-permute-start | bytes 12296 | tf_op jit(solution)/shard_map/while/body/eval_jaxpr/ppermute | solution.py:20
where the time goes:
time: 85.1 us; the launch traced here: 84.8 us
  blocking collectives  27.3 us (32%)
  waiting for transfers between devices  17.4 us (20%)
  starting transfers between devices  16.6 us (20%)
  local copies, waits for them, and re-layouts  16 us (19%)
  other arithmetic  7.04 us (8%)
    ppermute x9, waiting for transfers between devices, padded_2(): lax.ppermute(lax.slice_in_dim(block, block.shape[dim] - width, None, axis...  14.6 us
    all_gather x1, blocking collectives, body(): lax.all_gather(start_coarse[None], 'tm', axis=0, tiled=True)  14.1 us
    ppermute x9, starting transfers between devices, padded_2(): lax.ppermute(lax.slice_in_dim(block, 0, width, axis=dim), axis, backward)  13.3 us
    all_gather x1, blocking collectives, body(): lax.all_gather(defect[None], 'tm', axis=0, tiled=True)  13.1 us
    another operation x1, local copies, waits for them, and re-layouts, restrict(): field.reshape(field.shape[0], field.shape[1] // CF, CF, field.shape[2] //...  6.49 us
    reshape x1, local copies, waits for them, and re-layouts, restrict(): field.reshape(field.shape[0], field.shape[1] // CF, CF, field.shape[2] //...  5.67 us
    reduce_sum x2, other arithmetic, restrict(): return jnp.mean(blocks, axis=(2, 4))  5.09 us
    ppermute x9, starting transfers between devices, padded_2(): lax.ppermute(lax.slice_in_dim(block, block.shape[dim] - width, None, axis...  3.32 us
  transfers between devices with their start and end apart: 18, of which 13 were waited for; matrix products, arithmetic and copies ran while one was open for 23% of the time, Pallas kernels for 0%

commit v1 on v0

v1 whole, which is shorter than its diff:
```python
import functools

import jax
import jax.numpy as jnp
from jax import lax
from jax.experimental import pallas as pl
from jax.experimental.pallas import tpu as pltpu
from jax.sharding import PartitionSpec as P

FSTEPS = 4
CF = 4
COURANT = 0.06
DIFFUSION = 0.04
COARSE_COURANT = COURANT * FSTEPS / CF
COARSE_DIFFUSION = DIFFUSION * FSTEPS / (CF * CF)
EXT = 1
HALO = FSTEPS + CF * EXT
LANES = 128
VMEM = pl.BlockSpec(memory_space=pltpu.VMEM)
HIGHEST = lax.Precision.HIGHEST


def shifted(field, amount, axis):
    return pltpu.roll(field, amount % field.shape[axis], axis)


def advance(fields, courant, diffusion, pitch):
    u, v = fields
    along_u, along_v = courant * u, courant * v
    above = jnp.maximum(along_u, 0.0) + diffusion
    below = above - along_u
    left = jnp.maximum(along_v, 0.0) + diffusion
    right = left - along_v
    center = 1.0 - ((above + below) + (left + right))
    return [
        center * q
        + (above * shifted(q, pitch, 0) + below * shifted(q, -pitch, 0))
        + (left * shifted(q, 1, 1) + right * shifted(q, -1, 1))
        for q in fields
    ]


def column_means(field):
    fine = CF * LANES
    rows = lax.broadcasted_iota(jnp.int32, (fine, LANES), 0)
    cols = lax.broadcasted_iota(jnp.int32, (fine, LANES), 1)
    weights = jnp.where(rows // CF == cols, 1.0 / (CF * CF), 0.0).astype(jnp.float32)
    pieces = [field[:, at : at + fine] for at in range(0, field.shape[1], fine)]
    stacked = jnp.concatenate(pieces, axis=0)
    sums = jnp.dot(stacked, weights, precision=HIGHEST, preferred_element_type=jnp.float32)
    count = field.shape[0]
    return jnp.concatenate([sums[i * count : (i + 1) * count] for i in range(len(pieces))], axis=1)


def group_rows(field):
    total, step = field, 1
    while step < CF:
        total = total + shifted(total, -step, 0)
        step *= 2
    return total


def spread(tile):
    fine = CF * LANES
    rows = lax.broadcasted_iota(jnp.int32, (LANES, fine), 0)
    cols = lax.broadcasted_iota(jnp.int32, (LANES, fine), 1)
    weights = jnp.where(cols // CF == rows, 1.0, 0.0).astype(jnp.float32)
    pieces = [tile[:, at : at + LANES] for at in range(0, tile.shape[1], LANES)]
    stacked = jnp.concatenate(pieces, axis=0)
    wide = jnp.dot(stacked, weights, precision=HIGHEST, preferred_element_type=jnp.float32)
    count = tile.shape[0]
    return jnp.concatenate([wide[i * count : (i + 1) * count] for i in range(len(pieces))], axis=1)


def repeat_rows(field, first, pitch, count):
    cols = field.shape[1]
    return jnp.concatenate(
        [
            jnp.broadcast_to(field[first + m * pitch : first + m * pitch + 1], (CF, cols))
            for m in range(count // CF)
        ],
        axis=0,
    )


def fine_kernel(near_ref, own_ref, far_ref, sent_ref, base_ref):
    rows = own_ref.shape[1]
    odd = lax.axis_index("space") % 2 == 1
    first_group = lax.axis_index("tm") == 0
    fields = []
    for q in range(2):
        near, far = near_ref[q], far_ref[q]
        low, high = jnp.where(odd, near, far), jnp.where(odd, far, near)
        fields.append(jnp.concatenate([low, own_ref[q], high], axis=0))
    start = [group_rows(column_means(q)) for q in fields]
    for _ in range(FSTEPS):
        fields = advance(fields, COURANT, DIFFUSION, 1)
    end = [group_rows(column_means(q)) for q in fields]
    coarse = advance(start, COARSE_COURANT, COARSE_DIFFUSION, CF)
    for q in range(2):
        defect = end[q] - coarse[q]
        sent = jnp.where(first_group, coarse[q] + defect, defect)
        for m in range(rows // CF + 2 * EXT):
            at = HALO - CF * EXT + CF * m
            sent_ref[q, m : m + 1, :] = sent[at : at + 1]
        lifted = spread(repeat_rows(end[q], HALO, CF, rows))
        base_ref[q] = fields[q][HALO : HALO + rows] - lifted


def window_kernel(depth, own_ref, near_ref, far_ref, *rest):
    others, window_ref = rest[:-1], rest[-1]
    odd = lax.axis_index("space") % 2 == 1
    inner = own_ref.shape[1] - 2 * EXT
    for q in range(2):
        near, far = near_ref[q], far_ref[q]
        low, high = [jnp.where(odd, near, far)], [jnp.where(odd, far, near)]
        low += [others[2 * d][q] for d in range(depth - 1)]
        high += [others[2 * d + 1][q] for d in range(depth - 1)]
        parts = [low[-1][: EXT + inner]]
        parts += [part[EXT : EXT + inner] for part in reversed(low[:-1])]
        parts += [own_ref[q, EXT : EXT + inner]]
        parts += [part[EXT : EXT + inner] for part in high[:-1]]
        parts += [high[-1][EXT:]]
        window_ref[q] = jnp.concatenate(parts, axis=0)


def chain_kernel(base_ref, *rest):
    held, out_ref = rest[:-1], rest[-1]
    groups = len(held)
    group = lax.axis_index("tm")

    def of(index):
        wanted = lax.bitwise_xor(group, index)
        picked = [held[0][q] for q in range(2)]
        for k in range(1, groups):
            picked = [jnp.where(wanted == k, held[k][q], picked[q]) for q in range(2)]
        return picked

    path = of(0)
    for index in range(1, groups):
        term = of(index)
        after = advance(path, COARSE_COURANT, COARSE_DIFFUSION, 1)
        path = [jnp.where(index <= group, after[q] + term[q], path[q]) for q in range(2)]
    rows = base_ref.shape[1]
    first = (path[0].shape[0] - rows // CF) // 2
    for q in range(2):
        out_ref[q] = base_ref[q] + spread(repeat_rows(path[q], first, 1, rows))


def call(kernel, shapes, *operands):
    return pl.pallas_call(
        kernel,
        out_shape=[jax.ShapeDtypeStruct(shape, jnp.float32) for shape in shapes],
        in_specs=[VMEM] * len(operands),
        out_specs=[VMEM] * len(shapes),
        compiler_params=pltpu.CompilerParams(vmem_limit_bytes=16 * 1024 * 1024),
    )(*operands)


def exchange(near_block, far_block):
    count = lax.axis_size("space")
    far = [(i, (i + 1 if i % 2 else i - 1) % count) for i in range(count)]
    near = [(i, i ^ 1) for i in range(count)]
    from_far = lax.ppermute(far_block, "space", far)
    from_near = lax.ppermute(near_block, "space", near)
    return from_near, from_far


def body(c_state):
    own = c_state[0]
    rows, cols = own.shape[1:]
    count, groups = lax.axis_size("space"), lax.axis_size("tm")
    assert rows == HALO and count % 2 == 0 and groups & (groups - 1) == 0
    inner, wide = rows // CF, cols // CF
    near, far = exchange(own, own)
    sent, base = call(fine_kernel, [(2, inner + 2 * EXT, wide), own.shape], near, own, far)
    reach = groups - 1
    depth = -(-(reach - EXT) // inner)
    pieces = [sent, *exchange(sent, sent)]
    for d in range(2, depth + 1):
        for sign in (1, -1):
            pairs = [(i, (i + sign * d) % count) for i in range(count)]
            pieces.append(lax.ppermute(sent, "space", pairs))
    (window,) = call(
        functools.partial(window_kernel, depth), [(2, inner * (2 * depth + 1) + 2 * EXT, wide)], *pieces
    )
    held = [window] + [None] * (groups - 1)
    for k in range(groups - 1, 0, -1):
        held[k] = lax.ppermute(window, "tm", [(i, i ^ k) for i in range(groups)])
    (after,) = call(chain_kernel, [own.shape], base, *held)
    return after[None]


def solution(mesh):
    placed = (P("tm", None, "space", None),)
    return jax.shard_map(
        body, mesh=mesh, in_specs=placed, out_specs=P("tm", None, "space", None), check_vma=False
    )
```

time: 85.1 us -> 25.6 us (0.30)
  blocking collectives: 27.3 us -> 0 us
  local copies, waits for them, and re-layouts: 16 us -> 0.91 us
  waiting for transfers between devices: 17.4 us -> 9.11 us
  other arithmetic: 7.04 us -> 0 us
  starting transfers between devices: 16.6 us -> 11.8 us
  Pallas kernels: 0 us -> 3.67 us
    all_gather x2 -> x0, blocking collectives: 27.3 us -> none  [the longest x1 14.1 us: body(): lax.all_gather(start_coarse[None], 'tm', axis=0, tiled=True)]
    ppermute x18 -> x7, waiting for transfers between devices: 17.4 us -> 9.11 us  [the longest x2 4.94 us: exchange(): from_far = lax.ppermute(far_block, 'space', far)]
    another operation x1 -> x0, local copies, waits for them, and re-layouts: 6.49 us -> none  [restrict(): field.reshape(field.shape[0], field.shape[1] // CF, CF, field.shape[2] //...]
    reshape x3 -> x0, local copies, waits for them, and re-layouts: 6.43 us -> none  [the longest x1 5.67 us: restrict(): field.reshape(field.shape[0], field.shape[1] // CF, CF, field.shape[2] //...]
    reduce_sum x2 -> x0, other arithmetic: 5.09 us -> none  [restrict(): return jnp.mean(blocks, axis=(2, 4))]
    ppermute x18 -> x7, starting transfers between devices: 16.6 us -> 11.8 us  [the longest x2 5.93 us: exchange(): from_far = lax.ppermute(far_block, 'space', far)]
    pallas_call x0 -> x3, Pallas kernels: none -> 3.67 us  [call(): pl.pallas_call(kernel, out_shape=[jax.ShapeDtypeStruct(shape, jnp.float32...]
    slice x36 -> x0, local copies, waits for them, and re-layouts: 2.58 us -> none  [the longest x18 1.38 us: advance(): col_left = jnp.roll(center, 1, axis=2)]
  transfers between devices with their start and end apart: 18 -> 7, of which waited for: 13 -> 4; matrix products, arithmetic and copies ran while one was open for 23% -> 0% of each run, Pallas kernels for 0% -> 0%
where the time goes in v1:
time: 25.6 us; the launch traced here: 25.5 us
  starting transfers between devices  11.8 us (46%)
  waiting for transfers between devices  9.11 us (36%)
  Pallas kernels  3.67 us (14%)
  local copies, waits for them, and re-layouts  0.91 us (4%)
    ppermute x2, starting transfers between devices, exchange(): from_far = lax.ppermute(far_block, 'space', far)  5.93 us
    ppermute x3, starting transfers between devices, body(): held[k] = lax.ppermute(window, 'tm', [(i, i ^ k) for i in range(groups)])  5.82 us
    ppermute x2, waiting for transfers between devices, exchange(): from_far = lax.ppermute(far_block, 'space', far)  4.94 us
    ppermute x3, waiting for transfers between devices, body(): held[k] = lax.ppermute(window, 'tm', [(i, i ^ k) for i in range(groups)])  4.17 us
    pallas_call x3, Pallas kernels, call(): pl.pallas_call(kernel, out_shape=[jax.ShapeDtypeStruct(shape, jnp.float32...  3.67 us
    unnamed x2, local copies, waits for them, and re-layouts  0.91 us
  transfers between devices with their start and end apart: 7, of which 4 were waited for; matrix products, arithmetic and copies ran while one was open for 0% of the time, Pallas kernels for 0%

profile of v1, /device:TPU:0, one launch (start us, length us, event | category | flops | bytes accessed | tf_op | source)
XLA Modules:
  0.0 25.5 jit_solution(10171071096143331007)
XLA Ops:
  0.0 3.4 %collective-permute-start.1 = (f32[2,8,2048]{2,1,0:T(8,128)}, f32[2,8,2048]{2,1,0:T(8,128)S(1)}, u32[]{:S(2)}, u32[]{:S(2)}) collective-permute-start(f32[2,8,2048]{2,1,0:T(8,128)} %bitcast.2), channel_id=1, source_target_pairs={{0,7},{1,2},{2,1},{3,4},{4,3},{5,6},{6,5},{7,0},{8,15},{9,10},{10,... | collective-permute-start | bytes 393224 | tf_op jit(solution)/shard_map/ppermute | solution.py:164
  3.4 0.0 collective-permute-start
  3.4 3.4 %collective-permute-done.1.far_ref = f32[2,8,2048]{2,1,0:T(8,128)S(1)} collective-permute-done((f32[2,8,2048]{2,1,0:T(8,128)}, f32[2,8,2048]{2,1,0:T(8,128)S(1)}, u32[]{:S(2)}, u32[]{:S(2)}) %collective-permute-start.1) | collective-permute-done | bytes 131104 | tf_op jit(solution)/shard_map/ppermute | solution.py:164
  6.8 0.0 collective-permute-done.near_ref
  6.8 0.0 copy-start
  6.8 0.9 %copy-done = f32[1,2,8,2048]{3,2,1,0:T(8,128)S(1)} copy-done((f32[1,2,8,2048]{3,2,1,0:T(8,128)S(1)}, f32[1,2,8,2048]{3,2,1,0:T(8,128)}, u32[]{:S(2)}) %copy-start) | copy-done | bytes 131096
  7.7 2.4 %shard_map.17 = (f32[2,4,512]{2,1,0:T(4,128)S(1)}, f32[2,8,2048]{2,1,0:T(8,128)S(1)}) custom-call(f32[2,8,2048]{2,1,0:T(8,128)S(1)} %collective-permute-done.near_ref, f32[2,8,2048]{2,1,0:T(8,128)S(1)} %bitcast.4, f32[2,8,2048]{2,1,0:T(8,128)S(1)} %collective-permute-done.1.far_ref), custom_call_target="tpu_custom_call" | custom-call | tf_op jit(solution)/shard_map/pallas_call | solution.py:151
  10.1 2.6 %collective-permute-start.3 = (f32[2,4,512]{2,1,0:T(4,128)S(1)}, f32[2,4,512]{2,1,0:T(4,128)S(1)}, u32[]{:S(2)}, u32[]{:S(2)}) collective-permute-start(f32[2,4,512]{2,1,0:T(4,128)S(1)} %get-tuple-element.8.own_ref), channel_id=1, source_target_pairs={{0,7},{1,2},{2,1},{3,4},{4,3},{5,6},{6,5},{7,0},{8,15},{9,10},{10,... | collective-permute-start | bytes 49160 | tf_op jit(solution)/shard_map/ppermute | solution.py:164
  12.7 0.0 collective-permute-start.2
  12.7 1.5 %collective-permute-done.3.far_ref = f32[2,4,512]{2,1,0:T(4,128)S(1)} collective-permute-done((f32[2,4,512]{2,1,0:T(4,128)S(1)}, f32[2,4,512]{2,1,0:T(4,128)S(1)}, u32[]{:S(2)}, u32[]{:S(2)}) %collective-permute-start.3) | collective-permute-done | bytes 16416 | tf_op jit(solution)/shard_map/ppermute | solution.py:164
  14.2 0.0 collective-permute-done.2.near_ref
  14.2 5.2 %collective-permute-start.6 = (f32[2,8,512]{2,1,0:T(8,128)S(1)}, f32[2,8,512]{2,1,0:T(8,128)S(1)}, u32[]{:S(2)}, u32[]{:S(2)}) collective-permute-start(f32[2,8,512]{2,1,0:T(8,128)S(1)} %shard_map.18.rest_0_), channel_id=1, source_target_pairs={{0,24},{8,16},{16,8},{24,0},{1,25},{9,17},{17,9},{25,1},{2,26},{10... | collective-permute-start | bytes 98312 | tf_op jit(solution)/shard_map/ppermute | solution.py:189
  19.4 0.0 collective-permute-start.5
  19.4 0.6 %collective-permute-start.4 = (f32[2,8,512]{2,1,0:T(8,128)S(1)}, f32[2,8,512]{2,1,0:T(8,128)S(1)}, u32[]{:S(2)}, u32[]{:S(2)}) collective-permute-start(f32[2,8,512]{2,1,0:T(8,128)S(1)} %shard_map.18.rest_0_), channel_id=1, source_target_pairs={{0,8},{8,0},{16,24},{24,16},{1,9},{9,1},{17,25},{25,17},{2,10},{10... | collective-permute-start | bytes 98312 | tf_op jit(solution)/shard_map/ppermute | solution.py:189
  20.1 1.4 %collective-permute-done.6.rest_3_ = f32[2,8,512]{2,1,0:T(8,128)S(1)} collective-permute-done((f32[2,8,512]{2,1,0:T(8,128)S(1)}, f32[2,8,512]{2,1,0:T(8,128)S(1)}, u32[]{:S(2)}, u32[]{:S(2)}) %collective-permute-start.6) | collective-permute-done | bytes 32800 | tf_op jit(solution)/shard_map/ppermute | solution.py:189
  21.4 2.8 %collective-permute-done.5.rest_2_ = f32[2,8,512]{2,1,0:T(8,128)S(1)} collective-permute-done((f32[2,8,512]{2,1,0:T(8,128)S(1)}, f32[2,8,512]{2,1,0:T(8,128)S(1)}, u32[]{:S(2)}, u32[]{:S(2)}) %collective-permute-start.5) | collective-permute-done | bytes 32800 | tf_op jit(solution)/shard_map/ppermute | solution.py:189
  24.2 0.0 collective-permute-done.4.rest_1_
  24.2 1.2 %shard_map.19 = f32[2,8,2048]{2,1,0:T(8,128)} custom-call(f32[2,8,2048]{2,1,0:T(8,128)S(1)} %get-tuple-element.7.base_ref, f32[2,8,512]{2,1,0:T(8,128)S(1)} %shard_map.18.rest_0_, f32[2,8,512]{2,1,0:T(8,128)S(1)} %collective-permute-done.4.rest_1_, f32[2,8,512]{2,1,0:T(8,128)S(1)} %collective-permute-done.5.rest_2_, ...), custom_call_target="tpu_custom_call" | custom-call | tf_op jit(solution)/shard_map/pallas_call | solution.py:151
  (1 shorter events, 0.0 us)
Async XLA Ops:
  0.0 6.8 %collective-permute-start.1 = (f32[2,8,2048]{2,1,0:T(8,128)}, f32[2,8,2048]{2,1,0:T(8,128)S(1)}, u32[]{:S(2)}, u32[]{:S(2)}) collective-permute-start(f32[2,8,2048]{2,1,0:T(8,128)} %bitcast.2), channel_id=1, source_target_pairs={{0,7},{1,2},{2,1},{3,4},{4,3},{5,6},{6,5},{7,0},{8,15},{9,10},{10,... | collective-permute-start | bytes 393224 | tf_op jit(solution)/shard_map/ppermute | solution.py:164
  3.4 3.4 %collective-permute-start = (f32[2,8,2048]{2,1,0:T(8,128)}, f32[2,8,2048]{2,1,0:T(8,128)S(1)}, u32[]{:S(2)}, u32[]{:S(2)}) collective-permute-start(f32[2,8,2048]{2,1,0:T(8,128)} %bitcast.3), channel_id=1, source_target_pairs={{0,1},{1,0},{2,3},{3,2},{4,5},{5,4},{6,7},{7,6},{8,9},{9,8},{10,11... | collective-permute-start | bytes 393224 | tf_op jit(solution)/shard_map/ppermute | solution.py:165
  6.8 0.9 %copy-start = (f32[1,2,8,2048]{3,2,1,0:T(8,128)S(1)}, f32[1,2,8,2048]{3,2,1,0:T(8,128)}, u32[]{:S(2)}) copy-start(f32[1,2,8,2048]{3,2,1,0:T(8,128)} %param.1) | copy-start | bytes 393220
  10.1 4.1 %collective-permute-start.3 = (f32[2,4,512]{2,1,0:T(4,128)S(1)}, f32[2,4,512]{2,1,0:T(4,128)S(1)}, u32[]{:S(2)}, u32[]{:S(2)}) collective-permute-start(f32[2,4,512]{2,1,0:T(4,128)S(1)} %get-tuple-element.8.own_ref), channel_id=1, source_target_pairs={{0,7},{1,2},{2,1},{3,4},{4,3},{5,6},{6,5},{7,0},{8,15},{9,10},{10,... | collective-permute-start | bytes 49160 | tf_op jit(solution)/shard_map/ppermute | solution.py:164
  12.7 1.5 %collective-permute-start.2 = (f32[2,4,512]{2,1,0:T(4,128)S(1)}, f32[2,4,512]{2,1,0:T(4,128)S(1)}, u32[]{:S(2)}, u32[]{:S(2)}) collective-permute-start(f32[2,4,512]{2,1,0:T(4,128)S(1)} %get-tuple-element.8.own_ref), channel_id=1, source_target_pairs={{0,1},{1,0},{2,3},{3,2},{4,5},{5,4},{6,7},{7,6},{8,9},{9,8},{10,11... | collective-permute-start | bytes 49160 | tf_op jit(solution)/shard_map/ppermute | solution.py:165
  14.2 7.2 %collective-permute-start.6 = (f32[2,8,512]{2,1,0:T(8,128)S(1)}, f32[2,8,512]{2,1,0:T(8,128)S(1)}, u32[]{:S(2)}, u32[]{:S(2)}) collective-permute-start(f32[2,8,512]{2,1,0:T(8,128)S(1)} %shard_map.18.rest_0_), channel_id=1, source_target_pairs={{0,24},{8,16},{16,8},{24,0},{1,25},{9,17},{17,9},{25,1},{2,26},{10... | collective-permute-start | bytes 98312 | tf_op jit(solution)/shard_map/ppermute | solution.py:189
  19.4 4.8 %collective-permute-start.5 = (f32[2,8,512]{2,1,0:T(8,128)S(1)}, f32[2,8,512]{2,1,0:T(8,128)S(1)}, u32[]{:S(2)}, u32[]{:S(2)}) collective-permute-start(f32[2,8,512]{2,1,0:T(8,128)S(1)} %shard_map.18.rest_0_), channel_id=1, source_target_pairs={{0,16},{8,24},{16,0},{24,8},{1,17},{9,25},{17,1},{25,9},{2,18},{10... | collective-permute-start | bytes 98312 | tf_op jit(solution)/shard_map/ppermute | solution.py:189
  19.4 4.8 %collective-permute-start.4 = (f32[2,8,512]{2,1,0:T(8,128)S(1)}, f32[2,8,512]{2,1,0:T(8,128)S(1)}, u32[]{:S(2)}, u32[]{:S(2)}) collective-permute-start(f32[2,8,512]{2,1,0:T(8,128)S(1)} %shard_map.18.rest_0_), channel_id=1, source_target_pairs={{0,8},{8,0},{16,24},{24,16},{1,9},{9,1},{17,25},{25,17},{2,10},{10... | collective-permute-start | bytes 98312 | tf_op jit(solution)/shard_map/ppermute | solution.py:189

commit v2 on v1

v2 whole, which is shorter than its diff:
```python
import functools

import jax
import jax.numpy as jnp
from jax import lax
from jax.experimental import pallas as pl
from jax.experimental.pallas import tpu as pltpu
from jax.sharding import PartitionSpec as P

FSTEPS = 4
CF = 4
COURANT = 0.06
DIFFUSION = 0.04
COARSE_COURANT = COURANT * FSTEPS / CF
COARSE_DIFFUSION = DIFFUSION * FSTEPS / (CF * CF)
EXT = 1
HALO = FSTEPS + CF * EXT
LANES = 128
VMEM = pl.BlockSpec(memory_space=pltpu.VMEM)
ROWS = 8


def shifted(field, amount, axis):
    return pltpu.roll(field, amount % field.shape[axis], axis)


def advance(fields, courant, diffusion, pitch):
    u, v = fields
    along_u, along_v = courant * u, courant * v
    above = jnp.maximum(along_u, 0.0) + diffusion
    below = above - along_u
    left = jnp.maximum(along_v, 0.0) + diffusion
    right = left - along_v
    center = 1.0 - ((above + below) + (left + right))
    return [
        center * q
        + (above * shifted(q, pitch, 0) + below * shifted(q, -pitch, 0))
        + (left * shifted(q, 1, 1) + right * shifted(q, -1, 1))
        for q in fields
    ]


def exact_dot(field, weights):
    total = None
    for part in range(3):
        piece = field.astype(jnp.bfloat16)
        if part < 2:
            field = field - piece.astype(jnp.float32)
        product = jnp.dot(piece, weights, preferred_element_type=jnp.float32)
        total = product if total is None else total + product
    return total


def block_weights(shape, value):
    long = 0 if shape[0] > shape[1] else 1
    at = lax.broadcasted_iota(jnp.int32, shape, long)
    to = lax.broadcasted_iota(jnp.int32, shape, 1 - long)
    return jnp.where(at // CF == to, value, 0.0).astype(jnp.bfloat16)


def by_pieces(field, weights):
    width, count = weights.shape[0], field.shape[0]
    pieces = [field[:, at : at + width] for at in range(0, field.shape[1], width)]
    done = exact_dot(jnp.concatenate(pieces, axis=0), weights)
    return jnp.concatenate([done[i * count : (i + 1) * count] for i in range(len(pieces))], axis=1)


def packed_sums(tiles):
    packed = None
    for i, tile in enumerate(tiles):
        total = tile + shifted(tile, -1, 0)
        total = total + shifted(total, -2, 0)
        if packed is None:
            packed = total
        else:
            row = lax.broadcasted_iota(jnp.int32, tile.shape, 0)
            packed = jnp.where(row % CF == i, shifted(total, i, 0), packed)
    return packed


def sums_of(means, i):
    return [means[i : i + 1], means[CF + i : CF + i + 1]]


def repeat_rows(first, second):
    cols = first.shape[1]
    row = lax.broadcasted_iota(jnp.int32, (ROWS, cols), 0)
    return jnp.where(
        row < CF, jnp.broadcast_to(first, (ROWS, cols)), jnp.broadcast_to(second, (ROWS, cols))
    )


def near_kernel(
    near_ref, own_hbm, first_ref, second_ref, kept_ref, means_ref, gather_ref, spread_ref, own_ref, sem
):
    load = pltpu.make_async_copy(own_hbm, own_ref, sem)
    load.start()
    gather_ref[...] = block_weights(gather_ref.shape, 1.0 / (CF * CF))
    spread_ref[...] = block_weights(spread_ref.shape, 1.0)
    odd = lax.axis_index("space") % 2 == 1
    load.wait()
    fields = []
    for q in range(2):
        near, own = near_ref[q], own_ref[q]
        low, high = jnp.where(odd, near, own), jnp.where(odd, own, near)
        fields.append(jnp.concatenate([low, high], axis=0))
    near_sums = packed_sums([near_ref[0], near_ref[1], own_ref[0], own_ref[1]])
    for k in range(1, FSTEPS + 1):
        for q in range(2):
            own = jnp.where(odd, fields[q][ROWS:], fields[q][:ROWS])
            first_ref[k - 1, q] = pltpu.roll(own, jnp.where(odd, k, ROWS - k), 0)
            second_ref[k - 1, q] = pltpu.roll(own, jnp.where(odd, k + 1, ROWS - 1 - k), 0)
        fields = advance(fields, COURANT, DIFFUSION, 1)
    kept = [shifted(q, -CF, 0)[:ROWS] for q in fields]
    for q in range(2):
        kept_ref[q] = kept[q]
    end_sums = packed_sums(kept)
    both = by_pieces(jnp.concatenate([near_sums, end_sums], axis=0), gather_ref[...])
    means_ref[...] = both


def far_kernel(far_ref, first_ref, second_ref, means_ref, gather_ref, end_ref, sent_ref, ends_ref):
    odd = lax.axis_index("space") % 2 == 1
    first_group = lax.axis_index("tm") == 0
    sign = jnp.where(odd, 1.0, -1.0)
    turn = jnp.where(odd, 1, ROWS - 1)
    fields = [far_ref[0], far_ref[1]]
    starts = packed_sums(fields)
    row = lax.broadcasted_iota(jnp.int32, fields[0].shape, 0)
    edge = row == jnp.where(odd, 0, ROWS - 1)
    for k in range(FSTEPS):
        outer = fields
        fields = [jnp.where(edge, first_ref[k, q], pltpu.roll(outer[q], turn, 0)) for q in range(2)]
        inner = [jnp.where(edge, second_ref[k, q], pltpu.roll(fields[q], turn, 0)) for q in range(2)]
        along_u, along_v = (sign * COURANT) * fields[0], COURANT * fields[1]
        toward = jnp.maximum(along_u, 0.0) + DIFFUSION
        away = toward - along_u
        left = jnp.maximum(along_v, 0.0) + DIFFUSION
        right = left - along_v
        center = 1.0 - ((toward + away) + (left + right))
        fields = [
            center * fields[q]
            + (toward * inner[q] + away * outer[q])
            + (left * shifted(fields[q], 1, 1) + right * shifted(fields[q], -1, 1))
            for q in range(2)
        ]
    for q in range(2):
        end_ref[q] = fields[q]
    ends = packed_sums(fields)
    pack = jnp.where(row % CF < 2, ends, shifted(starts, 2, 0))
    far_means = by_pieces(pack, gather_ref[...])
    means = means_ref[...]
    near_means, near_ends = means[:ROWS], means[ROWS:]
    start, end = [], []
    for q in range(2):
        near, own, far = sums_of(near_means, q), sums_of(near_means, 2 + q), sums_of(far_means, 2 + q)
        this, that = sums_of(near_ends, q), sums_of(far_means, q)
        none = jnp.zeros_like(own[0])
        low = [jnp.where(odd, near[i], far[i]) for i in range(2)]
        high = [jnp.where(odd, far[i], near[i]) for i in range(2)]
        start.append(jnp.concatenate([*low, *own, *high, none, none], axis=0))
        low = [jnp.where(odd, this[i], that[i]) for i in range(2)]
        high = [jnp.where(odd, that[i], this[i]) for i in range(2)]
        end.append(jnp.concatenate([none, *low, *high, none, none, none], axis=0))
        ends_ref[q] = jnp.concatenate([low[1], high[0]], axis=0)
    coarse = advance(start, COARSE_COURANT, COARSE_DIFFUSION, 1)
    for q in range(2):
        defect = end[q] - coarse[q]
        sent = jnp.where(first_group, coarse[q] + defect, defect)
        sent_ref[q] = sent[EXT : EXT + 2 + 2 * EXT]


def window_kernel(depth, own_ref, near_ref, far_ref, *rest):
    others, window_ref = rest[:-1], rest[-1]
    odd = lax.axis_index("space") % 2 == 1
    inner = own_ref.shape[1] - 2 * EXT
    for q in range(2):
        near, far = near_ref[q], far_ref[q]
        low, high = [jnp.where(odd, near, far)], [jnp.where(odd, far, near)]
        low += [others[2 * d][q] for d in range(depth - 1)]
        high += [others[2 * d + 1][q] for d in range(depth - 1)]
        parts = [low[-1][: EXT + inner]]
        parts += [part[EXT : EXT + inner] for part in reversed(low[:-1])]
        parts += [own_ref[q, EXT : EXT + inner]]
        parts += [part[EXT : EXT + inner] for part in high[:-1]]
        parts += [high[-1][EXT:]]
        window_ref[q] = jnp.concatenate(parts, axis=0)


def chain_kernel(kept_ref, end_ref, ends_ref, spread_ref, *rest):
    held, out_ref = rest[:-1], rest[-1]
    groups = len(held)
    group = lax.axis_index("tm")

    def of(index):
        wanted = lax.bitwise_xor(group, index)
        picked = [held[0][q] for q in range(2)]
        for k in range(1, groups):
            picked = [jnp.where(wanted == k, held[k][q], picked[q]) for q in range(2)]
        return picked

    path = of(0)
    for index in range(1, groups):
        term = of(index)
        after = advance(path, COARSE_COURANT, COARSE_DIFFUSION, 1)
        path = [jnp.where(index <= group, after[q] + term[q], path[q]) for q in range(2)]
    first = (path[0].shape[0] - 2) // 2
    odd = lax.axis_index("space") % 2 == 1
    moves = []
    for q in range(2):
        move = path[q][first : first + 2] - ends_ref[q]
        moves.append(repeat_rows(move[:1], move[1:]))
    lifted = by_pieces(jnp.concatenate(moves, axis=0), spread_ref[...])
    for q in range(2):
        kept, end = kept_ref[q], end_ref[q]
        upper = lax.broadcasted_iota(jnp.int32, kept.shape, 0) >= CF
        own = shifted(jnp.where(upper == odd, kept, end), CF, 0)
        out_ref[q] = own + lifted[q * ROWS : (q + 1) * ROWS]


def call(kernel, shapes, operands, cost=0, hbm=(), scratch=()):
    where = [pl.BlockSpec(memory_space=pl.ANY) if i in hbm else VMEM for i in range(len(operands))]
    return pl.pallas_call(
        kernel,
        out_shape=[jax.ShapeDtypeStruct(shape, dtype) for shape, dtype in shapes],
        in_specs=where,
        out_specs=[VMEM] * len(shapes),
        scratch_shapes=scratch,
        cost_estimate=pl.CostEstimate(flops=cost, bytes_accessed=cost // 8, transcendentals=0),
        compiler_params=pltpu.CompilerParams(vmem_limit_bytes=16 * 1024 * 1024),
    )(*operands)


def exchange(near_block, far_block):
    count = lax.axis_size("space")
    far = [(i, (i + 1 if i % 2 else i - 1) % count) for i in range(count)]
    near = [(i, i ^ 1) for i in range(count)]
    from_far = lax.ppermute(far_block, "space", far)
    from_near = lax.ppermute(near_block, "space", near)
    return from_near, from_far


def body(c_state):
    own = c_state[0]
    rows, cols = own.shape[1:]
    count, groups = lax.axis_size("space"), lax.axis_size("tm")
    assert rows == HALO == ROWS and count % 2 == 0 and groups & (groups - 1) == 0
    full, half = jnp.float32, jnp.bfloat16
    inner, wide = rows // CF, cols // CF
    near, far = exchange(own, own)
    edges = ((FSTEPS, *own.shape), full)
    first, second, kept, means, gather, spread = call(
        near_kernel,
        [
            edges,
            edges,
            (own.shape, full),
            ((2 * ROWS, wide), full),
            ((CF * LANES, LANES), half),
            ((LANES, CF * LANES), half),
        ],
        (near, own),
        cost=8_000_000,
        hbm=(1,),
        scratch=[pltpu.VMEM(own.shape, full), pltpu.SemaphoreType.DMA],
    )
    end, sent, ends = call(
        far_kernel,
        [(own.shape, full), ((2, inner + 2 * EXT, wide), full), ((2, inner, wide), full)],
        (far, first, second, means, gather),
        cost=2_000_000,
    )
    reach = groups - 1
    depth = -(-(reach - EXT) // inner)
    pieces = [sent, *exchange(sent, sent)]
    for d in range(2, depth + 1):
        for sign in (1, -1):
            pairs = [(i, (i + sign * d) % count) for i in range(count)]
            pieces.append(lax.ppermute(sent, "space", pairs))
    (window,) = call(
        functools.partial(window_kernel, depth),
        [((2, inner * (2 * depth + 1) + 2 * EXT, wide), full)],
        pieces,
    )
    held = [window] + [None] * (groups - 1)
    for k in range(groups - 1, 0, -1):
        held[k] = lax.ppermute(window, "tm", [(i, i ^ k) for i in range(groups)])
    (after,) = call(chain_kernel, [(own.shape, full)], (kept, end, ends, spread, *held), cost=1_000_000)
    return after[None]


def solution(mesh):
    placed = (P("tm", None, "space", None),)
    return jax.shard_map(
        body, mesh=mesh, in_specs=placed, out_specs=P("tm", None, "space", None), check_vma=False
    )
```

time: 25.6 us -> 22.3 us (0.87)
  waiting for transfers between devices: 9.11 us -> 7.28 us
  starting transfers between devices: 11.8 us -> 10.7 us
  Pallas kernels: 3.67 us -> 3.25 us
    ppermute x2, waiting for transfers between devices: 4.94 us -> 3.11 us  [exchange(): from_far = lax.ppermute(far_block, 'space', far)]
    ppermute x3, starting transfers between devices: 5.82 us -> 4.51 us  [body(): held[k] = lax.ppermute(window, 'tm', [(i, i ^ k) for i in range(groups)])]
    ppermute x2, starting transfers between devices: 0.01 us -> 0.5 us  [exchange(): from_near = lax.ppermute(near_block, 'space', near)]
    pallas_call x3 -> x4, Pallas kernels: 3.67 us -> 3.25 us  [call(): pl.pallas_call(kernel, out_shape=[jax.ShapeDtypeStruct(shape, dtype) for...]
  transfers between devices with their start and end apart: 7 -> 7, of which waited for: 4 -> 4; matrix products, arithmetic and copies ran while one was open for 0% -> 0% of each run, Pallas kernels for 0% -> 6%
where the time goes in v2:
time: 22.3 us; the launch traced here: 22.2 us
  starting transfers between devices  10.7 us (48%)
  waiting for transfers between devices  7.28 us (33%)
  Pallas kernels  3.25 us (15%)
  local copies, waits for them, and re-layouts  0.93 us (4%)
    ppermute x2, starting transfers between devices, exchange(): from_far = lax.ppermute(far_block, 'space', far)  5.68 us
    ppermute x3, starting transfers between devices, body(): held[k] = lax.ppermute(window, 'tm', [(i, i ^ k) for i in range(groups)])  4.51 us
    ppermute x3, waiting for transfers between devices, body(): held[k] = lax.ppermute(window, 'tm', [(i, i ^ k) for i in range(groups)])  4.17 us
    pallas_call x4, Pallas kernels, call(): pl.pallas_call(kernel, out_shape=[jax.ShapeDtypeStruct(shape, dtype) for...  3.25 us
    ppermute x2, waiting for transfers between devices, exchange(): from_far = lax.ppermute(far_block, 'space', far)  3.11 us
    unnamed x2, local copies, waits for them, and re-layouts  0.93 us
    ppermute x2, starting transfers between devices, exchange(): from_near = lax.ppermute(near_block, 'space', near)  0.5 us
  transfers between devices with their start and end apart: 7, of which 4 were waited for; matrix products, arithmetic and copies ran while one was open for 0% of the time, Pallas kernels for 6%

profile of v2, /device:TPU:0, one launch (start us, length us, event | category | flops | bytes accessed | tf_op | source)
XLA Modules:
  0.0 22.2 jit_solution(2545289804661259334)
XLA Ops:
  0.0 0.5 %collective-permute-start = (f32[2,8,2048]{2,1,0:T(8,128)}, f32[2,8,2048]{2,1,0:T(8,128)S(1)}, u32[]{:S(2)}, u32[]{:S(2)}) collective-permute-start(f32[2,8,2048]{2,1,0:T(8,128)} %bitcast.2), channel_id=1, source_target_pairs={{0,1},{1,0},{2,3},{3,2},{4,5},{5,4},{6,7},{7,6},{8,9},{9,8},{10,11... | collective-permute-start | bytes 393224 | tf_op jit(solution)/shard_map/ppermute | solution.py:239
  0.5 3.5 %collective-permute-start.1 = (f32[2,8,2048]{2,1,0:T(8,128)}, f32[2,8,2048]{2,1,0:T(8,128)S(1)}, u32[]{:S(2)}, u32[]{:S(2)}) collective-permute-start(f32[2,8,2048]{2,1,0:T(8,128)} %bitcast.3), channel_id=1, source_target_pairs={{0,7},{1,2},{2,1},{3,4},{4,3},{5,6},{6,5},{7,0},{8,15},{9,10},{10,... | collective-permute-start | bytes 393224 | tf_op jit(solution)/shard_map/ppermute | solution.py:238
  4.0 0.0 collective-permute-done.near_ref
  4.0 0.0 copy-start
  4.0 0.9 %copy-done = f32[1,2,8,2048]{3,2,1,0:T(8,128)S(1)} copy-done((f32[1,2,8,2048]{3,2,1,0:T(8,128)S(1)}, f32[1,2,8,2048]{3,2,1,0:T(8,128)}, u32[]{:S(2)}) %copy-start) | copy-done | bytes 131096
  5.0 1.4 %shard_map.17 = (f32[4,2,8,2048]{3,2,1,0:T(8,128)S(1)}, f32[4,2,8,2048]{3,2,1,0:T(8,128)S(1)}, f32[2,8,2048]{2,1,0:T(8,128)S(1)}, f32[16,512]{1,0:T(8,128)S(1)},...) custom-call(f32[2,8,2048]{2,1,0:T(8,128)S(1)} %collective-permute-done.near_ref, f32[2,8,2048]{2,1,0:T(8,128)S(1)} %bitcast.4), custom_call_target="tpu_custom_call" | custom-call | flops 8000000 | bytes 1000000 | tf_op jit(solution)/shard_map/pallas_call | solution.py:223
  6.4 1.1 %collective-permute-done.1.far_ref = f32[2,8,2048]{2,1,0:T(8,128)S(1)} collective-permute-done((f32[2,8,2048]{2,1,0:T(8,128)}, f32[2,8,2048]{2,1,0:T(8,128)S(1)}, u32[]{:S(2)}, u32[]{:S(2)}) %collective-permute-start.1) | collective-permute-done | bytes 131104 | tf_op jit(solution)/shard_map/ppermute | solution.py:238
  7.5 0.8 %shard_map.18 = (f32[2,8,2048]{2,1,0:T(8,128)S(1)}, f32[2,4,512]{2,1,0:T(4,128)S(1)}, f32[2,2,512]{2,1,0:T(2,128)S(1)}) custom-call(f32[2,8,2048]{2,1,0:T(8,128)S(1)} %collective-permute-done.1.far_ref, f32[4,2,8,2048]{3,2,1,0:T(8,128)S(1)} %get-tuple-element.15.first_ref, f32[4,2,8,2048]{3,2,1,0:T(8,128)S(1)} %get-tuple-element.16.second_ref, ...), custom_call_target="tpu_custom_call" | custom-call | flops 2000000 | bytes 250000 | tf_op jit(solution)/shard_map/pallas_call | solution.py:223
  8.3 2.1 %collective-permute-start.3 = (f32[2,4,512]{2,1,0:T(4,128)S(1)}, f32[2,4,512]{2,1,0:T(4,128)S(1)}, u32[]{:S(2)}, u32[]{:S(2)}) collective-permute-start(f32[2,4,512]{2,1,0:T(4,128)S(1)} %get-tuple-element.22.own_ref), channel_id=1, source_target_pairs={{0,7},{1,2},{2,1},{3,4},{4,3},{5,6},{6,5},{7,0},{8,15},{9,10},{10,... | collective-permute-start | bytes 49160 | tf_op jit(solution)/shard_map/ppermute | solution.py:238
  10.4 0.0 collective-permute-start.2
  10.4 2.0 %collective-permute-done.3.far_ref = f32[2,4,512]{2,1,0:T(4,128)S(1)} collective-permute-done((f32[2,4,512]{2,1,0:T(4,128)S(1)}, f32[2,4,512]{2,1,0:T(4,128)S(1)}, u32[]{:S(2)}, u32[]{:S(2)}) %collective-permute-start.3) | collective-permute-done | bytes 16416 | tf_op jit(solution)/shard_map/ppermute | solution.py:238
  12.4 0.0 collective-permute-done.2.near_ref
  12.4 3.9 %collective-permute-start.6 = (f32[2,8,512]{2,1,0:T(8,128)S(1)}, f32[2,8,512]{2,1,0:T(8,128)S(1)}, u32[]{:S(2)}, u32[]{:S(2)}) collective-permute-start(f32[2,8,512]{2,1,0:T(8,128)S(1)} %shard_map.19.rest_0_), channel_id=1, source_target_pairs={{0,24},{8,16},{16,8},{24,0},{1,25},{9,17},{17,9},{25,1},{2,26},{10... | collective-permute-start | bytes 98312 | tf_op jit(solution)/shard_map/ppermute | solution.py:287
  16.3 0.0 collective-permute-start.5
  16.3 0.6 %collective-permute-start.4 = (f32[2,8,512]{2,1,0:T(8,128)S(1)}, f32[2,8,512]{2,1,0:T(8,128)S(1)}, u32[]{:S(2)}, u32[]{:S(2)}) collective-permute-start(f32[2,8,512]{2,1,0:T(8,128)S(1)} %shard_map.19.rest_0_), channel_id=1, source_target_pairs={{0,8},{8,0},{16,24},{24,16},{1,9},{9,1},{17,25},{25,17},{2,10},{10... | collective-permute-start | bytes 98312 | tf_op jit(solution)/shard_map/ppermute | solution.py:287
  16.9 1.5 %collective-permute-done.6.rest_3_ = f32[2,8,512]{2,1,0:T(8,128)S(1)} collective-permute-done((f32[2,8,512]{2,1,0:T(8,128)S(1)}, f32[2,8,512]{2,1,0:T(8,128)S(1)}, u32[]{:S(2)}, u32[]{:S(2)}) %collective-permute-start.6) | collective-permute-done | bytes 32800 | tf_op jit(solution)/shard_map/ppermute | solution.py:287
  18.5 2.6 %collective-permute-done.5.rest_2_ = f32[2,8,512]{2,1,0:T(8,128)S(1)} collective-permute-done((f32[2,8,512]{2,1,0:T(8,128)S(1)}, f32[2,8,512]{2,1,0:T(8,128)S(1)}, u32[]{:S(2)}, u32[]{:S(2)}) %collective-permute-start.5) | collective-permute-done | bytes 32800 | tf_op jit(solution)/shard_map/ppermute | solution.py:287
  21.1 0.0 collective-permute-done.4.rest_1_
  21.1 1.1 %shard_map.20 = f32[2,8,2048]{2,1,0:T(8,128)} custom-call(f32[2,8,2048]{2,1,0:T(8,128)S(1)} %get-tuple-element.14.kept_ref, f32[2,8,2048]{2,1,0:T(8,128)S(1)} %get-tuple-element.19.end_ref, f32[2,2,512]{2,1,0:T(2,128)S(1)} %get-tuple-element.20.ends_ref, bf16[128,512]{1,0:T(8,128)(2,1)S(1)} %get-tuple-element.21.spread_ref, ...), custom_call_target="tpu_custom_call" | custom-call | flops 1000000 | bytes 125000 | tf_op jit(solution)/shard_map/pallas_call | solution.py:223
  (1 shorter events, 0.0 us)
Async XLA Ops:
  0.0 4.0 %collective-permute-start = (f32[2,8,2048]{2,1,0:T(8,128)}, f32[2,8,2048]{2,1,0:T(8,128)S(1)}, u32[]{:S(2)}, u32[]{:S(2)}) collective-permute-start(f32[2,8,2048]{2,1,0:T(8,128)} %bitcast.2), channel_id=1, source_target_pairs={{0,1},{1,0},{2,3},{3,2},{4,5},{5,4},{6,7},{7,6},{8,9},{9,8},{10,11... | collective-permute-start | bytes 393224 | tf_op jit(solution)/shard_map/ppermute | solution.py:239
  0.5 7.0 %collective-permute-start.1 = (f32[2,8,2048]{2,1,0:T(8,128)}, f32[2,8,2048]{2,1,0:T(8,128)S(1)}, u32[]{:S(2)}, u32[]{:S(2)}) collective-permute-start(f32[2,8,2048]{2,1,0:T(8,128)} %bitcast.3), channel_id=1, source_target_pairs={{0,7},{1,2},{2,1},{3,4},{4,3},{5,6},{6,5},{7,0},{8,15},{9,10},{10,... | collective-permute-start | bytes 393224 | tf_op jit(solution)/shard_map/ppermute | solution.py:238
  4.0 0.9 %copy-start = (f32[1,2,8,2048]{3,2,1,0:T(8,128)S(1)}, f32[1,2,8,2048]{3,2,1,0:T(8,128)}, u32[]{:S(2)}) copy-start(f32[1,2,8,2048]{3,2,1,0:T(8,128)} %param.1) | copy-start | bytes 393220
  8.3 4.1 %collective-permute-start.3 = (f32[2,4,512]{2,1,0:T(4,128)S(1)}, f32[2,4,512]{2,1,0:T(4,128)S(1)}, u32[]{:S(2)}, u32[]{:S(2)}) collective-permute-start(f32[2,4,512]{2,1,0:T(4,128)S(1)} %get-tuple-element.22.own_ref), channel_id=1, source_target_pairs={{0,7},{1,2},{2,1},{3,4},{4,3},{5,6},{6,5},{7,0},{8,15},{9,10},{10,... | collective-permute-start | bytes 49160 | tf_op jit(solution)/shard_map/ppermute | solution.py:238
  10.4 2.0 %collective-permute-start.2 = (f32[2,4,512]{2,1,0:T(4,128)S(1)}, f32[2,4,512]{2,1,0:T(4,128)S(1)}, u32[]{:S(2)}, u32[]{:S(2)}) collective-permute-start(f32[2,4,512]{2,1,0:T(4,128)S(1)} %get-tuple-element.22.own_ref), channel_id=1, source_target_pairs={{0,1},{1,0},{2,3},{3,2},{4,5},{5,4},{6,7},{7,6},{8,9},{9,8},{10,11... | collective-permute-start | bytes 49160 | tf_op jit(solution)/shard_map/ppermute | solution.py:239
  12.4 6.1 %collective-permute-start.6 = (f32[2,8,512]{2,1,0:T(8,128)S(1)}, f32[2,8,512]{2,1,0:T(8,128)S(1)}, u32[]{:S(2)}, u32[]{:S(2)}) collective-permute-start(f32[2,8,512]{2,1,0:T(8,128)S(1)} %shard_map.19.rest_0_), channel_id=1, source_target_pairs={{0,24},{8,16},{16,8},{24,0},{1,25},{9,17},{17,9},{25,1},{2,26},{10... | collective-permute-start | bytes 98312 | tf_op jit(solution)/shard_map/ppermute | solution.py:287
  16.3 4.8 %collective-permute-start.5 = (f32[2,8,512]{2,1,0:T(8,128)S(1)}, f32[2,8,512]{2,1,0:T(8,128)S(1)}, u32[]{:S(2)}, u32[]{:S(2)}) collective-permute-start(f32[2,8,512]{2,1,0:T(8,128)S(1)} %shard_map.19.rest_0_), channel_id=1, source_target_pairs={{0,16},{8,24},{16,0},{24,8},{1,17},{9,25},{17,1},{25,9},{2,18},{10... | collective-permute-start | bytes 98312 | tf_op jit(solution)/shard_map/ppermute | solution.py:287
  16.3 4.8 %collective-permute-start.4 = (f32[2,8,512]{2,1,0:T(8,128)S(1)}, f32[2,8,512]{2,1,0:T(8,128)S(1)}, u32[]{:S(2)}, u32[]{:S(2)}) collective-permute-start(f32[2,8,512]{2,1,0:T(8,128)S(1)} %shard_map.19.rest_0_), channel_id=1, source_target_pairs={{0,8},{8,0},{16,24},{24,16},{1,9},{9,1},{17,25},{25,17},{2,10},{10... | collective-permute-start | bytes 98312 | tf_op jit(solution)/shard_map/ppermute | solution.py:287

commit v3 on v2

--- a/solution.py
+++ b/solution.py
@@ -6,6 +6,7 @@
 from jax.experimental import pallas as pl
 from jax.experimental.pallas import tpu as pltpu
 from jax.sharding import PartitionSpec as P
+
 
 FSTEPS = 4
 CF = 4
@@ -90,21 +91,27 @@
     )
 
 
-def near_kernel(
-    near_ref, own_hbm, first_ref, second_ref, kept_ref, means_ref, gather_ref, spread_ref, own_ref, sem
-):
+def ready_kernel(own_hbm, own_ref, sums_ref, gather_ref, spread_ref, sem):
     load = pltpu.make_async_copy(own_hbm, own_ref, sem)
     load.start()
     gather_ref[...] = block_weights(gather_ref.shape, 1.0 / (CF * CF))
     spread_ref[...] = block_weights(spread_ref.shape, 1.0)
+    load.wait()
+    sums_ref[...] = packed_sums([own_ref[0], own_ref[1]])
+
+
+def near_kernel(
+    near_ref, own_ref, sums_ref, gather_ref, first_ref, second_ref, kept_ref, means_ref
+):
     odd = lax.axis_index("space") % 2 == 1
-    load.wait()
     fields = []
     for q in range(2):
         near, own = near_ref[q], own_ref[q]
         low, high = jnp.where(odd, near, own), jnp.where(odd, own, near)
         fields.append(jnp.concatenate([low, high], axis=0))
-    near_sums = packed_sums([near_ref[0], near_ref[1], own_ref[0], own_ref[1]])
+    near_sums = packed_sums([near_ref[0], near_ref[1]])
+    row = lax.broadcasted_iota(jnp.int32, near_sums.shape, 0)
+    near_sums = jnp.where(row % CF < 2, near_sums, shifted(sums_ref[...], 2, 0))
     for k in range(1, FSTEPS + 1):
         for q in range(2):
             own = jnp.where(odd, fields[q][ROWS:], fields[q][:ROWS])
@@ -191,12 +198,22 @@
     held, out_ref = rest[:-1], rest[-1]
     groups = len(held)
     group = lax.axis_index("tm")
+    reach = max(ref.shape[1] for ref in held)
+
+    def placed(ref, q):
+        term = ref[q]
+        spare = (reach - term.shape[0]) // 2
+        if spare:
+            none = jnp.zeros((spare, term.shape[1]), jnp.float32)
+            term = jnp.concatenate([none, term, none], axis=0)
+        return term
+
+    terms = [[placed(ref, q) for q in range(2)] for ref in held]
 
     def of(index):
-        wanted = lax.bitwise_xor(group, index)
-        picked = [held[0][q] for q in range(2)]
-        for k in range(1, groups):
-            picked = [jnp.where(wanted == k, held[k][q], picked[q]) for q in range(2)]
+        picked = terms[0]
+        for k in range(1, groups - index):
+            picked = [jnp.where(group == index + k, terms[k][q], picked[q]) for q in range(2)]
         return picked
 
     path = of(0)
@@ -231,38 +248,42 @@
     )(*operands)
 
 
-def exchange(near_block, far_block):
+def exchange(block):
     count = lax.axis_size("space")
     far = [(i, (i + 1 if i % 2 else i - 1) % count) for i in range(count)]
     near = [(i, i ^ 1) for i in range(count)]
-    from_far = lax.ppermute(far_block, "space", far)
-    from_near = lax.ppermute(near_block, "space", near)
+    from_far = lax.ppermute(block, "space", far)
+    from_near = lax.ppermute(block, "space", near)
     return from_near, from_far
 
 
-def body(c_state):
+def step(c_state):
     own = c_state[0]
     rows, cols = own.shape[1:]
     count, groups = lax.axis_size("space"), lax.axis_size("tm")
-    assert rows == HALO == ROWS and count % 2 == 0 and groups & (groups - 1) == 0
+    assert rows == HALO == ROWS and count % 2 == 0
     full, half = jnp.float32, jnp.bfloat16
     inner, wide = rows // CF, cols // CF
-    near, far = exchange(own, own)
-    edges = ((FSTEPS, *own.shape), full)
-    first, second, kept, means, gather, spread = call(
-        near_kernel,
+    near, far = exchange(own)
+    own_here, own_sums, gather, spread = call(
+        ready_kernel,
         [
-            edges,
-            edges,
             (own.shape, full),
-            ((2 * ROWS, wide), full),
+            ((ROWS, cols), full),
             ((CF * LANES, LANES), half),
             ((LANES, CF * LANES), half),
         ],
-        (near, own),
+        (own,),
+        cost=4_000_000,
+        hbm=(0,),
+        scratch=[pltpu.SemaphoreType.DMA],
+    )
+    edges = ((FSTEPS, *own.shape), full)
+    first, second, kept, means = call(
+        near_kernel,
+        [edges, edges, (own.shape, full), ((2 * ROWS, wide), full)],
+        (near, own_here, own_sums, gather),
         cost=8_000_000,
-        hbm=(1,),
-        scratch=[pltpu.VMEM(own.shape, full), pltpu.SemaphoreType.DMA],
     )
     end, sent, ends = call(
         far_kernel,
@@ -272,7 +293,7 @@
     )
     reach = groups - 1
     depth = -(-(reach - EXT) // inner)
-    pieces = [sent, *exchange(sent, sent)]
+    pieces = [sent, *exchange(sent)]
     for d in range(2, depth + 1):
         for sign in (1, -1):
             pairs = [(i, (i + sign * d) % count) for i in range(count)]
@@ -282,9 +303,10 @@
         [((2, inner * (2 * depth + 1) + 2 * EXT, wide), full)],
         pieces,
     )
-    held = [window] + [None] * (groups - 1)
-    for k in range(groups - 1, 0, -1):
-        held[k] = lax.ppermute(window, "tm", [(i, i ^ k) for i in range(groups)])
+    held = [sent]
+    for k in range(1, groups):
+        pairs = [(i, (i + k) % groups) for i in range(groups)]
+        held.append(lax.ppermute(sent if k <= EXT else window, "tm", pairs))
     (after,) = call(chain_kernel, [(own.shape, full)], (kept, end, ends, spread, *held), cost=1_000_000)
     return after[None]
 
@@ -292,5 +314,5 @@
 def solution(mesh):
     placed = (P("tm", None, "space", None),)
     return jax.shard_map(
-        body, mesh=mesh, in_specs=placed, out_specs=P("tm", None, "space", None), check_vma=False
-    )
+        step, mesh=mesh, in_specs=placed, out_specs=P("tm", None, "space", None), check_vma=False
+    )

time: 22.3 us -> 23.5 us (1.054)
  waiting for transfers between devices: 7.28 us -> 7.96 us
  starting transfers between devices: 10.7 us -> 11.1 us
    ppermute x7, waiting for transfers between devices: 7.28 us -> 7.96 us  [the longest x3 4.86 us: step(): held.append(lax.ppermute(sent if k <= EXT else window, 'tm', pairs))]
    ppermute x7, starting transfers between devices: 10.7 us -> 11.1 us  [the longest x2 5.68 us: exchange(): from_far = lax.ppermute(block, 'space', far)]
    pallas_call x4 -> x5, Pallas kernels: 3.25 us -> 3.26 us  [call(): pl.pallas_call(kernel, out_shape=[jax.ShapeDtypeStruct(shape, dtype) for...]
  transfers between devices with their start and end apart: 7 -> 7, of which waited for: 4 -> 3; matrix products, arithmetic and copies ran while one was open for 0% -> 0% of each run, Pallas kernels for 6% -> 6%
where the time goes in v3:
time: 23.5 us; the launch traced here: 23.3 us
  starting transfers between devices  11.1 us (47%)
  waiting for transfers between devices  7.96 us (34%)
  Pallas kernels  3.26 us (14%)
  local copies, waits for them, and re-layouts  0.94 us (4%)
    ppermute x2, starting transfers between devices, exchange(): from_far = lax.ppermute(block, 'space', far)  5.68 us
    ppermute x3, starting transfers between devices, step(): held.append(lax.ppermute(sent if k <= EXT else window, 'tm', pairs))  4.88 us
    ppermute x3, waiting for transfers between devices, step(): held.append(lax.ppermute(sent if k <= EXT else window, 'tm', pairs))  4.86 us
    pallas_call x5, Pallas kernels, call(): pl.pallas_call(kernel, out_shape=[jax.ShapeDtypeStruct(shape, dtype) for...  3.26 us
    ppermute x2, waiting for transfers between devices, exchange(): from_far = lax.ppermute(block, 'space', far)  3.09 us
    unnamed x2, local copies, waits for them, and re-layouts  0.94 us
    ppermute x2, starting transfers between devices, exchange(): from_near = lax.ppermute(block, 'space', near)  0.56 us
  transfers between devices with their start and end apart: 7, of which 3 were waited for; matrix products, arithmetic and copies ran while one was open for 0% of the time, Pallas kernels for 6%

profile of v3, /device:TPU:0, one launch (start us, length us, event | category | flops | bytes accessed | tf_op | source)
XLA Modules:
  0.0 23.3 jit_solution(12659728346757711258)
XLA Ops:
  0.0 0.5 %collective-permute-start = (f32[2,8,2048]{2,1,0:T(8,128)}, f32[2,8,2048]{2,1,0:T(8,128)S(1)}, u32[]{:S(2)}, u32[]{:S(2)}) collective-permute-start(f32[2,8,2048]{2,1,0:T(8,128)} %bitcast.2), channel_id=1, source_target_pairs={{0,1},{1,0},{2,3},{3,2},{4,5},{5,4},{6,7},{7,6},{8,9},{9,8},{10,11... | collective-permute-start | bytes 393224 | tf_op jit(solution)/shard_map/ppermute | solution.py:256
  0.5 3.5 %collective-permute-start.1 = (f32[2,8,2048]{2,1,0:T(8,128)}, f32[2,8,2048]{2,1,0:T(8,128)S(1)}, u32[]{:S(2)}, u32[]{:S(2)}) collective-permute-start(f32[2,8,2048]{2,1,0:T(8,128)} %bitcast.3), channel_id=1, source_target_pairs={{0,7},{1,2},{2,1},{3,4},{4,3},{5,6},{6,5},{7,0},{8,15},{9,10},{10,... | collective-permute-start | bytes 393224 | tf_op jit(solution)/shard_map/ppermute | solution.py:255
  4.0 0.0 copy-start
  4.0 0.9 %copy-done = f32[1,2,8,2048]{3,2,1,0:T(8,128)S(1)} copy-done((f32[1,2,8,2048]{3,2,1,0:T(8,128)S(1)}, f32[1,2,8,2048]{3,2,1,0:T(8,128)}, u32[]{:S(2)}) %copy-start) | copy-done | bytes 131096
  5.0 0.2 shard_map.17
  5.2 0.0 collective-permute-done.near_ref
  5.2 1.2 %shard_map.18 = (f32[4,2,8,2048]{3,2,1,0:T(8,128)S(1)}, f32[4,2,8,2048]{3,2,1,0:T(8,128)S(1)}, f32[2,8,2048]{2,1,0:T(8,128)S(1)}, f32[16,512]{1,0:T(8,128)S(1)}) custom-call(f32[2,8,2048]{2,1,0:T(8,128)S(1)} %collective-permute-done.near_ref, f32[2,8,2048]{2,1,0:T(8,128)S(1)} %get-tuple-element.16.own_ref, f32[8,2048]{1,0:T(8,128)S(1)} %get-tuple-element.17.sums_ref, ...), custom_call_target="tpu_custom_call" | custom-call | flops 8000000 | bytes 1000000 | tf_op jit(solution)/shard_map/pallas_call | solution.py:240
  6.4 1.1 %collective-permute-done.1.far_ref = f32[2,8,2048]{2,1,0:T(8,128)S(1)} collective-permute-done((f32[2,8,2048]{2,1,0:T(8,128)}, f32[2,8,2048]{2,1,0:T(8,128)S(1)}, u32[]{:S(2)}, u32[]{:S(2)}) %collective-permute-start.1) | collective-permute-done | bytes 131104 | tf_op jit(solution)/shard_map/ppermute | solution.py:255
  7.5 0.8 %shard_map.19 = (f32[2,8,2048]{2,1,0:T(8,128)S(1)}, f32[2,4,512]{2,1,0:T(4,128)S(1)}, f32[2,2,512]{2,1,0:T(2,128)S(1)}) custom-call(f32[2,8,2048]{2,1,0:T(8,128)S(1)} %collective-permute-done.1.far_ref, f32[4,2,8,2048]{3,2,1,0:T(8,128)S(1)} %get-tuple-element.20.first_ref, f32[4,2,8,2048]{3,2,1,0:T(8,128)S(1)} %get-tuple-element.21.second_ref, ...), custom_call_target="tpu_custom_call" | custom-call | flops 2000000 | bytes 250000 | tf_op jit(solution)/shard_map/pallas_call | solution.py:240
  8.3 0.1 collective-permute-start.3
  8.3 2.1 %collective-permute-start.4 = (f32[2,4,512]{2,1,0:T(4,128)S(1)}, f32[2,4,512]{2,1,0:T(4,128)S(1)}, u32[]{:S(2)}, u32[]{:S(2)}) collective-permute-start(f32[2,4,512]{2,1,0:T(4,128)S(1)} %get-tuple-element.26.own_ref.rest_0_), channel_id=1, source_target_pairs={{0,7},{1,2},{2,1},{3,4},{4,3},{5,6},{6,5},{7,0},{8,15},{9,10},{10,... | collective-permute-start | bytes 49160 | tf_op jit(solution)/shard_map/ppermute | solution.py:255
  10.5 0.0 collective-permute-done.3.near_ref
  10.5 2.0 %collective-permute-done.4.far_ref = f32[2,4,512]{2,1,0:T(4,128)S(1)} collective-permute-done((f32[2,4,512]{2,1,0:T(4,128)S(1)}, f32[2,4,512]{2,1,0:T(4,128)S(1)}, u32[]{:S(2)}, u32[]{:S(2)}) %collective-permute-start.4) | collective-permute-done | bytes 16416 | tf_op jit(solution)/shard_map/ppermute | solution.py:255
  12.5 2.9 %collective-permute-start.5 = (f32[2,8,512]{2,1,0:T(8,128)S(1)}, f32[2,8,512]{2,1,0:T(8,128)S(1)}, u32[]{:S(2)}, u32[]{:S(2)}) collective-permute-start(f32[2,8,512]{2,1,0:T(8,128)S(1)} %shard_map.20), channel_id=1, source_target_pairs={{0,16},{8,24},{16,0},{24,8},{1,17},{9,25},{17,1},{25,9},{2,18},{10... | collective-permute-start | bytes 98312 | tf_op jit(solution)/shard_map/ppermute | solution.py:309
  15.3 1.3 %collective-permute-start.6 = (f32[2,8,512]{2,1,0:T(8,128)S(1)}, f32[2,8,512]{2,1,0:T(8,128)S(1)}, u32[]{:S(2)}, u32[]{:S(2)}) collective-permute-start(f32[2,8,512]{2,1,0:T(8,128)S(1)} %shard_map.20), channel_id=1, source_target_pairs={{0,24},{8,0},{16,8},{24,16},{1,25},{9,1},{17,9},{25,17},{2,26},{10... | collective-permute-start | bytes 98312 | tf_op jit(solution)/shard_map/ppermute | solution.py:309
  16.7 0.7 %collective-permute-start.2 = (f32[2,4,512]{2,1,0:T(4,128)S(1)}, f32[2,4,512]{2,1,0:T(4,128)S(1)}, u32[]{:S(2)}, u32[]{:S(2)}) collective-permute-start(f32[2,4,512]{2,1,0:T(4,128)S(1)} %get-tuple-element.26.own_ref.rest_0_), channel_id=1, source_target_pairs={{0,8},{8,16},{16,24},{24,0},{1,9},{9,17},{17,25},{25,1},{2,10},{10... | collective-permute-start | bytes 49160 | tf_op jit(solution)/shard_map/ppermute | solution.py:309
  17.4 4.9 %collective-permute-done.2.rest_1_ = f32[2,4,512]{2,1,0:T(4,128)S(1)} collective-permute-done((f32[2,4,512]{2,1,0:T(4,128)S(1)}, f32[2,4,512]{2,1,0:T(4,128)S(1)}, u32[]{:S(2)}, u32[]{:S(2)}) %collective-permute-start.2) | collective-permute-done | bytes 16416 | tf_op jit(solution)/shard_map/ppermute | solution.py:309
  22.2 0.0 collective-permute-done.5.rest_2_
  22.2 0.0 collective-permute-done.6.rest_3_
  22.2 1.1 %shard_map.21 = f32[2,8,2048]{2,1,0:T(8,128)} custom-call(f32[2,8,2048]{2,1,0:T(8,128)S(1)} %get-tuple-element.19.kept_ref, f32[2,8,2048]{2,1,0:T(8,128)S(1)} %get-tuple-element.23.end_ref, f32[2,2,512]{2,1,0:T(2,128)S(1)} %get-tuple-element.24.ends_ref, bf16[128,512]{1,0:T(8,128)(2,1)S(1)} %get-tuple-element.25.spread_ref, ...), custom_call_target="tpu_custom_call" | custom-call | flops 1000000 | bytes 125000 | tf_op jit(solution)/shard_map/pallas_call | solution.py:240
  (1 shorter events, 0.0 us)
Async XLA Ops:
  0.0 5.2 %collective-permute-start = (f32[2,8,2048]{2,1,0:T(8,128)}, f32[2,8,2048]{2,1,0:T(8,128)S(1)}, u32[]{:S(2)}, u32[]{:S(2)}) collective-permute-start(f32[2,8,2048]{2,1,0:T(8,128)} %bitcast.2), channel_id=1, source_target_pairs={{0,1},{1,0},{2,3},{3,2},{4,5},{5,4},{6,7},{7,6},{8,9},{9,8},{10,11... | collective-permute-start | bytes 393224 | tf_op jit(solution)/shard_map/ppermute | solution.py:256
  0.5 7.0 %collective-permute-start.1 = (f32[2,8,2048]{2,1,0:T(8,128)}, f32[2,8,2048]{2,1,0:T(8,128)S(1)}, u32[]{:S(2)}, u32[]{:S(2)}) collective-permute-start(f32[2,8,2048]{2,1,0:T(8,128)} %bitcast.3), channel_id=1, source_target_pairs={{0,7},{1,2},{2,1},{3,4},{4,3},{5,6},{6,5},{7,0},{8,15},{9,10},{10,... | collective-permute-start | bytes 393224 | tf_op jit(solution)/shard_map/ppermute | solution.py:255
  4.0 0.9 %copy-start = (f32[1,2,8,2048]{3,2,1,0:T(8,128)S(1)}, f32[1,2,8,2048]{3,2,1,0:T(8,128)}, u32[]{:S(2)}) copy-start(f32[1,2,8,2048]{3,2,1,0:T(8,128)} %param.1) | copy-start | bytes 393220
  8.3 2.2 %collective-permute-start.3 = (f32[2,4,512]{2,1,0:T(4,128)S(1)}, f32[2,4,512]{2,1,0:T(4,128)S(1)}, u32[]{:S(2)}, u32[]{:S(2)}) collective-permute-start(f32[2,4,512]{2,1,0:T(4,128)S(1)} %get-tuple-element.26.own_ref.rest_0_), channel_id=1, source_target_pairs={{0,1},{1,0},{2,3},{3,2},{4,5},{5,4},{6,7},{7,6},{8,9},{9,8},{10,11... | collective-permute-start | bytes 49160 | tf_op jit(solution)/shard_map/ppermute | solution.py:256
  8.3 4.1 %collective-permute-start.4 = (f32[2,4,512]{2,1,0:T(4,128)S(1)}, f32[2,4,512]{2,1,0:T(4,128)S(1)}, u32[]{:S(2)}, u32[]{:S(2)}) collective-permute-start(f32[2,4,512]{2,1,0:T(4,128)S(1)} %get-tuple-element.26.own_ref.rest_0_), channel_id=1, source_target_pairs={{0,7},{1,2},{2,1},{3,4},{4,3},{5,6},{6,5},{7,0},{8,15},{9,10},{10,... | collective-permute-start | bytes 49160 | tf_op jit(solution)/shard_map/ppermute | solution.py:255
  12.5 9.7 %collective-permute-start.5 = (f32[2,8,512]{2,1,0:T(8,128)S(1)}, f32[2,8,512]{2,1,0:T(8,128)S(1)}, u32[]{:S(2)}, u32[]{:S(2)}) collective-permute-start(f32[2,8,512]{2,1,0:T(8,128)S(1)} %shard_map.20), channel_id=1, source_target_pairs={{0,16},{8,24},{16,0},{24,8},{1,17},{9,25},{17,1},{25,9},{2,18},{10... | collective-permute-start | bytes 98312 | tf_op jit(solution)/shard_map/ppermute | solution.py:309
  15.3 6.9 %collective-permute-start.6 = (f32[2,8,512]{2,1,0:T(8,128)S(1)}, f32[2,8,512]{2,1,0:T(8,128)S(1)}, u32[]{:S(2)}, u32[]{:S(2)}) collective-permute-start(f32[2,8,512]{2,1,0:T(8,128)S(1)} %shard_map.20), channel_id=1, source_target_pairs={{0,24},{8,0},{16,8},{24,16},{1,25},{9,1},{17,9},{25,17},{2,26},{10... | collective-permute-start | bytes 98312 | tf_op jit(solution)/shard_map/ppermute | solution.py:309
  16.7 5.5 %collective-permute-start.2 = (f32[2,4,512]{2,1,0:T(4,128)S(1)}, f32[2,4,512]{2,1,0:T(4,128)S(1)}, u32[]{:S(2)}, u32[]{:S(2)}) collective-permute-start(f32[2,4,512]{2,1,0:T(4,128)S(1)} %get-tuple-element.26.own_ref.rest_0_), channel_id=1, source_target_pairs={{0,8},{8,16},{16,24},{24,0},{1,9},{9,17},{17,25},{25,1},{2,10},{10... | collective-permute-start | bytes 49160 | tf_op jit(solution)/shard_map/ppermute | solution.py:309

commit v4 on v3

--- a/solution.py
+++ b/solution.py
@@ -248,13 +248,25 @@
     )(*operands)
 
 
-def exchange(block):
-    count = lax.axis_size("space")
+def exchange(block, among):
+    count, groups = lax.axis_size("space"), lax.axis_size("tm")
     far = [(i, (i + 1 if i % 2 else i - 1) % count) for i in range(count)]
     near = [(i, i ^ 1) for i in range(count)]
-    from_far = lax.ppermute(block, "space", far)
+    mixed = [
+        (t * count + a, t * count + b)
+        for t in range(groups)
+        for a, b in (far if t < among else near)
+    ]
+    from_far = lax.ppermute(block, ("tm", "space"), mixed)
     from_near = lax.ppermute(block, "space", near)
     return from_near, from_far
+
+
+def forward(groups, distance):
+    pairs = [(i, (i + distance) % groups) for i in range(groups)]
+    if distance == 2 and groups > 2:
+        pairs[-2:] = [(groups - 2, 1), (groups - 1, 0)]
+    return pairs
 
 
 def step(c_state):
@@ -264,7 +276,7 @@
     assert rows == HALO == ROWS and count % 2 == 0
     full, half = jnp.float32, jnp.bfloat16
     inner, wide = rows // CF, cols // CF
-    near, far = exchange(own)
+    near, far = exchange(own, groups)
     own_here, own_sums, gather, spread = call(
         ready_kernel,
         [
@@ -293,7 +305,7 @@
     )
     reach = groups - 1
     depth = -(-(reach - EXT) // inner)
-    pieces = [sent, *exchange(sent)]
+    pieces = [sent, *exchange(sent, groups - 1 - EXT)]
     for d in range(2, depth + 1):
         for sign in (1, -1):
             pairs = [(i, (i + sign * d) % count) for i in range(count)]
@@ -305,8 +317,7 @@
     )
     held = [sent]
     for k in range(1, groups):
-        pairs = [(i, (i + k) % groups) for i in range(groups)]
-        held.append(lax.ppermute(sent if k <= EXT else window, "tm", pairs))
+        held.append(lax.ppermute(sent if k <= EXT else window, "tm", forward(groups, k)))
     (after,) = call(chain_kernel, [(own.shape, full)], (kept, end, ends, spread, *held), cost=1_000_000)
     return after[None]
 

time: 23.5 us -> 23.1 us (0.983)
  starting transfers between devices: 11.1 us -> 10.1 us
  waiting for transfers between devices: 7.96 us -> 8.63 us
    ppermute x5, starting transfers between devices: 10.6 us -> 9.55 us  [the longest x2 5.68 us: exchange(): from_far = lax.ppermute(block, ('tm', 'space'), mixed)]
    ppermute x5, waiting for transfers between devices: 7.95 us -> 8.62 us  [the longest x3 5.54 us: step(): lax.ppermute(sent if k <= EXT else window, 'tm', forward(groups, k))]
where the time goes in v4:
time: 23.1 us; the launch traced here: 23 us
  starting transfers between devices  10.1 us (44%)
  waiting for transfers between devices  8.63 us (37%)
  Pallas kernels  3.26 us (14%)
  local copies, waits for them, and re-layouts  0.94 us (4%)
    ppermute x2, starting transfers between devices, exchange(): from_far = lax.ppermute(block, ('tm', 'space'), mixed)  5.68 us
    ppermute x3, waiting for transfers between devices, step(): lax.ppermute(sent if k <= EXT else window, 'tm', forward(groups, k))  5.54 us
    ppermute x3, starting transfers between devices, step(): lax.ppermute(sent if k <= EXT else window, 'tm', forward(groups, k))  3.87 us
    pallas_call x5, Pallas kernels, call(): pl.pallas_call(kernel, out_shape=[jax.ShapeDtypeStruct(shape, dtype) for...  3.26 us
    ppermute x2, waiting for transfers between devices, exchange(): from_far = lax.ppermute(block, ('tm', 'space'), mixed)  3.09 us
    unnamed x2, local copies, waits for them, and re-layouts  0.94 us
    ppermute x2, starting transfers between devices, exchange(): from_near = lax.ppermute(block, 'space', near)  0.56 us
  transfers between devices with their start and end apart: 7, of which 3 were waited for; matrix products, arithmetic and copies ran while one was open for 0% of the time, Pallas kernels for 6%

profile of v4, /device:TPU:0, one launch (start us, length us, event | category | flops | bytes accessed | tf_op | source)
XLA Modules:
  0.0 23.0 jit_solution(11512620045678058144)
XLA Ops:
  0.0 0.5 %collective-permute-start = (f32[2,8,2048]{2,1,0:T(8,128)}, f32[2,8,2048]{2,1,0:T(8,128)S(1)}, u32[]{:S(2)}, u32[]{:S(2)}) collective-permute-start(f32[2,8,2048]{2,1,0:T(8,128)} %bitcast.2), channel_id=1, source_target_pairs={{0,1},{1,0},{2,3},{3,2},{4,5},{5,4},{6,7},{7,6},{8,9},{9,8},{10,11... | collective-permute-start | bytes 393224 | tf_op jit(solution)/shard_map/ppermute | solution.py:261
  0.5 3.5 %collective-permute-start.1 = (f32[2,8,2048]{2,1,0:T(8,128)}, f32[2,8,2048]{2,1,0:T(8,128)S(1)}, u32[]{:S(2)}, u32[]{:S(2)}) collective-permute-start(f32[2,8,2048]{2,1,0:T(8,128)} %bitcast.3), channel_id=1, source_target_pairs={{0,7},{1,2},{2,1},{3,4},{4,3},{5,6},{6,5},{7,0},{8,15},{9,10},{10,... | collective-permute-start | bytes 393224 | tf_op jit(solution)/shard_map/ppermute | solution.py:260
  4.0 0.0 copy-start
  4.0 0.9 %copy-done = f32[1,2,8,2048]{3,2,1,0:T(8,128)S(1)} copy-done((f32[1,2,8,2048]{3,2,1,0:T(8,128)S(1)}, f32[1,2,8,2048]{3,2,1,0:T(8,128)}, u32[]{:S(2)}) %copy-start) | copy-done | bytes 131096
  5.0 0.2 shard_map.17
  5.2 0.0 collective-permute-done.near_ref
  5.2 1.2 %shard_map.18 = (f32[4,2,8,2048]{3,2,1,0:T(8,128)S(1)}, f32[4,2,8,2048]{3,2,1,0:T(8,128)S(1)}, f32[2,8,2048]{2,1,0:T(8,128)S(1)}, f32[16,512]{1,0:T(8,128)S(1)}) custom-call(f32[2,8,2048]{2,1,0:T(8,128)S(1)} %collective-permute-done.near_ref, f32[2,8,2048]{2,1,0:T(8,128)S(1)} %get-tuple-element.16.own_ref, f32[8,2048]{1,0:T(8,128)S(1)} %get-tuple-element.17.sums_ref, ...), custom_call_target="tpu_custom_call" | custom-call | flops 8000000 | bytes 1000000 | tf_op jit(solution)/shard_map/pallas_call | solution.py:240
  6.4 1.1 %collective-permute-done.1.far_ref = f32[2,8,2048]{2,1,0:T(8,128)S(1)} collective-permute-done((f32[2,8,2048]{2,1,0:T(8,128)}, f32[2,8,2048]{2,1,0:T(8,128)S(1)}, u32[]{:S(2)}, u32[]{:S(2)}) %collective-permute-start.1) | collective-permute-done | bytes 131104 | tf_op jit(solution)/shard_map/ppermute | solution.py:260
  7.5 0.8 %shard_map.19 = (f32[2,8,2048]{2,1,0:T(8,128)S(1)}, f32[2,4,512]{2,1,0:T(4,128)S(1)}, f32[2,2,512]{2,1,0:T(2,128)S(1)}) custom-call(f32[2,8,2048]{2,1,0:T(8,128)S(1)} %collective-permute-done.1.far_ref, f32[4,2,8,2048]{3,2,1,0:T(8,128)S(1)} %get-tuple-element.20.first_ref, f32[4,2,8,2048]{3,2,1,0:T(8,128)S(1)} %get-tuple-element.21.second_ref, ...), custom_call_target="tpu_custom_call" | custom-call | flops 2000000 | bytes 250000 | tf_op jit(solution)/shard_map/pallas_call | solution.py:240
  8.3 0.1 collective-permute-start.3
  8.3 2.1 %collective-permute-start.4 = (f32[2,4,512]{2,1,0:T(4,128)S(1)}, f32[2,4,512]{2,1,0:T(4,128)S(1)}, u32[]{:S(2)}, u32[]{:S(2)}) collective-permute-start(f32[2,4,512]{2,1,0:T(4,128)S(1)} %get-tuple-element.26.own_ref.rest_0_), channel_id=1, source_target_pairs={{0,7},{1,2},{2,1},{3,4},{4,3},{5,6},{6,5},{7,0},{8,15},{9,10},{10,... | collective-permute-start | bytes 49160 | tf_op jit(solution)/shard_map/ppermute | solution.py:260
  10.5 0.0 collective-permute-done.3.near_ref
  10.5 2.0 %collective-permute-done.4.far_ref = f32[2,4,512]{2,1,0:T(4,128)S(1)} collective-permute-done((f32[2,4,512]{2,1,0:T(4,128)S(1)}, f32[2,4,512]{2,1,0:T(4,128)S(1)}, u32[]{:S(2)}, u32[]{:S(2)}) %collective-permute-start.4) | collective-permute-done | bytes 16416 | tf_op jit(solution)/shard_map/ppermute | solution.py:260
  12.5 0.1 collective-permute-start.5
  12.5 3.8 %collective-permute-start.6 = (f32[2,8,512]{2,1,0:T(8,128)S(1)}, f32[2,8,512]{2,1,0:T(8,128)S(1)}, u32[]{:S(2)}, u32[]{:S(2)}) collective-permute-start(f32[2,8,512]{2,1,0:T(8,128)S(1)} %shard_map.20), channel_id=1, source_target_pairs={{0,24},{8,0},{16,8},{24,16},{1,25},{9,1},{17,9},{25,17},{2,26},{10... | collective-permute-start | bytes 98312 | tf_op jit(solution)/shard_map/ppermute | solution.py:320
  16.4 0.0 collective-permute-start.2
  16.4 5.5 %collective-permute-done.2.rest_1_ = f32[2,4,512]{2,1,0:T(4,128)S(1)} collective-permute-done((f32[2,4,512]{2,1,0:T(4,128)S(1)}, f32[2,4,512]{2,1,0:T(4,128)S(1)}, u32[]{:S(2)}, u32[]{:S(2)}) %collective-permute-start.2) | collective-permute-done | bytes 16416 | tf_op jit(solution)/shard_map/ppermute | solution.py:320
  21.9 0.0 collective-permute-done.5.rest_2_
  21.9 0.0 collective-permute-done.6.rest_3_
  21.9 1.1 %shard_map.21 = f32[2,8,2048]{2,1,0:T(8,128)} custom-call(f32[2,8,2048]{2,1,0:T(8,128)S(1)} %get-tuple-element.19.kept_ref, f32[2,8,2048]{2,1,0:T(8,128)S(1)} %get-tuple-element.23.end_ref, f32[2,2,512]{2,1,0:T(2,128)S(1)} %get-tuple-element.24.ends_ref, bf16[128,512]{1,0:T(8,128)(2,1)S(1)} %get-tuple-element.25.spread_ref, ...), custom_call_target="tpu_custom_call" | custom-call | flops 1000000 | bytes 125000 | tf_op jit(solution)/shard_map/pallas_call | solution.py:240
  (1 shorter events, 0.0 us)
Async XLA Ops:
  0.0 5.2 %collective-permute-start = (f32[2,8,2048]{2,1,0:T(8,128)}, f32[2,8,2048]{2,1,0:T(8,128)S(1)}, u32[]{:S(2)}, u32[]{:S(2)}) collective-permute-start(f32[2,8,2048]{2,1,0:T(8,128)} %bitcast.2), channel_id=1, source_target_pairs={{0,1},{1,0},{2,3},{3,2},{4,5},{5,4},{6,7},{7,6},{8,9},{9,8},{10,11... | collective-permute-start | bytes 393224 | tf_op jit(solution)/shard_map/ppermute | solution.py:261
  0.5 7.0 %collective-permute-start.1 = (f32[2,8,2048]{2,1,0:T(8,128)}, f32[2,8,2048]{2,1,0:T(8,128)S(1)}, u32[]{:S(2)}, u32[]{:S(2)}) collective-permute-start(f32[2,8,2048]{2,1,0:T(8,128)} %bitcast.3), channel_id=1, source_target_pairs={{0,7},{1,2},{2,1},{3,4},{4,3},{5,6},{6,5},{7,0},{8,15},{9,10},{10,... | collective-permute-start | bytes 393224 | tf_op jit(solution)/shard_map/ppermute | solution.py:260
  4.0 0.9 %copy-start = (f32[1,2,8,2048]{3,2,1,0:T(8,128)S(1)}, f32[1,2,8,2048]{3,2,1,0:T(8,128)}, u32[]{:S(2)}) copy-start(f32[1,2,8,2048]{3,2,1,0:T(8,128)} %param.1) | copy-start | bytes 393220
  8.3 2.2 %collective-permute-start.3 = (f32[2,4,512]{2,1,0:T(4,128)S(1)}, f32[2,4,512]{2,1,0:T(4,128)S(1)}, u32[]{:S(2)}, u32[]{:S(2)}) collective-permute-start(f32[2,4,512]{2,1,0:T(4,128)S(1)} %get-tuple-element.26.own_ref.rest_0_), channel_id=1, source_target_pairs={{0,1},{1,0},{2,3},{3,2},{4,5},{5,4},{6,7},{7,6},{8,9},{9,8},{10,11... | collective-permute-start | bytes 49160 | tf_op jit(solution)/shard_map/ppermute | solution.py:261
  8.3 4.1 %collective-permute-start.4 = (f32[2,4,512]{2,1,0:T(4,128)S(1)}, f32[2,4,512]{2,1,0:T(4,128)S(1)}, u32[]{:S(2)}, u32[]{:S(2)}) collective-permute-start(f32[2,4,512]{2,1,0:T(4,128)S(1)} %get-tuple-element.26.own_ref.rest_0_), channel_id=1, source_target_pairs={{0,7},{1,2},{2,1},{3,4},{4,3},{5,6},{6,5},{7,0},{8,15},{9,10},{10,... | collective-permute-start | bytes 49160 | tf_op jit(solution)/shard_map/ppermute | solution.py:260
  12.5 9.4 %collective-permute-start.5 = (f32[2,8,512]{2,1,0:T(8,128)S(1)}, f32[2,8,512]{2,1,0:T(8,128)S(1)}, u32[]{:S(2)}, u32[]{:S(2)}) collective-permute-start(f32[2,8,512]{2,1,0:T(8,128)S(1)} %shard_map.20), channel_id=1, source_target_pairs={{0,16},{8,24},{16,8},{24,0},{1,17},{9,25},{17,9},{25,1},{2,18},{10... | collective-permute-start | bytes 98312 | tf_op jit(solution)/shard_map/ppermute | solution.py:320
  12.5 9.4 %collective-permute-start.6 = (f32[2,8,512]{2,1,0:T(8,128)S(1)}, f32[2,8,512]{2,1,0:T(8,128)S(1)}, u32[]{:S(2)}, u32[]{:S(2)}) collective-permute-start(f32[2,8,512]{2,1,0:T(8,128)S(1)} %shard_map.20), channel_id=1, source_target_pairs={{0,24},{8,0},{16,8},{24,16},{1,25},{9,1},{17,9},{25,17},{2,26},{10... | collective-permute-start | bytes 98312 | tf_op jit(solution)/shard_map/ppermute | solution.py:320
  16.4 5.5 %collective-permute-start.2 = (f32[2,4,512]{2,1,0:T(4,128)S(1)}, f32[2,4,512]{2,1,0:T(4,128)S(1)}, u32[]{:S(2)}, u32[]{:S(2)}) collective-permute-start(f32[2,4,512]{2,1,0:T(4,128)S(1)} %get-tuple-element.26.own_ref.rest_0_), channel_id=1, source_target_pairs={{0,8},{8,16},{16,24},{24,0},{1,9},{9,17},{17,25},{25,1},{2,10},{10... | collective-permute-start | bytes 49160 | tf_op jit(solution)/shard_map/ppermute | solution.py:320

commit v5 on v4

--- a/solution.py
+++ b/solution.py
@@ -19,6 +19,7 @@
 LANES = 128
 VMEM = pl.BlockSpec(memory_space=pltpu.VMEM)
 ROWS = 8
+OUT_PIECES = 2
 
 
 def shifted(field, amount, axis):
@@ -194,10 +195,7 @@
         window_ref[q] = jnp.concatenate(parts, axis=0)
 
 
-def chain_kernel(kept_ref, end_ref, ends_ref, spread_ref, *rest):
-    held, out_ref = rest[:-1], rest[-1]
-    groups = len(held)
-    group = lax.axis_index("tm")
+def corrected(group, groups, held, kept_ref, end_ref, ends_ref, spread_ref, out_hbm, stage_ref, sems):
     reach = max(ref.shape[1] for ref in held)
 
     def placed(ref, q):
@@ -211,8 +209,10 @@
     terms = [[placed(ref, q) for q in range(2)] for ref in held]
 
     def of(index):
-        picked = terms[0]
-        for k in range(1, groups - index):
+        if index == groups - 1:
+            return terms[0]
+        picked = terms[min(len(terms) - 1, groups - 1 - index)]
+        for k in range(min(len(terms) - 1, groups - 1 - index) - 1, -1, -1):
             picked = [jnp.where(group == index + k, terms[k][q], picked[q]) for q in range(2)]
         return picked
 
@@ -221,27 +221,58 @@
         term = of(index)
         after = advance(path, COARSE_COURANT, COARSE_DIFFUSION, 1)
         path = [jnp.where(index <= group, after[q] + term[q], path[q]) for q in range(2)]
-    first = (path[0].shape[0] - 2) // 2
+    first = (reach - 2) // 2
     odd = lax.axis_index("space") % 2 == 1
-    moves = []
+    moves, own = [], []
     for q in range(2):
         move = path[q][first : first + 2] - ends_ref[q]
         moves.append(repeat_rows(move[:1], move[1:]))
+        upper = lax.broadcasted_iota(jnp.int32, kept_ref.shape[1:], 0) >= CF
+        own.append(shifted(jnp.where(upper == odd, kept_ref[q], end_ref[q]), CF, 0))
     lifted = by_pieces(jnp.concatenate(moves, axis=0), spread_ref[...])
-    for q in range(2):
-        kept, end = kept_ref[q], end_ref[q]
-        upper = lax.broadcasted_iota(jnp.int32, kept.shape, 0) >= CF
-        own = shifted(jnp.where(upper == odd, kept, end), CF, 0)
-        out_ref[q] = own + lifted[q * ROWS : (q + 1) * ROWS]
-
-
-def call(kernel, shapes, operands, cost=0, hbm=(), scratch=()):
+    copies = []
+    width = out_hbm.shape[2] // OUT_PIECES
+    for i in range(OUT_PIECES):
+        cols = slice(i * width, (i + 1) * width)
+        for q in range(2):
+            stage_ref[q, :, cols] = own[q][:, cols] + lifted[q * ROWS : (q + 1) * ROWS, cols]
+        copy = pltpu.make_async_copy(stage_ref.at[:, :, cols], out_hbm.at[:, :, cols], sems.at[i])
+        copy.start()
+        copies.append(copy)
+    for copy in copies:
+        copy.wait()
+
+
+def early_kernel(among, kept_ref, end_ref, ends_ref, spread_ref, *rest):
+    held, (out_hbm, stage_ref, sems) = rest[:-3], rest[-3:]
+    group = lax.axis_index("tm")
+
+    @pl.when(group < among)
+    def _():
+        corrected(
+            group, among, held, kept_ref, end_ref, ends_ref, spread_ref, out_hbm, stage_ref, sems
+        )
+
+
+def late_kernel(groups, among, before_hbm, kept_ref, end_ref, ends_ref, spread_ref, *rest):
+    held, (out_hbm, stage_ref, sems) = rest[:-3], rest[-3:]
+    group = lax.axis_index("tm")
+
+    @pl.when(group >= among)
+    def _():
+        corrected(
+            group, groups, held, kept_ref, end_ref, ends_ref, spread_ref, out_hbm, stage_ref, sems
+        )
+
+
+def call(kernel, shapes, operands, cost=0, hbm=(), scratch=(), out=VMEM, alias=None):
     where = [pl.BlockSpec(memory_space=pl.ANY) if i in hbm else VMEM for i in range(len(operands))]
     return pl.pallas_call(
         kernel,
         out_shape=[jax.ShapeDtypeStruct(shape, dtype) for shape, dtype in shapes],
         in_specs=where,
-        out_specs=[VMEM] * len(shapes),
+        out_specs=[out] * len(shapes),
+        input_output_aliases=alias or {},
         scratch_shapes=scratch,
         cost_estimate=pl.CostEstimate(flops=cost, bytes_accessed=cost // 8, transcendentals=0),
         compiler_params=pltpu.CompilerParams(vmem_limit_bytes=16 * 1024 * 1024),
@@ -318,7 +349,28 @@
     held = [sent]
     for k in range(1, groups):
         held.append(lax.ppermute(sent if k <= EXT else window, "tm", forward(groups, k)))
-    (after,) = call(chain_kernel, [(own.shape, full)], (kept, end, ends, spread, *held), cost=1_000_000)
+    whole = (own.shape, full)
+    scratch = [pltpu.VMEM(own.shape, full), pltpu.SemaphoreType.DMA((OUT_PIECES,))]
+    among = min(groups, 1 + EXT)
+    (after,) = call(
+        functools.partial(early_kernel, among),
+        [whole],
+        (kept, end, ends, spread, *held[:among]),
+        cost=1_000_000,
+        scratch=scratch,
+        out=pl.BlockSpec(memory_space=pltpu.HBM),
+    )
+    if groups > among:
+        (after,) = call(
+            functools.partial(late_kernel, groups, among),
+            [whole],
+            (after, kept, end, ends, spread, *held),
+            cost=1_000_000,
+            hbm=(0,),
+            scratch=scratch,
+            out=pl.BlockSpec(memory_space=pltpu.HBM),
+            alias={0: 0},
+        )
     return after[None]
 
 

time: 23.1 us -> 23 us (level)
    pallas_call x5 -> x6, Pallas kernels: 3.26 us -> 3.14 us  [call(): pl.pallas_call(kernel, out_shape=[jax.ShapeDtypeStruct(shape, dtype) for...]
  transfers between devices with their start and end apart: 7 -> 7, of which waited for: 3 -> 3; matrix products, arithmetic and copies ran while one was open for 0% -> 0% of each run, Pallas kernels for 6% -> 10%
where the time goes in v5:
time: 23 us; the launch traced here: 22.9 us
  starting transfers between devices  10.1 us (44%)
  waiting for transfers between devices  8.63 us (38%)
  Pallas kernels  3.14 us (14%)
  local copies, waits for them, and re-layouts  0.94 us (4%)
    ppermute x2, starting transfers between devices, exchange(): from_far = lax.ppermute(block, ('tm', 'space'), mixed)  5.68 us
    ppermute x3, waiting for transfers between devices, step(): lax.ppermute(sent if k <= EXT else window, 'tm', forward(groups, k))  5.54 us
    ppermute x3, starting transfers between devices, step(): lax.ppermute(sent if k <= EXT else window, 'tm', forward(groups, k))  3.87 us
    pallas_call x6, Pallas kernels, call(): pl.pallas_call(kernel, out_shape=[jax.ShapeDtypeStruct(shape, dtype) for...  3.14 us
    ppermute x2, waiting for transfers between devices, exchange(): from_far = lax.ppermute(block, ('tm', 'space'), mixed)  3.09 us
    unnamed x2, local copies, waits for them, and re-layouts  0.94 us
    ppermute x2, starting transfers between devices, exchange(): from_near = lax.ppermute(block, 'space', near)  0.56 us
  transfers between devices with their start and end apart: 7, of which 3 were waited for; matrix products, arithmetic and copies ran while one was open for 0% of the time, Pallas kernels for 10%

profile of v5, /device:TPU:0, one launch (start us, length us, event | category | flops | bytes accessed | tf_op | source)
XLA Modules:
  0.0 22.9 jit_solution(14570999907385899228)
XLA Ops:
  0.0 0.5 %collective-permute-start = (f32[2,8,2048]{2,1,0:T(8,128)}, f32[2,8,2048]{2,1,0:T(8,128)S(1)}, u32[]{:S(2)}, u32[]{:S(2)}) collective-permute-start(f32[2,8,2048]{2,1,0:T(8,128)} %bitcast.2), channel_id=1, source_target_pairs={{0,1},{1,0},{2,3},{3,2},{4,5},{5,4},{6,7},{7,6},{8,9},{9,8},{10,11... | collective-permute-start | bytes 393224 | tf_op jit(solution)/shard_map/ppermute | solution.py:292
  0.5 3.5 %collective-permute-start.1 = (f32[2,8,2048]{2,1,0:T(8,128)}, f32[2,8,2048]{2,1,0:T(8,128)S(1)}, u32[]{:S(2)}, u32[]{:S(2)}) collective-permute-start(f32[2,8,2048]{2,1,0:T(8,128)} %bitcast.3), channel_id=1, source_target_pairs={{0,7},{1,2},{2,1},{3,4},{4,3},{5,6},{6,5},{7,0},{8,15},{9,10},{10,... | collective-permute-start | bytes 393224 | tf_op jit(solution)/shard_map/ppermute | solution.py:291
  4.0 0.0 copy-start
  4.0 0.9 %copy-done = f32[1,2,8,2048]{3,2,1,0:T(8,128)S(1)} copy-done((f32[1,2,8,2048]{3,2,1,0:T(8,128)S(1)}, f32[1,2,8,2048]{3,2,1,0:T(8,128)}, u32[]{:S(2)}) %copy-start) | copy-done | bytes 131096
  5.0 0.2 shard_map.17
  5.2 0.0 collective-permute-done.near_ref
  5.2 1.2 %shard_map.18 = (f32[4,2,8,2048]{3,2,1,0:T(8,128)S(1)}, f32[4,2,8,2048]{3,2,1,0:T(8,128)S(1)}, f32[2,8,2048]{2,1,0:T(8,128)S(1)}, f32[16,512]{1,0:T(8,128)S(1)}) custom-call(f32[2,8,2048]{2,1,0:T(8,128)S(1)} %collective-permute-done.near_ref, f32[2,8,2048]{2,1,0:T(8,128)S(1)} %get-tuple-element.16.own_ref, f32[8,2048]{1,0:T(8,128)S(1)} %get-tuple-element.17.sums_ref, ...), custom_call_target="tpu_custom_call" | custom-call | flops 8000000 | bytes 1000000 | tf_op jit(solution)/shard_map/pallas_call | solution.py:270
  6.4 1.1 %collective-permute-done.1.far_ref = f32[2,8,2048]{2,1,0:T(8,128)S(1)} collective-permute-done((f32[2,8,2048]{2,1,0:T(8,128)}, f32[2,8,2048]{2,1,0:T(8,128)S(1)}, u32[]{:S(2)}, u32[]{:S(2)}) %collective-permute-start.1) | collective-permute-done | bytes 131104 | tf_op jit(solution)/shard_map/ppermute | solution.py:291
  7.5 0.8 %shard_map.19 = (f32[2,8,2048]{2,1,0:T(8,128)S(1)}, f32[2,4,512]{2,1,0:T(4,128)S(1)}, f32[2,2,512]{2,1,0:T(2,128)S(1)}) custom-call(f32[2,8,2048]{2,1,0:T(8,128)S(1)} %collective-permute-done.1.far_ref, f32[4,2,8,2048]{3,2,1,0:T(8,128)S(1)} %get-tuple-element.20.first_ref, f32[4,2,8,2048]{3,2,1,0:T(8,128)S(1)} %get-tuple-element.21.second_ref, ...), custom_call_target="tpu_custom_call" | custom-call | flops 2000000 | bytes 250000 | tf_op jit(solution)/shard_map/pallas_call | solution.py:270
  8.3 0.1 collective-permute-start.3
  8.3 2.1 %collective-permute-start.4 = (f32[2,4,512]{2,1,0:T(4,128)S(1)}, f32[2,4,512]{2,1,0:T(4,128)S(1)}, u32[]{:S(2)}, u32[]{:S(2)}) collective-permute-start(f32[2,4,512]{2,1,0:T(4,128)S(1)} %get-tuple-element.26.rest_0_.own_ref), channel_id=1, source_target_pairs={{0,7},{1,2},{2,1},{3,4},{4,3},{5,6},{6,5},{7,0},{8,15},{9,10},{10,... | collective-permute-start | bytes 49160 | tf_op jit(solution)/shard_map/ppermute | solution.py:291
  10.5 0.0 collective-permute-done.3.near_ref
  10.5 2.0 %collective-permute-done.4.far_ref = f32[2,4,512]{2,1,0:T(4,128)S(1)} collective-permute-done((f32[2,4,512]{2,1,0:T(4,128)S(1)}, f32[2,4,512]{2,1,0:T(4,128)S(1)}, u32[]{:S(2)}, u32[]{:S(2)}) %collective-permute-start.4) | collective-permute-done | bytes 16416 | tf_op jit(solution)/shard_map/ppermute | solution.py:291
  12.5 0.1 collective-permute-start.5
  12.5 3.8 %collective-permute-start.6 = (f32[2,8,512]{2,1,0:T(8,128)S(1)}, f32[2,8,512]{2,1,0:T(8,128)S(1)}, u32[]{:S(2)}, u32[]{:S(2)}) collective-permute-start(f32[2,8,512]{2,1,0:T(8,128)S(1)} %shard_map.21), channel_id=1, source_target_pairs={{0,24},{8,0},{16,8},{24,16},{1,25},{9,1},{17,9},{25,17},{2,26},{10... | collective-permute-start | bytes 98312 | tf_op jit(solution)/shard_map/ppermute | solution.py:351
  16.4 0.0 collective-permute-start.2
  16.4 5.5 %collective-permute-done.2.rest_1_ = f32[2,4,512]{2,1,0:T(4,128)S(1)} collective-permute-done((f32[2,4,512]{2,1,0:T(4,128)S(1)}, f32[2,4,512]{2,1,0:T(4,128)S(1)}, u32[]{:S(2)}, u32[]{:S(2)}) %collective-permute-start.2) | collective-permute-done | bytes 16416 | tf_op jit(solution)/shard_map/ppermute | solution.py:351
  21.9 0.9 %shard_map.20.before_hbm = f32[2,8,2048]{2,1,0:T(8,128)} custom-call(f32[2,8,2048]{2,1,0:T(8,128)S(1)} %get-tuple-element.19.kept_ref, f32[2,8,2048]{2,1,0:T(8,128)S(1)} %get-tuple-element.23.end_ref, f32[2,2,512]{2,1,0:T(2,128)S(1)} %get-tuple-element.24.ends_ref, bf16[128,512]{1,0:T(8,128)(2,1)S(1)} %get-tuple-element.25.spread_ref, ...), custom_call_target="tpu_custom_call" | custom-call | flops 1000000 | bytes 125000 | tf_op jit(solution)/shard_map/pallas_call | solution.py:270
  22.8 0.0 collective-permute-done.5.rest_2_
  22.8 0.0 collective-permute-done.6.rest_3_
  (2 shorter events, 0.0 us)
Async XLA Ops:
  0.0 5.2 %collective-permute-start = (f32[2,8,2048]{2,1,0:T(8,128)}, f32[2,8,2048]{2,1,0:T(8,128)S(1)}, u32[]{:S(2)}, u32[]{:S(2)}) collective-permute-start(f32[2,8,2048]{2,1,0:T(8,128)} %bitcast.2), channel_id=1, source_target_pairs={{0,1},{1,0},{2,3},{3,2},{4,5},{5,4},{6,7},{7,6},{8,9},{9,8},{10,11... | collective-permute-start | bytes 393224 | tf_op jit(solution)/shard_map/ppermute | solution.py:292
  0.5 7.0 %collective-permute-start.1 = (f32[2,8,2048]{2,1,0:T(8,128)}, f32[2,8,2048]{2,1,0:T(8,128)S(1)}, u32[]{:S(2)}, u32[]{:S(2)}) collective-permute-start(f32[2,8,2048]{2,1,0:T(8,128)} %bitcast.3), channel_id=1, source_target_pairs={{0,7},{1,2},{2,1},{3,4},{4,3},{5,6},{6,5},{7,0},{8,15},{9,10},{10,... | collective-permute-start | bytes 393224 | tf_op jit(solution)/shard_map/ppermute | solution.py:291
  4.0 0.9 %copy-start = (f32[1,2,8,2048]{3,2,1,0:T(8,128)S(1)}, f32[1,2,8,2048]{3,2,1,0:T(8,128)}, u32[]{:S(2)}) copy-start(f32[1,2,8,2048]{3,2,1,0:T(8,128)} %param.1) | copy-start | bytes 393220
  8.3 2.2 %collective-permute-start.3 = (f32[2,4,512]{2,1,0:T(4,128)S(1)}, f32[2,4,512]{2,1,0:T(4,128)S(1)}, u32[]{:S(2)}, u32[]{:S(2)}) collective-permute-start(f32[2,4,512]{2,1,0:T(4,128)S(1)} %get-tuple-element.26.rest_0_.own_ref), channel_id=1, source_target_pairs={{0,1},{1,0},{2,3},{3,2},{4,5},{5,4},{6,7},{7,6},{8,9},{9,8},{10,11... | collective-permute-start | bytes 49160 | tf_op jit(solution)/shard_map/ppermute | solution.py:292
  8.3 4.1 %collective-permute-start.4 = (f32[2,4,512]{2,1,0:T(4,128)S(1)}, f32[2,4,512]{2,1,0:T(4,128)S(1)}, u32[]{:S(2)}, u32[]{:S(2)}) collective-permute-start(f32[2,4,512]{2,1,0:T(4,128)S(1)} %get-tuple-element.26.rest_0_.own_ref), channel_id=1, source_target_pairs={{0,7},{1,2},{2,1},{3,4},{4,3},{5,6},{6,5},{7,0},{8,15},{9,10},{10,... | collective-permute-start | bytes 49160 | tf_op jit(solution)/shard_map/ppermute | solution.py:291
  12.5 10.4 %collective-permute-start.5 = (f32[2,8,512]{2,1,0:T(8,128)S(1)}, f32[2,8,512]{2,1,0:T(8,128)S(1)}, u32[]{:S(2)}, u32[]{:S(2)}) collective-permute-start(f32[2,8,512]{2,1,0:T(8,128)S(1)} %shard_map.21), channel_id=1, source_target_pairs={{0,16},{8,24},{16,8},{24,0},{1,17},{9,25},{17,9},{25,1},{2,18},{10... | collective-permute-start | bytes 98312 | tf_op jit(solution)/shard_map/ppermute | solution.py:351
  12.5 10.3 %collective-permute-start.6 = (f32[2,8,512]{2,1,0:T(8,128)S(1)}, f32[2,8,512]{2,1,0:T(8,128)S(1)}, u32[]{:S(2)}, u32[]{:S(2)}) collective-permute-start(f32[2,8,512]{2,1,0:T(8,128)S(1)} %shard_map.21), channel_id=1, source_target_pairs={{0,24},{8,0},{16,8},{24,16},{1,25},{9,1},{17,9},{25,17},{2,26},{10... | collective-permute-start | bytes 98312 | tf_op jit(solution)/shard_map/ppermute | solution.py:351
  16.4 5.5 %collective-permute-start.2 = (f32[2,4,512]{2,1,0:T(4,128)S(1)}, f32[2,4,512]{2,1,0:T(4,128)S(1)}, u32[]{:S(2)}, u32[]{:S(2)}) collective-permute-start(f32[2,4,512]{2,1,0:T(4,128)S(1)} %get-tuple-element.26.rest_0_.own_ref), channel_id=1, source_target_pairs={{0,8},{8,16},{16,24},{24,0},{1,9},{9,17},{17,25},{25,1},{2,10},{10... | collective-permute-start | bytes 49160 | tf_op jit(solution)/shard_map/ppermute | solution.py:351

commit v6 on v5

--- a/solution.py
+++ b/solution.py
@@ -127,36 +127,55 @@
     means_ref[...] = both
 
 
-def far_kernel(far_ref, first_ref, second_ref, means_ref, gather_ref, end_ref, sent_ref, ends_ref):
+def slanted(outer, first, second, odd):
+    sign = jnp.where(odd, 1.0, -1.0)
+    turn = jnp.where(odd, 1, ROWS - 1)
+    row = lax.broadcasted_iota(jnp.int32, outer[0].shape, 0)
+    edge = row == jnp.where(odd, 0, ROWS - 1)
+    fields = [jnp.where(edge, first[q], pltpu.roll(outer[q], turn, 0)) for q in range(2)]
+    inner = [jnp.where(edge, second[q], pltpu.roll(fields[q], turn, 0)) for q in range(2)]
+    along_u, along_v = (sign * COURANT) * fields[0], COURANT * fields[1]
+    toward = jnp.maximum(along_u, 0.0) + DIFFUSION
+    away = toward - along_u
+    left = jnp.maximum(along_v, 0.0) + DIFFUSION
+    right = left - along_v
+    center = 1.0 - ((toward + away) + (left + right))
+    return [
+        center * fields[q]
+        + (toward * inner[q] + away * outer[q])
+        + (left * shifted(fields[q], 1, 1) + right * shifted(fields[q], -1, 1))
+        for q in range(2)
+    ]
+
+
+def window_means(ends, starts, gather):
+    packed = packed_sums(ends)
+    row = lax.broadcasted_iota(jnp.int32, packed.shape, 0)
+    packed = jnp.where(row % CF < 2, packed, shifted(packed_sums(starts), 2, 0))
+    return by_pieces(packed, gather)
+
+
+def passed_on(end, start, first_group):
+    coarse = advance(start, COARSE_COURANT, COARSE_DIFFUSION, 1)
+    defects = [end[q] - coarse[q] for q in range(2)]
+    return [jnp.where(first_group, coarse[q] + defects[q], defects[q]) for q in range(2)]
+
+
+def far_kernel(
+    far_ref, first_ref, second_ref, means_ref, gather_ref, end_ref, sent_ref, ends_ref, trail_ref, far_means_ref
+):
     odd = lax.axis_index("space") % 2 == 1
     first_group = lax.axis_index("tm") == 0
-    sign = jnp.where(odd, 1.0, -1.0)
-    turn = jnp.where(odd, 1, ROWS - 1)
     fields = [far_ref[0], far_ref[1]]
-    starts = packed_sums(fields)
-    row = lax.broadcasted_iota(jnp.int32, fields[0].shape, 0)
-    edge = row == jnp.where(odd, 0, ROWS - 1)
     for k in range(FSTEPS):
-        outer = fields
-        fields = [jnp.where(edge, first_ref[k, q], pltpu.roll(outer[q], turn, 0)) for q in range(2)]
-        inner = [jnp.where(edge, second_ref[k, q], pltpu.roll(fields[q], turn, 0)) for q in range(2)]
-        along_u, along_v = (sign * COURANT) * fields[0], COURANT * fields[1]
-        toward = jnp.maximum(along_u, 0.0) + DIFFUSION
-        away = toward - along_u
-        left = jnp.maximum(along_v, 0.0) + DIFFUSION
-        right = left - along_v
-        center = 1.0 - ((toward + away) + (left + right))
-        fields = [
-            center * fields[q]
-            + (toward * inner[q] + away * outer[q])
-            + (left * shifted(fields[q], 1, 1) + right * shifted(fields[q], -1, 1))
-            for q in range(2)
-        ]
+        fields = slanted(fields, first_ref[k], second_ref[k], odd)
+        if k < FSTEPS - 1:
+            for q in range(2):
+                trail_ref[k, q] = fields[q]
     for q in range(2):
         end_ref[q] = fields[q]
-    ends = packed_sums(fields)
-    pack = jnp.where(row % CF < 2, ends, shifted(starts, 2, 0))
-    far_means = by_pieces(pack, gather_ref[...])
+    far_means = window_means(fields, [far_ref[0], far_ref[1]], gather_ref[...])
+    far_means_ref[...] = far_means
     means = means_ref[...]
     near_means, near_ends = means[:ROWS], means[ROWS:]
     start, end = [], []
@@ -171,11 +190,46 @@
         high = [jnp.where(odd, that[i], this[i]) for i in range(2)]
         end.append(jnp.concatenate([none, *low, *high, none, none, none], axis=0))
         ends_ref[q] = jnp.concatenate([low[1], high[0]], axis=0)
-    coarse = advance(start, COARSE_COURANT, COARSE_DIFFUSION, 1)
-    for q in range(2):
-        defect = end[q] - coarse[q]
-        sent = jnp.where(first_group, coarse[q] + defect, defect)
-        sent_ref[q] = sent[EXT : EXT + 2 + 2 * EXT]
+    sent = passed_on(end, start, first_group)
+    for q in range(2):
+        sent_ref[q] = sent[q][EXT : EXT + 2 + 2 * EXT]
+
+
+def outer_kernel(
+    among, far_ref, trail_ref, farther_ref, far_means_ref, gather_ref, sent_ref, near_ref, window_ref
+):
+    odd = lax.axis_index("space") % 2 == 1
+    turn = jnp.where(odd, 1, ROWS - 1)
+    group = lax.axis_index("tm")
+
+    @pl.when(group >= among)
+    def _():
+        window_ref[...] = jnp.zeros_like(window_ref)
+
+    @pl.when(group < among)
+    def _():
+        fields = [farther_ref[0], farther_ref[1]]
+        for k in range(FSTEPS):
+            beside = far_ref if k == 0 else trail_ref.at[k - 1]
+            first = [pltpu.roll(beside[q], turn, 0) for q in range(2)]
+            second = [pltpu.roll(first[q], turn, 0) for q in range(2)]
+            fields = slanted(fields, first, second, odd)
+        outer_means = window_means(fields, [farther_ref[0], farther_ref[1]], gather_ref[...])
+        far_means = far_means_ref[...]
+        start, end = [], []
+        for q in range(2):
+            far, farther = sums_of(far_means, 2 + q), sums_of(outer_means, 2 + q)
+            none = jnp.zeros_like(far[0])
+            low = [jnp.where(odd, far[i], farther[i]) for i in range(2)]
+            high = [jnp.where(odd, farther[i], far[i]) for i in range(2)]
+            start.append(jnp.concatenate([*low, *high] + [none] * 4, axis=0))
+            end.append(jnp.concatenate([none, *sums_of(outer_means, q)] + [none] * 5, axis=0))
+        added = passed_on(end, start, group == 0)
+        for q in range(2):
+            rows = added[q][1:3]
+            low = jnp.where(odd, near_ref[q, :2], rows)
+            high = jnp.where(odd, rows, near_ref[q, 2:])
+            window_ref[q] = jnp.concatenate([low, sent_ref[q], high], axis=0)
 
 
 def window_kernel(depth, own_ref, near_ref, far_ref, *rest):
@@ -279,25 +333,24 @@
     )(*operands)
 
 
-def exchange(block, among):
+def from_near(block):
+    pairs = [(i, i ^ 1) for i in range(lax.axis_size("space"))]
+    return lax.ppermute(block, "space", pairs)
+
+
+def from_far(block, step, among):
     count, groups = lax.axis_size("space"), lax.axis_size("tm")
-    far = [(i, (i + 1 if i % 2 else i - 1) % count) for i in range(count)]
-    near = [(i, i ^ 1) for i in range(count)]
-    mixed = [
-        (t * count + a, t * count + b)
-        for t in range(groups)
-        for a, b in (far if t < among else near)
-    ]
-    from_far = lax.ppermute(block, ("tm", "space"), mixed)
-    from_near = lax.ppermute(block, "space", near)
-    return from_near, from_far
+    pairs = []
+    for t in range(groups):
+        for i in range(count):
+            away = step if (i + step) % 2 == 0 else -step
+            to = (i + away) % count if t < among else i ^ 1
+            pairs.append((t * count + i, t * count + to))
+    return lax.ppermute(block, ("tm", "space"), pairs)
 
 
 def forward(groups, distance):
-    pairs = [(i, (i + distance) % groups) for i in range(groups)]
-    if distance == 2 and groups > 2:
-        pairs[-2:] = [(groups - 2, 1), (groups - 1, 0)]
-    return pairs
+    return [(i, (i + distance) % groups) for i in range(groups)]
 
 
 def step(c_state):
@@ -307,7 +360,11 @@
     assert rows == HALO == ROWS and count % 2 == 0
     full, half = jnp.float32, jnp.bfloat16
     inner, wide = rows // CF, cols // CF
-    near, far = exchange(own, groups)
+    reach, among = groups - 1, groups - 1 - EXT
+    depth = -(-(reach - EXT) // inner)
+    far = from_far(own, 1, groups)
+    near = from_near(own)
+    farther = from_far(own, 2, among) if depth == 1 else None
     own_here, own_sums, gather, spread = call(
         ready_kernel,
         [
@@ -328,41 +385,52 @@
         (near, own_here, own_sums, gather),
         cost=8_000_000,
     )
-    end, sent, ends = call(
+    sent_shape = (2, inner + 2 * EXT, wide)
+    end, sent, ends, trail, far_means = call(
         far_kernel,
-        [(own.shape, full), ((2, inner + 2 * EXT, wide), full), ((2, inner, wide), full)],
+        [
+            (own.shape, full),
+            (sent_shape, full),
+            ((2, inner, wide), full),
+            ((FSTEPS - 1, *own.shape), full),
+            ((ROWS, wide), full),
+        ],
         (far, first, second, means, gather),
         cost=2_000_000,
     )
-    reach = groups - 1
-    depth = -(-(reach - EXT) // inner)
-    pieces = [sent, *exchange(sent, groups - 1 - EXT)]
-    for d in range(2, depth + 1):
-        for sign in (1, -1):
-            pairs = [(i, (i + sign * d) % count) for i in range(count)]
-            pieces.append(lax.ppermute(sent, "space", pairs))
-    (window,) = call(
-        functools.partial(window_kernel, depth),
-        [((2, inner * (2 * depth + 1) + 2 * EXT, wide), full)],
-        pieces,
-    )
+    near_rows = from_near(sent)
+    window = ((2, inner * (2 * depth + 1) + 2 * EXT, wide), full)
+    if depth == 1:
+        (window,) = call(
+            functools.partial(outer_kernel, among),
+            [window],
+            (far, trail, farther, far_means, gather, sent, near_rows),
+            cost=2_000_000,
+        )
+    else:
+        pieces = [sent, near_rows, from_far(sent, 1, among)]
+        for d in range(2, depth + 1):
+            for sign in (1, -1):
+                pairs = [(i, (i + sign * d) % count) for i in range(count)]
+                pieces.append(lax.ppermute(sent, "space", pairs))
+        (window,) = call(functools.partial(window_kernel, depth), [window], pieces)
     held = [sent]
     for k in range(1, groups):
         held.append(lax.ppermute(sent if k <= EXT else window, "tm", forward(groups, k)))
     whole = (own.shape, full)
     scratch = [pltpu.VMEM(own.shape, full), pltpu.SemaphoreType.DMA((OUT_PIECES,))]
-    among = min(groups, 1 + EXT)
+    early = min(groups, 1 + EXT)
     (after,) = call(
-        functools.partial(early_kernel, among),
+        functools.partial(early_kernel, early),
         [whole],
-        (kept, end, ends, spread, *held[:among]),
+        (kept, end, ends, spread, *held[:early]),
         cost=1_000_000,
         scratch=scratch,
         out=pl.BlockSpec(memory_space=pltpu.HBM),
     )
-    if groups > among:
+    if groups > early:
         (after,) = call(
-            functools.partial(late_kernel, groups, among),
+            functools.partial(late_kernel, groups, early),
             [whole],
             (after, kept, end, ends, spread, *held),
             cost=1_000_000,

time: 23 us -> 22.7 us (0.987)
  starting transfers between devices: 10.1 us -> 8.2 us
  Pallas kernels: 3.14 us -> 3.97 us
  waiting for transfers between devices: 8.63 us -> 9.35 us
    ppermute x4, starting transfers between devices: 6.24 us -> 4.11 us  [the longest x2 3.55 us: from_far(): return lax.ppermute(block, ('tm', 'space'), pairs)]
    pallas_call x6, Pallas kernels: 3.14 us -> 3.97 us  [call(): pl.pallas_call(kernel, out_shape=[jax.ShapeDtypeStruct(shape, dtype) for...]
    ppermute x4, waiting for transfers between devices: 3.09 us -> 3.81 us  [the longest x2 3.8 us: from_far(): return lax.ppermute(block, ('tm', 'space'), pairs)]
  transfers between devices with their start and end apart: 7 -> 7, of which waited for: 3 -> 3; matrix products, arithmetic and copies ran while one was open for 0% -> 0% of each run, Pallas kernels for 10% -> 14%
where the time goes in v6:
time: 22.7 us; the launch traced here: 22.6 us
  waiting for transfers between devices  9.35 us (41%)
  starting transfers between devices  8.2 us (36%)
  Pallas kernels  3.97 us (17%)
  local copies, waits for them, and re-layouts  0.97 us (4%)
    ppermute x3, waiting for transfers between devices, step(): lax.ppermute(sent if k <= EXT else window, 'tm', forward(groups, k))  5.54 us
    ppermute x3, starting transfers between devices, step(): lax.ppermute(sent if k <= EXT else window, 'tm', forward(groups, k))  4.09 us
    pallas_call x6, Pallas kernels, call(): pl.pallas_call(kernel, out_shape=[jax.ShapeDtypeStruct(shape, dtype) for...  3.97 us
    ppermute x2, waiting for transfers between devices, from_far(): return lax.ppermute(block, ('tm', 'space'), pairs)  3.8 us
    ppermute x2, starting transfers between devices, from_far(): return lax.ppermute(block, ('tm', 'space'), pairs)  3.55 us
    unnamed x2, local copies, waits for them, and re-layouts  0.97 us
    ppermute x2, starting transfers between devices, from_near(): return lax.ppermute(block, 'space', pairs)  0.56 us
  transfers between devices with their start and end apart: 7, of which 3 were waited for; matrix products, arithmetic and copies ran while one was open for 0% of the time, Pallas kernels for 14%

profile of v6, /device:TPU:0, one launch (start us, length us, event | category | flops | bytes accessed | tf_op | source)
XLA Modules:
  0.0 22.6 jit_solution(2276507979327488879)
XLA Ops:
  0.0 0.5 %collective-permute-start = (f32[2,8,2048]{2,1,0:T(8,128)}, f32[2,8,2048]{2,1,0:T(8,128)S(1)}, u32[]{:S(2)}, u32[]{:S(2)}) collective-permute-start(f32[2,8,2048]{2,1,0:T(8,128)} %bitcast.2), channel_id=1, source_target_pairs={{0,1},{1,0},{2,3},{3,2},{4,5},{5,4},{6,7},{7,6},{8,9},{9,8},{10,11... | collective-permute-start | bytes 393224 | tf_op jit(solution)/shard_map/ppermute | solution.py:338
  0.5 3.5 %collective-permute-start.1 = (f32[2,8,2048]{2,1,0:T(8,128)}, f32[2,8,2048]{2,1,0:T(8,128)S(1)}, u32[]{:S(2)}, u32[]{:S(2)}) collective-permute-start(f32[2,8,2048]{2,1,0:T(8,128)} %bitcast.3), channel_id=1, source_target_pairs={{0,7},{1,2},{2,1},{3,4},{4,3},{5,6},{6,5},{7,0},{8,15},{9,10},{10,... | collective-permute-start | bytes 393224 | tf_op jit(solution)/shard_map/ppermute | solution.py:349
  4.0 0.0 collective-permute-start.3
  4.0 0.0 copy-start
  4.0 1.0 %copy-done = f32[1,2,8,2048]{3,2,1,0:T(8,128)S(1)} copy-done((f32[1,2,8,2048]{3,2,1,0:T(8,128)S(1)}, f32[1,2,8,2048]{3,2,1,0:T(8,128)}, u32[]{:S(2)}) %copy-start) | copy-done | bytes 131096
  5.0 0.2 shard_map.17
  5.2 0.0 collective-permute-done.near_ref
  5.3 1.2 %shard_map.18 = (f32[4,2,8,2048]{3,2,1,0:T(8,128)S(1)}, f32[4,2,8,2048]{3,2,1,0:T(8,128)S(1)}, f32[2,8,2048]{2,1,0:T(8,128)S(1)}, f32[16,512]{1,0:T(8,128)S(1)}) custom-call(f32[2,8,2048]{2,1,0:T(8,128)S(1)} %collective-permute-done.near_ref, f32[2,8,2048]{2,1,0:T(8,128)S(1)} %get-tuple-element.18.own_ref, f32[8,2048]{1,0:T(8,128)S(1)} %get-tuple-element.19.sums_ref, ...), custom_call_target="tpu_custom_call" | custom-call | flops 8000000 | bytes 1000000 | tf_op jit(solution)/shard_map/pallas_call | solution.py:324
  6.4 1.6 %collective-permute-done.1.far_ref = f32[2,8,2048]{2,1,0:T(8,128)S(1)} collective-permute-done((f32[2,8,2048]{2,1,0:T(8,128)}, f32[2,8,2048]{2,1,0:T(8,128)S(1)}, u32[]{:S(2)}, u32[]{:S(2)}) %collective-permute-start.1) | collective-permute-done | bytes 131104 | tf_op jit(solution)/shard_map/ppermute | solution.py:349
  8.0 0.8 %shard_map.19 = (f32[2,8,2048]{2,1,0:T(8,128)S(1)}, f32[2,4,512]{2,1,0:T(4,128)S(1)}, f32[2,2,512]{2,1,0:T(2,128)S(1)}, f32[3,2,8,2048]{3,2,1,0:T(8,128)S(1)}, f32[8,512]{1,0:T(8,128)S(1)}) custom-call(f32[2,8,2048]{2,1,0:T(8,128)S(1)} %collective-permute-done.1.far_ref, f32[4,2,8,2048]{3,2,1,0:T(8,128)S(1)} %get-tuple-element.22.first_ref, ...), custom_call_target="tpu_custom_call" | custom-call | flops 2000000 | bytes 250000 | tf_op jit(solution)/shard_map/pallas_call | solution.py:324
  8.8 0.1 collective-permute-start.4
  8.9 2.2 %collective-permute-done.3.farther_ref = f32[2,8,2048]{2,1,0:T(8,128)S(1)} collective-permute-done((f32[2,8,2048]{2,1,0:T(8,128)}, f32[2,8,2048]{2,1,0:T(8,128)S(1)}, u32[]{:S(2)}, u32[]{:S(2)}) %collective-permute-start.3) | collective-permute-done | bytes 131104 | tf_op jit(solution)/shard_map/ppermute | solution.py:349
  11.1 0.0 collective-permute-done.4.near_ref
  11.1 0.8 %shard_map.21 = f32[2,8,512]{2,1,0:T(8,128)S(1)} custom-call(f32[2,8,2048]{2,1,0:T(8,128)S(1)} %collective-permute-done.1.far_ref, f32[3,2,8,2048]{3,2,1,0:T(8,128)S(1)} %get-tuple-element.29.trail_ref, f32[2,8,2048]{2,1,0:T(8,128)S(1)} %collective-permute-done.3.farther_ref, f32[8,512]{1,0:T(8,128)S(1)} %get-tuple-element.30.far_means_ref, ...), custom_call_target="tpu_custom_call" | custom-call | flops 2000000 | bytes 250000 | tf_op jit(solution)/shard_map/pallas_call | solution.py:324
  11.9 0.4 %collective-permute-start.5 = (f32[2,8,512]{2,1,0:T(8,128)S(1)}, f32[2,8,512]{2,1,0:T(8,128)S(1)}, u32[]{:S(2)}, u32[]{:S(2)}) collective-permute-start(f32[2,8,512]{2,1,0:T(8,128)S(1)} %shard_map.21), channel_id=1, source_target_pairs={{0,16},{8,24},{16,0},{24,8},{1,17},{9,25},{17,1},{25,9},{2,18},{10... | collective-permute-start | bytes 98312 | tf_op jit(solution)/shard_map/ppermute | solution.py:419
  12.3 3.7 %collective-permute-start.6 = (f32[2,8,512]{2,1,0:T(8,128)S(1)}, f32[2,8,512]{2,1,0:T(8,128)S(1)}, u32[]{:S(2)}, u32[]{:S(2)}) collective-permute-start(f32[2,8,512]{2,1,0:T(8,128)S(1)} %shard_map.21), channel_id=1, source_target_pairs={{0,24},{8,0},{16,8},{24,16},{1,25},{9,1},{17,9},{25,17},{2,26},{10... | collective-permute-start | bytes 98312 | tf_op jit(solution)/shard_map/ppermute | solution.py:419
  16.0 0.0 collective-permute-start.2
  16.0 5.5 %collective-permute-done.2.rest_1_ = f32[2,4,512]{2,1,0:T(4,128)S(1)} collective-permute-done((f32[2,4,512]{2,1,0:T(4,128)S(1)}, f32[2,4,512]{2,1,0:T(4,128)S(1)}, u32[]{:S(2)}, u32[]{:S(2)}) %collective-permute-start.2) | collective-permute-done | bytes 16416 | tf_op jit(solution)/shard_map/ppermute | solution.py:419
  21.6 0.9 %shard_map.20.before_hbm = f32[2,8,2048]{2,1,0:T(8,128)} custom-call(f32[2,8,2048]{2,1,0:T(8,128)S(1)} %get-tuple-element.21.kept_ref, f32[2,8,2048]{2,1,0:T(8,128)S(1)} %get-tuple-element.25.end_ref, f32[2,2,512]{2,1,0:T(2,128)S(1)} %get-tuple-element.26.ends_ref, bf16[128,512]{1,0:T(8,128)(2,1)S(1)} %get-tuple-element.27.spread_ref, ...), custom_call_target="tpu_custom_call" | custom-call | flops 1000000 | bytes 125000 | tf_op jit(solution)/shard_map/pallas_call | solution.py:324
  22.5 0.0 collective-permute-done.5.rest_2_
  22.5 0.0 collective-permute-done.6.rest_3_
  (1 shorter events, 0.0 us)
Async XLA Ops:
  0.0 5.2 %collective-permute-start = (f32[2,8,2048]{2,1,0:T(8,128)}, f32[2,8,2048]{2,1,0:T(8,128)S(1)}, u32[]{:S(2)}, u32[]{:S(2)}) collective-permute-start(f32[2,8,2048]{2,1,0:T(8,128)} %bitcast.2), channel_id=1, source_target_pairs={{0,1},{1,0},{2,3},{3,2},{4,5},{5,4},{6,7},{7,6},{8,9},{9,8},{10,11... | collective-permute-start | bytes 393224 | tf_op jit(solution)/shard_map/ppermute | solution.py:338
  0.5 7.5 %collective-permute-start.1 = (f32[2,8,2048]{2,1,0:T(8,128)}, f32[2,8,2048]{2,1,0:T(8,128)S(1)}, u32[]{:S(2)}, u32[]{:S(2)}) collective-permute-start(f32[2,8,2048]{2,1,0:T(8,128)} %bitcast.3), channel_id=1, source_target_pairs={{0,7},{1,2},{2,1},{3,4},{4,3},{5,6},{6,5},{7,0},{8,15},{9,10},{10,... | collective-permute-start | bytes 393224 | tf_op jit(solution)/shard_map/ppermute | solution.py:349
  4.0 7.1 %collective-permute-start.3 = (f32[2,8,2048]{2,1,0:T(8,128)}, f32[2,8,2048]{2,1,0:T(8,128)S(1)}, u32[]{:S(2)}, u32[]{:S(2)}) collective-permute-start(f32[2,8,2048]{2,1,0:T(8,128)} %bitcast.4), channel_id=1, source_target_pairs={{0,2},{1,7},{2,4},{3,1},{4,6},{5,3},{6,0},{7,5},{8,10},{9,15},{10,... | collective-permute-start | bytes 393224 | tf_op jit(solution)/shard_map/ppermute | solution.py:349
  4.0 1.0 %copy-start = (f32[1,2,8,2048]{3,2,1,0:T(8,128)S(1)}, f32[1,2,8,2048]{3,2,1,0:T(8,128)}, u32[]{:S(2)}) copy-start(f32[1,2,8,2048]{3,2,1,0:T(8,128)} %param.1) | copy-start | bytes 393220
  8.8 2.3 %collective-permute-start.4 = (f32[2,4,512]{2,1,0:T(4,128)S(1)}, f32[2,4,512]{2,1,0:T(4,128)S(1)}, u32[]{:S(2)}, u32[]{:S(2)}) collective-permute-start(f32[2,4,512]{2,1,0:T(4,128)S(1)} %get-tuple-element.28.rest_0_.sent_ref), channel_id=1, source_target_pairs={{0,1},{1,0},{2,3},{3,2},{4,5},{5,4},{6,7},{7,6},{8,9},{9,8},{10,11... | collective-permute-start | bytes 49160 | tf_op jit(solution)/shard_map/ppermute | solution.py:338
  11.9 10.6 %collective-permute-start.5 = (f32[2,8,512]{2,1,0:T(8,128)S(1)}, f32[2,8,512]{2,1,0:T(8,128)S(1)}, u32[]{:S(2)}, u32[]{:S(2)}) collective-permute-start(f32[2,8,512]{2,1,0:T(8,128)S(1)} %shard_map.21), channel_id=1, source_target_pairs={{0,16},{8,24},{16,0},{24,8},{1,17},{9,25},{17,1},{25,9},{2,18},{10... | collective-permute-start | bytes 98312 | tf_op jit(solution)/shard_map/ppermute | solution.py:419
  12.3 10.2 %collective-permute-start.6 = (f32[2,8,512]{2,1,0:T(8,128)S(1)}, f32[2,8,512]{2,1,0:T(8,128)S(1)}, u32[]{:S(2)}, u32[]{:S(2)}) collective-permute-start(f32[2,8,512]{2,1,0:T(8,128)S(1)} %shard_map.21), channel_id=1, source_target_pairs={{0,24},{8,0},{16,8},{24,16},{1,25},{9,1},{17,9},{25,17},{2,26},{10... | collective-permute-start | bytes 98312 | tf_op jit(solution)/shard_map/ppermute | solution.py:419
  16.0 5.5 %collective-permute-start.2 = (f32[2,4,512]{2,1,0:T(4,128)S(1)}, f32[2,4,512]{2,1,0:T(4,128)S(1)}, u32[]{:S(2)}, u32[]{:S(2)}) collective-permute-start(f32[2,4,512]{2,1,0:T(4,128)S(1)} %get-tuple-element.28.rest_0_.sent_ref), channel_id=1, source_target_pairs={{0,8},{8,16},{16,24},{24,0},{1,9},{9,17},{17,25},{25,1},{2,10},{10... | collective-permute-start | bytes 49160 | tf_op jit(solution)/shard_map/ppermute | solution.py:419

commit v7 on v6

--- a/solution.py
+++ b/solution.py
@@ -43,14 +43,15 @@
 
 
 def exact_dot(field, weights):
-    total = None
+    parts = []
     for part in range(3):
         piece = field.astype(jnp.bfloat16)
+        parts.append(piece)
         if part < 2:
             field = field - piece.astype(jnp.float32)
-        product = jnp.dot(piece, weights, preferred_element_type=jnp.float32)
-        total = product if total is None else total + product
-    return total
+    count = field.shape[0]
+    done = jnp.dot(jnp.concatenate(parts, axis=0), weights, preferred_element_type=jnp.float32)
+    return done[:count] + (done[count : 2 * count] + done[2 * count :])
 
 
 def block_weights(shape, value):
@@ -80,8 +81,12 @@
     return packed
 
 
-def sums_of(means, i):
-    return [means[i : i + 1], means[CF + i : CF + i + 1]]
+def place(base, tile, odd, moves):
+    row = lax.broadcasted_iota(jnp.int32, base.shape, 0)
+    for source, on_odd, on_even in moves:
+        turned = pltpu.roll(tile, jnp.where(odd, (on_odd - source) % ROWS, (on_even - source) % ROWS), 0)
+        base = jnp.where(row == jnp.where(odd, on_odd, on_even), turned, base)
+    return base
 
 
 def repeat_rows(first, second):
@@ -102,7 +107,7 @@
 
 
 def near_kernel(
-    near_ref, own_ref, sums_ref, gather_ref, first_ref, second_ref, kept_ref, means_ref
+    near_ref, own_ref, sums_ref, gather_ref, first_ref, second_ref, kept_ref, start_ref, end_ref
 ):
     odd = lax.axis_index("space") % 2 == 1
     fields = []
@@ -124,7 +129,12 @@
         kept_ref[q] = kept[q]
     end_sums = packed_sums(kept)
     both = by_pieces(jnp.concatenate([near_sums, end_sums], axis=0), gather_ref[...])
-    means_ref[...] = both
+    begun, ended = both[:ROWS], both[ROWS:]
+    none = jnp.zeros_like(begun)
+    for q in range(2):
+        own = ((2 + q, 1, 1), (CF + 2 + q, 2, 2))
+        start_ref[q] = place(none, begun, odd, ((q, 7, 3), (CF + q, 0, 4), *own))
+        end_ref[q] = place(none, ended, odd, ((q, 0, 2), (CF + q, 1, 3)))
 
 
 def slanted(outer, first, second, odd):
@@ -162,7 +172,17 @@
 
 
 def far_kernel(
-    far_ref, first_ref, second_ref, means_ref, gather_ref, end_ref, sent_ref, ends_ref, trail_ref, far_means_ref
+    far_ref,
+    first_ref,
+    second_ref,
+    near_start_ref,
+    near_end_ref,
+    gather_ref,
+    end_ref,
+    sent_ref,
+    ends_ref,
+    trail_ref,
+    far_means_ref,
 ):
     odd = lax.axis_index("space") % 2 == 1
     first_group = lax.axis_index("tm") == 0
@@ -176,23 +196,15 @@
         end_ref[q] = fields[q]
     far_means = window_means(fields, [far_ref[0], far_ref[1]], gather_ref[...])
     far_means_ref[...] = far_means
-    means = means_ref[...]
-    near_means, near_ends = means[:ROWS], means[ROWS:]
     start, end = [], []
     for q in range(2):
-        near, own, far = sums_of(near_means, q), sums_of(near_means, 2 + q), sums_of(far_means, 2 + q)
-        this, that = sums_of(near_ends, q), sums_of(far_means, q)
-        none = jnp.zeros_like(own[0])
-        low = [jnp.where(odd, near[i], far[i]) for i in range(2)]
-        high = [jnp.where(odd, far[i], near[i]) for i in range(2)]
-        start.append(jnp.concatenate([*low, *own, *high, none, none], axis=0))
-        low = [jnp.where(odd, this[i], that[i]) for i in range(2)]
-        high = [jnp.where(odd, that[i], this[i]) for i in range(2)]
-        end.append(jnp.concatenate([none, *low, *high, none, none, none], axis=0))
-        ends_ref[q] = jnp.concatenate([low[1], high[0]], axis=0)
+        moves = ((2 + q, 3, 7), (CF + 2 + q, 4, 0))
+        start.append(place(near_start_ref[q], far_means, odd, moves))
+        end.append(place(near_end_ref[q], far_means, odd, ((q, 2, 0), (CF + q, 3, 1))))
     sent = passed_on(end, start, first_group)
     for q in range(2):
-        sent_ref[q] = sent[q][EXT : EXT + 2 + 2 * EXT]
+        sent_ref[q] = sent[q][: 2 + 2 * EXT]
+        ends_ref[q] = end[q]
 
 
 def outer_kernel(
@@ -215,21 +227,23 @@
             second = [pltpu.roll(first[q], turn, 0) for q in range(2)]
             fields = slanted(fields, first, second, odd)
         outer_means = window_means(fields, [farther_ref[0], farther_ref[1]], gather_ref[...])
-        far_means = far_means_ref[...]
-        start, end = [], []
+        none = jnp.zeros((ROWS, outer_means.shape[1]), jnp.float32)
+        gap = none[:2]
+        start, end, window = [], [], []
         for q in range(2):
-            far, farther = sums_of(far_means, 2 + q), sums_of(outer_means, 2 + q)
-            none = jnp.zeros_like(far[0])
-            low = [jnp.where(odd, far[i], farther[i]) for i in range(2)]
-            high = [jnp.where(odd, farther[i], far[i]) for i in range(2)]
-            start.append(jnp.concatenate([*low, *high] + [none] * 4, axis=0))
-            end.append(jnp.concatenate([none, *sums_of(outer_means, q)] + [none] * 5, axis=0))
+            begun = place(none, far_means_ref[...], odd, ((2 + q, 5, 1), (CF + 2 + q, 6, 2)))
+            moves = ((2 + q, 7, 7), (CF + 2 + q, 0, 0))
+            start.append(place(begun, outer_means, odd, moves))
+            end.append(place(none, outer_means, odd, ((q, 6, 0), (CF + q, 7, 1))))
+            beside = jnp.concatenate([near_ref[q], near_ref[q]], axis=0)
+            middle = jnp.concatenate([gap, sent_ref[q], gap], axis=0)
+            row = lax.broadcasted_iota(jnp.int32, none.shape, 0)
+            window.append(jnp.where((row >= 2) & (row < 6), middle, beside))
         added = passed_on(end, start, group == 0)
+        fresh = (row >= 6) == odd
+        inside = (row >= 2) & (row < 6)
         for q in range(2):
-            rows = added[q][1:3]
-            low = jnp.where(odd, near_ref[q, :2], rows)
-            high = jnp.where(odd, rows, near_ref[q, 2:])
-            window_ref[q] = jnp.concatenate([low, sent_ref[q], high], axis=0)
+            window_ref[q] = jnp.where(fresh & jnp.logical_not(inside), added[q], window[q])
 
 
 def window_kernel(depth, own_ref, near_ref, far_ref, *rest):
@@ -279,7 +293,7 @@
     odd = lax.axis_index("space") % 2 == 1
     moves, own = [], []
     for q in range(2):
-        move = path[q][first : first + 2] - ends_ref[q]
+        move = path[q][first : first + 2] - ends_ref[q, EXT : EXT + 2]
         moves.append(repeat_rows(move[:1], move[1:]))
         upper = lax.broadcasted_iota(jnp.int32, kept_ref.shape[1:], 0) >= CF
         own.append(shifted(jnp.where(upper == odd, kept_ref[q], end_ref[q]), CF, 0))
@@ -379,9 +393,10 @@
         scratch=[pltpu.SemaphoreType.DMA],
     )
     edges = ((FSTEPS, *own.shape), full)
-    first, second, kept, means = call(
+    tile = ((2, ROWS, wide), full)
+    first, second, kept, near_start, near_end = call(
         near_kernel,
-        [edges, edges, (own.shape, full), ((2 * ROWS, wide), full)],
+        [edges, edges, (own.shape, full), tile, tile],
         (near, own_here, own_sums, gather),
         cost=8_000_000,
     )
@@ -391,11 +406,11 @@
         [
             (own.shape, full),
             (sent_shape, full),
-            ((2, inner, wide), full),
+            tile,
             ((FSTEPS - 1, *own.shape), full),
             ((ROWS, wide), full),
         ],
-        (far, first, second, means, gather),
+        (far, first, second, near_start, near_end, gather),
         cost=2_000_000,
     )
     near_rows = from_near(sent)

time: 22.7 us -> 22.6 us (level)
  no operation moved by 1% of the time
where the time goes in v7:
time: 22.6 us; the launch traced here: 22.5 us
  waiting for transfers between devices  9.41 us (42%)
  starting transfers between devices  8.2 us (36%)
  Pallas kernels  3.84 us (17%)
  local copies, waits for them, and re-layouts  0.97 us (4%)
    ppermute x3, waiting for transfers between devices, step(): lax.ppermute(sent if k <= EXT else window, 'tm', forward(groups, k))  5.54 us
    ppermute x3, starting transfers between devices, step(): lax.ppermute(sent if k <= EXT else window, 'tm', forward(groups, k))  4.09 us
    ppermute x2, waiting for transfers between devices, from_far(): return lax.ppermute(block, ('tm', 'space'), pairs)  3.87 us
    pallas_call x6, Pallas kernels, call(): pl.pallas_call(kernel, out_shape=[jax.ShapeDtypeStruct(shape, dtype) for...  3.84 us
    ppermute x2, starting transfers between devices, from_far(): return lax.ppermute(block, ('tm', 'space'), pairs)  3.55 us
    unnamed x2, local copies, waits for them, and re-layouts  0.97 us
    ppermute x2, starting transfers between devices, from_near(): return lax.ppermute(block, 'space', pairs)  0.56 us
  transfers between devices with their start and end apart: 7, of which 3 were waited for; matrix products, arithmetic and copies ran while one was open for 0% of the time, Pallas kernels for 14%

profile of v7, /device:TPU:0, one launch (start us, length us, event | category | flops | bytes accessed | tf_op | source)
XLA Modules:
  0.0 22.5 jit_solution(16076697056680926609)
XLA Ops:
  0.0 0.5 %collective-permute-start = (f32[2,8,2048]{2,1,0:T(8,128)}, f32[2,8,2048]{2,1,0:T(8,128)S(1)}, u32[]{:S(2)}, u32[]{:S(2)}) collective-permute-start(f32[2,8,2048]{2,1,0:T(8,128)} %bitcast.2), channel_id=1, source_target_pairs={{0,1},{1,0},{2,3},{3,2},{4,5},{5,4},{6,7},{7,6},{8,9},{9,8},{10,11... | collective-permute-start | bytes 393224 | tf_op jit(solution)/shard_map/ppermute | solution.py:352
  0.5 3.5 %collective-permute-start.1 = (f32[2,8,2048]{2,1,0:T(8,128)}, f32[2,8,2048]{2,1,0:T(8,128)S(1)}, u32[]{:S(2)}, u32[]{:S(2)}) collective-permute-start(f32[2,8,2048]{2,1,0:T(8,128)} %bitcast.3), channel_id=1, source_target_pairs={{0,7},{1,2},{2,1},{3,4},{4,3},{5,6},{6,5},{7,0},{8,15},{9,10},{10,... | collective-permute-start | bytes 393224 | tf_op jit(solution)/shard_map/ppermute | solution.py:363
  4.0 0.0 collective-permute-start.3
  4.0 0.0 copy-start
  4.0 1.0 %copy-done = f32[1,2,8,2048]{3,2,1,0:T(8,128)S(1)} copy-done((f32[1,2,8,2048]{3,2,1,0:T(8,128)S(1)}, f32[1,2,8,2048]{3,2,1,0:T(8,128)}, u32[]{:S(2)}) %copy-start) | copy-done | bytes 131096
  5.0 0.2 %shard_map.17 = (f32[2,8,2048]{2,1,0:T(8,128)S(1)}, f32[8,2048]{1,0:T(8,128)S(1)}, bf16[512,128]{1,0:T(8,128)(2,1)S(1)}, bf16[128,512]{1,0:T(8,128)(2,1)S(1)}) custom-call(f32[2,8,2048]{2,1,0:T(8,128)S(1)} %bitcast.5), custom_call_target="tpu_custom_call" | custom-call | flops 4000000 | bytes 500000 | tf_op jit(solution)/shard_map/pallas_call | solution.py:338
  5.2 0.0 collective-permute-done.near_ref
  5.3 1.2 %shard_map.18 = (f32[4,2,8,2048]{3,2,1,0:T(8,128)S(1)}, f32[4,2,8,2048]{3,2,1,0:T(8,128)S(1)}, f32[2,8,2048]{2,1,0:T(8,128)S(1)}, f32[2,8,512]{2,1,0:T(8,128)S(1)}, f32[2,8,512]{2,1,0:T(8,128)S(1)}) custom-call(f32[2,8,2048]{2,1,0:T(8,128)S(1)} %collective-permute-done.near_ref, f32[2,8,2048]{2,1,0:T(8,128)S(1)} %get-tuple-element.19.own_ref, ...), custom_call_target="tpu_custom_call" | custom-call | flops 8000000 | bytes 1000000 | tf_op jit(solution)/shard_map/pallas_call | solution.py:338
  6.4 1.6 %collective-permute-done.1.far_ref = f32[2,8,2048]{2,1,0:T(8,128)S(1)} collective-permute-done((f32[2,8,2048]{2,1,0:T(8,128)}, f32[2,8,2048]{2,1,0:T(8,128)S(1)}, u32[]{:S(2)}, u32[]{:S(2)}) %collective-permute-start.1) | collective-permute-done | bytes 131104 | tf_op jit(solution)/shard_map/ppermute | solution.py:363
  8.0 0.7 %shard_map.19 = (f32[2,8,2048]{2,1,0:T(8,128)S(1)}, f32[2,4,512]{2,1,0:T(4,128)S(1)}, f32[2,8,512]{2,1,0:T(8,128)S(1)}, f32[3,2,8,2048]{3,2,1,0:T(8,128)S(1)}, f32[8,512]{1,0:T(8,128)S(1)}) custom-call(f32[2,8,2048]{2,1,0:T(8,128)S(1)} %collective-permute-done.1.far_ref, f32[4,2,8,2048]{3,2,1,0:T(8,128)S(1)} %get-tuple-element.23.first_ref, ...), custom_call_target="tpu_custom_call" | custom-call | flops 2000000 | bytes 250000 | tf_op jit(solution)/shard_map/pallas_call | solution.py:338
  8.8 0.1 collective-permute-start.4
  8.8 2.3 %collective-permute-done.3.farther_ref = f32[2,8,2048]{2,1,0:T(8,128)S(1)} collective-permute-done((f32[2,8,2048]{2,1,0:T(8,128)}, f32[2,8,2048]{2,1,0:T(8,128)S(1)}, u32[]{:S(2)}, u32[]{:S(2)}) %collective-permute-start.3) | collective-permute-done | bytes 131104 | tf_op jit(solution)/shard_map/ppermute | solution.py:363
  11.1 0.0 collective-permute-done.4.near_ref
  11.1 0.8 %shard_map.21 = f32[2,8,512]{2,1,0:T(8,128)S(1)} custom-call(f32[2,8,2048]{2,1,0:T(8,128)S(1)} %collective-permute-done.1.far_ref, f32[3,2,8,2048]{3,2,1,0:T(8,128)S(1)} %get-tuple-element.31.trail_ref, f32[2,8,2048]{2,1,0:T(8,128)S(1)} %collective-permute-done.3.farther_ref, f32[8,512]{1,0:T(8,128)S(1)} %get-tuple-element.32.far_means_ref, ...), custom_call_target="tpu_custom_call" | custom-call | flops 2000000 | bytes 250000 | tf_op jit(solution)/shard_map/pallas_call | solution.py:338
  11.9 0.4 %collective-permute-start.5 = (f32[2,8,512]{2,1,0:T(8,128)S(1)}, f32[2,8,512]{2,1,0:T(8,128)S(1)}, u32[]{:S(2)}, u32[]{:S(2)}) collective-permute-start(f32[2,8,512]{2,1,0:T(8,128)S(1)} %shard_map.21), channel_id=1, source_target_pairs={{0,16},{8,24},{16,0},{24,8},{1,17},{9,25},{17,1},{25,9},{2,18},{10... | collective-permute-start | bytes 98312 | tf_op jit(solution)/shard_map/ppermute | solution.py:434
  12.2 3.7 %collective-permute-start.6 = (f32[2,8,512]{2,1,0:T(8,128)S(1)}, f32[2,8,512]{2,1,0:T(8,128)S(1)}, u32[]{:S(2)}, u32[]{:S(2)}) collective-permute-start(f32[2,8,512]{2,1,0:T(8,128)S(1)} %shard_map.21), channel_id=1, source_target_pairs={{0,24},{8,0},{16,8},{24,16},{1,25},{9,1},{17,9},{25,17},{2,26},{10... | collective-permute-start | bytes 98312 | tf_op jit(solution)/shard_map/ppermute | solution.py:434
  16.0 0.0 collective-permute-start.2
  16.0 5.5 %collective-permute-done.2.rest_1_ = f32[2,4,512]{2,1,0:T(4,128)S(1)} collective-permute-done((f32[2,4,512]{2,1,0:T(4,128)S(1)}, f32[2,4,512]{2,1,0:T(4,128)S(1)}, u32[]{:S(2)}, u32[]{:S(2)}) %collective-permute-start.2) | collective-permute-done | bytes 16416 | tf_op jit(solution)/shard_map/ppermute | solution.py:434
  21.5 0.9 %shard_map.20.before_hbm = f32[2,8,2048]{2,1,0:T(8,128)} custom-call(f32[2,8,2048]{2,1,0:T(8,128)S(1)} %get-tuple-element.22.kept_ref, f32[2,8,2048]{2,1,0:T(8,128)S(1)} %get-tuple-element.27.end_ref, f32[2,8,512]{2,1,0:T(8,128)S(1)} %get-tuple-element.28.ends_ref, bf16[128,512]{1,0:T(8,128)(2,1)S(1)} %get-tuple-element.29.spread_ref, ...), custom_call_target="tpu_custom_call" | custom-call | flops 1000000 | bytes 125000 | tf_op jit(solution)/shard_map/pallas_call | solution.py:338
  22.4 0.0 collective-permute-done.5.rest_2_
  22.5 0.0 collective-permute-done.6.rest_3_
  (1 shorter events, 0.0 us)
Async XLA Ops:
  0.0 5.2 %collective-permute-start = (f32[2,8,2048]{2,1,0:T(8,128)}, f32[2,8,2048]{2,1,0:T(8,128)S(1)}, u32[]{:S(2)}, u32[]{:S(2)}) collective-permute-start(f32[2,8,2048]{2,1,0:T(8,128)} %bitcast.2), channel_id=1, source_target_pairs={{0,1},{1,0},{2,3},{3,2},{4,5},{5,4},{6,7},{7,6},{8,9},{9,8},{10,11... | collective-permute-start | bytes 393224 | tf_op jit(solution)/shard_map/ppermute | solution.py:352
  0.5 7.5 %collective-permute-start.1 = (f32[2,8,2048]{2,1,0:T(8,128)}, f32[2,8,2048]{2,1,0:T(8,128)S(1)}, u32[]{:S(2)}, u32[]{:S(2)}) collective-permute-start(f32[2,8,2048]{2,1,0:T(8,128)} %bitcast.3), channel_id=1, source_target_pairs={{0,7},{1,2},{2,1},{3,4},{4,3},{5,6},{6,5},{7,0},{8,15},{9,10},{10,... | collective-permute-start | bytes 393224 | tf_op jit(solution)/shard_map/ppermute | solution.py:363
  4.0 7.1 %collective-permute-start.3 = (f32[2,8,2048]{2,1,0:T(8,128)}, f32[2,8,2048]{2,1,0:T(8,128)S(1)}, u32[]{:S(2)}, u32[]{:S(2)}) collective-permute-start(f32[2,8,2048]{2,1,0:T(8,128)} %bitcast.4), channel_id=1, source_target_pairs={{0,2},{1,7},{2,4},{3,1},{4,6},{5,3},{6,0},{7,5},{8,10},{9,15},{10,... | collective-permute-start | bytes 393224 | tf_op jit(solution)/shard_map/ppermute | solution.py:363
  4.0 1.0 %copy-start = (f32[1,2,8,2048]{3,2,1,0:T(8,128)S(1)}, f32[1,2,8,2048]{3,2,1,0:T(8,128)}, u32[]{:S(2)}) copy-start(f32[1,2,8,2048]{3,2,1,0:T(8,128)} %param.1) | copy-start | bytes 393220
  8.8 2.4 %collective-permute-start.4 = (f32[2,4,512]{2,1,0:T(4,128)S(1)}, f32[2,4,512]{2,1,0:T(4,128)S(1)}, u32[]{:S(2)}, u32[]{:S(2)}) collective-permute-start(f32[2,4,512]{2,1,0:T(4,128)S(1)} %get-tuple-element.30.rest_0_.sent_ref), channel_id=1, source_target_pairs={{0,1},{1,0},{2,3},{3,2},{4,5},{5,4},{6,7},{7,6},{8,9},{9,8},{10,11... | collective-permute-start | bytes 49160 | tf_op jit(solution)/shard_map/ppermute | solution.py:352
  11.9 10.6 %collective-permute-start.5 = (f32[2,8,512]{2,1,0:T(8,128)S(1)}, f32[2,8,512]{2,1,0:T(8,128)S(1)}, u32[]{:S(2)}, u32[]{:S(2)}) collective-permute-start(f32[2,8,512]{2,1,0:T(8,128)S(1)} %shard_map.21), channel_id=1, source_target_pairs={{0,16},{8,24},{16,0},{24,8},{1,17},{9,25},{17,1},{25,9},{2,18},{10... | collective-permute-start | bytes 98312 | tf_op jit(solution)/shard_map/ppermute | solution.py:434
  12.2 10.2 %collective-permute-start.6 = (f32[2,8,512]{2,1,0:T(8,128)S(1)}, f32[2,8,512]{2,1,0:T(8,128)S(1)}, u32[]{:S(2)}, u32[]{:S(2)}) collective-permute-start(f32[2,8,512]{2,1,0:T(8,128)S(1)} %shard_map.21), channel_id=1, source_target_pairs={{0,24},{8,0},{16,8},{24,16},{1,25},{9,1},{17,9},{25,17},{2,26},{10... | collective-permute-start | bytes 98312 | tf_op jit(solution)/shard_map/ppermute | solution.py:434
  16.0 5.5 %collective-permute-start.2 = (f32[2,4,512]{2,1,0:T(4,128)S(1)}, f32[2,4,512]{2,1,0:T(4,128)S(1)}, u32[]{:S(2)}, u32[]{:S(2)}) collective-permute-start(f32[2,4,512]{2,1,0:T(4,128)S(1)} %get-tuple-element.30.rest_0_.sent_ref), channel_id=1, source_target_pairs={{0,8},{8,16},{16,24},{24,0},{1,9},{9,17},{17,25},{25,1},{2,10},{10... | collective-permute-start | bytes 49160 | tf_op jit(solution)/shard_map/ppermute | solution.py:434

commit v8 on v7

--- a/solution.py
+++ b/solution.py
@@ -20,6 +20,7 @@
 VMEM = pl.BlockSpec(memory_space=pltpu.VMEM)
 ROWS = 8
 OUT_PIECES = 2
+HOLD_TURNS = 80
 
 
 def shifted(field, amount, axis):
@@ -97,7 +98,7 @@
     )
 
 
-def ready_kernel(own_hbm, own_ref, sums_ref, gather_ref, spread_ref, sem):
+def ready_kernel(held_ref, own_hbm, own_ref, sums_ref, gather_ref, spread_ref, sem):
     load = pltpu.make_async_copy(own_hbm, own_ref, sem)
     load.start()
     gather_ref[...] = block_weights(gather_ref.shape, 1.0 / (CF * CF))
@@ -333,8 +334,12 @@
         )
 
 
-def call(kernel, shapes, operands, cost=0, hbm=(), scratch=(), out=VMEM, alias=None):
-    where = [pl.BlockSpec(memory_space=pl.ANY) if i in hbm else VMEM for i in range(len(operands))]
+def call(kernel, shapes, operands, cost=0, hbm=(), smem=(), scratch=(), out=VMEM, alias=None):
+    where = [VMEM] * len(operands)
+    for i in hbm:
+        where[i] = pl.BlockSpec(memory_space=pl.ANY)
+    for i in smem:
+        where[i] = pl.BlockSpec(memory_space=pltpu.SMEM)
     return pl.pallas_call(
         kernel,
         out_shape=[jax.ShapeDtypeStruct(shape, dtype) for shape, dtype in shapes],
@@ -347,6 +352,12 @@
     )(*operands)
 
 
+def hold():
+    at = lax.axis_index("space") % 4
+    turns = jnp.where((at == 1) | (at == 2), HOLD_TURNS, 0)
+    return lax.fori_loop(0, turns, lambda i, x: x * 1664525 + 1013904223, at)
+
+
 def from_near(block):
     pairs = [(i, i ^ 1) for i in range(lax.axis_size("space"))]
     return lax.ppermute(block, "space", pairs)
@@ -364,7 +375,10 @@
 
 
 def forward(groups, distance):
-    return [(i, (i + distance) % groups) for i in range(groups)]
+    pairs = [(i, (i + distance) % groups) for i in range(groups)]
+    if distance == 2 and groups > 2:
+        pairs[-2:] = [(groups - 2, 1), (groups - 1, 0)]
+    return pairs
 
 
 def step(c_state):
@@ -376,6 +390,7 @@
     inner, wide = rows // CF, cols // CF
     reach, among = groups - 1, groups - 1 - EXT
     depth = -(-(reach - EXT) // inner)
+    held_back = hold()
     far = from_far(own, 1, groups)
     near = from_near(own)
     farther = from_far(own, 2, among) if depth == 1 else None
@@ -387,9 +402,10 @@
             ((CF * LANES, LANES), half),
             ((LANES, CF * LANES), half),
         ],
-        (own,),
+        (held_back.reshape(1), own),
         cost=4_000_000,
-        hbm=(0,),
+        hbm=(1,),
+        smem=(0,),
         scratch=[pltpu.SemaphoreType.DMA],
     )
     edges = ((FSTEPS, *own.shape), full)

time: 22.6 us -> 22.4 us (level)
  no operation moved by 1% of the time
where the time goes in v8:
time: 22.4 us; the launch traced here: 22.3 us
  waiting for transfers between devices  9.41 us (42%)
  starting transfers between devices  7.99 us (36%)
  Pallas kernels  3.85 us (17%)
  local copies, waits for them, and re-layouts  0.97 us (4%)
    ppermute x3, waiting for transfers between devices, step(): lax.ppermute(sent if k <= EXT else window, 'tm', forward(groups, k))  5.54 us
    ppermute x3, starting transfers between devices, step(): lax.ppermute(sent if k <= EXT else window, 'tm', forward(groups, k))  3.88 us
    ppermute x2, waiting for transfers between devices, from_far(): return lax.ppermute(block, ('tm', 'space'), pairs)  3.87 us
    pallas_call x6, Pallas kernels, call(): pl.pallas_call(kernel, out_shape=[jax.ShapeDtypeStruct(shape, dtype) for...  3.85 us
    ppermute x2, starting transfers between devices, from_far(): return lax.ppermute(block, ('tm', 'space'), pairs)  3.55 us
    unnamed x2, local copies, waits for them, and re-layouts  0.97 us
    ppermute x2, starting transfers between devices, from_near(): return lax.ppermute(block, 'space', pairs)  0.56 us
  transfers between devices with their start and end apart: 7, of which 3 were waited for; matrix products, arithmetic and copies ran while one was open for 0% of the time, Pallas kernels for 14%

profile of v8, /device:TPU:0, one launch (start us, length us, event | category | flops | bytes accessed | tf_op | source)
XLA Modules:
  0.0 22.3 jit_solution(3452356519697755596)
XLA Ops:
  0.0 0.5 %collective-permute-start = (f32[2,8,2048]{2,1,0:T(8,128)}, f32[2,8,2048]{2,1,0:T(8,128)S(1)}, u32[]{:S(2)}, u32[]{:S(2)}) collective-permute-start(f32[2,8,2048]{2,1,0:T(8,128)} %bitcast.3), channel_id=1, source_target_pairs={{0,1},{1,0},{2,3},{3,2},{4,5},{5,4},{6,7},{7,6},{8,9},{9,8},{10,11... | collective-permute-start | bytes 393224 | tf_op jit(solution)/shard_map/ppermute | solution.py:363
  0.5 3.5 %collective-permute-start.1 = (f32[2,8,2048]{2,1,0:T(8,128)}, f32[2,8,2048]{2,1,0:T(8,128)S(1)}, u32[]{:S(2)}, u32[]{:S(2)}) collective-permute-start(f32[2,8,2048]{2,1,0:T(8,128)} %bitcast.4), channel_id=1, source_target_pairs={{0,7},{1,2},{2,1},{3,4},{4,3},{5,6},{6,5},{7,0},{8,15},{9,10},{10,... | collective-permute-start | bytes 393224 | tf_op jit(solution)/shard_map/ppermute | solution.py:374
  4.0 0.0 collective-permute-start.3
  4.0 0.0 copy-start
  4.0 1.0 %copy-done = f32[1,2,8,2048]{3,2,1,0:T(8,128)S(1)} copy-done((f32[1,2,8,2048]{3,2,1,0:T(8,128)S(1)}, f32[1,2,8,2048]{3,2,1,0:T(8,128)}, u32[]{:S(2)}) %copy-start) | copy-done | bytes 131096
  5.0 0.2 %shard_map.17 = (f32[2,8,2048]{2,1,0:T(8,128)S(1)}, f32[8,2048]{1,0:T(8,128)S(1)}, bf16[512,128]{1,0:T(8,128)(2,1)S(1)}, bf16[128,512]{1,0:T(8,128)(2,1)S(1)}) custom-call(s32[1]{0:T(128)} %bitcast.1.held_ref, f32[2,8,2048]{2,1,0:T(8,128)S(1)} %bitcast.6), custom_call_target="tpu_custom_call" | custom-call | flops 4000000 | bytes 500000 | tf_op jit(solution)/shard_map/pallas_call | solution.py:343
  5.2 0.0 collective-permute-done.near_ref
  5.3 1.2 %shard_map.18 = (f32[4,2,8,2048]{3,2,1,0:T(8,128)S(1)}, f32[4,2,8,2048]{3,2,1,0:T(8,128)S(1)}, f32[2,8,2048]{2,1,0:T(8,128)S(1)}, f32[2,8,512]{2,1,0:T(8,128)S(1)}, f32[2,8,512]{2,1,0:T(8,128)S(1)}) custom-call(f32[2,8,2048]{2,1,0:T(8,128)S(1)} %collective-permute-done.near_ref, f32[2,8,2048]{2,1,0:T(8,128)S(1)} %get-tuple-element.38.own_ref, ...), custom_call_target="tpu_custom_call" | custom-call | flops 8000000 | bytes 1000000 | tf_op jit(solution)/shard_map/pallas_call | solution.py:343
  6.4 1.6 %collective-permute-done.1.far_ref = f32[2,8,2048]{2,1,0:T(8,128)S(1)} collective-permute-done((f32[2,8,2048]{2,1,0:T(8,128)}, f32[2,8,2048]{2,1,0:T(8,128)S(1)}, u32[]{:S(2)}, u32[]{:S(2)}) %collective-permute-start.1) | collective-permute-done | bytes 131104 | tf_op jit(solution)/shard_map/ppermute | solution.py:374
  8.0 0.7 %shard_map.19 = (f32[2,8,2048]{2,1,0:T(8,128)S(1)}, f32[2,4,512]{2,1,0:T(4,128)S(1)}, f32[2,8,512]{2,1,0:T(8,128)S(1)}, f32[3,2,8,2048]{3,2,1,0:T(8,128)S(1)}, f32[8,512]{1,0:T(8,128)S(1)}) custom-call(f32[2,8,2048]{2,1,0:T(8,128)S(1)} %collective-permute-done.1.far_ref, f32[4,2,8,2048]{3,2,1,0:T(8,128)S(1)} %get-tuple-element.42.first_ref, ...), custom_call_target="tpu_custom_call" | custom-call | flops 2000000 | bytes 250000 | tf_op jit(solution)/shard_map/pallas_call | solution.py:343
  8.8 0.1 collective-permute-start.4
  8.8 2.3 %collective-permute-done.3.farther_ref = f32[2,8,2048]{2,1,0:T(8,128)S(1)} collective-permute-done((f32[2,8,2048]{2,1,0:T(8,128)}, f32[2,8,2048]{2,1,0:T(8,128)S(1)}, u32[]{:S(2)}, u32[]{:S(2)}) %collective-permute-start.3) | collective-permute-done | bytes 131104 | tf_op jit(solution)/shard_map/ppermute | solution.py:374
  11.1 0.0 collective-permute-done.4.near_ref
  11.1 0.8 %shard_map.21 = f32[2,8,512]{2,1,0:T(8,128)S(1)} custom-call(f32[2,8,2048]{2,1,0:T(8,128)S(1)} %collective-permute-done.1.far_ref, f32[3,2,8,2048]{3,2,1,0:T(8,128)S(1)} %get-tuple-element.50.trail_ref, f32[2,8,2048]{2,1,0:T(8,128)S(1)} %collective-permute-done.3.farther_ref, f32[8,512]{1,0:T(8,128)S(1)} %get-tuple-element.51.far_means_ref, ...), custom_call_target="tpu_custom_call" | custom-call | flops 2000000 | bytes 250000 | tf_op jit(solution)/shard_map/pallas_call | solution.py:343
  11.9 0.4 %collective-permute-start.5 = (f32[2,8,512]{2,1,0:T(8,128)S(1)}, f32[2,8,512]{2,1,0:T(8,128)S(1)}, u32[]{:S(2)}, u32[]{:S(2)}) collective-permute-start(f32[2,8,512]{2,1,0:T(8,128)S(1)} %shard_map.21), channel_id=1, source_target_pairs={{0,16},{8,24},{16,8},{24,0},{1,17},{9,25},{17,9},{25,1},{2,18},{10... | collective-permute-start | bytes 98312 | tf_op jit(solution)/shard_map/ppermute | solution.py:450
  12.2 3.5 %collective-permute-start.6 = (f32[2,8,512]{2,1,0:T(8,128)S(1)}, f32[2,8,512]{2,1,0:T(8,128)S(1)}, u32[]{:S(2)}, u32[]{:S(2)}) collective-permute-start(f32[2,8,512]{2,1,0:T(8,128)S(1)} %shard_map.21), channel_id=1, source_target_pairs={{0,24},{8,0},{16,8},{24,16},{1,25},{9,1},{17,9},{25,17},{2,26},{10... | collective-permute-start | bytes 98312 | tf_op jit(solution)/shard_map/ppermute | solution.py:450
  15.8 0.0 collective-permute-start.2
  15.8 5.5 %collective-permute-done.2.rest_1_ = f32[2,4,512]{2,1,0:T(4,128)S(1)} collective-permute-done((f32[2,4,512]{2,1,0:T(4,128)S(1)}, f32[2,4,512]{2,1,0:T(4,128)S(1)}, u32[]{:S(2)}, u32[]{:S(2)}) %collective-permute-start.2) | collective-permute-done | bytes 16416 | tf_op jit(solution)/shard_map/ppermute | solution.py:450
  21.3 0.9 %shard_map.20.before_hbm = f32[2,8,2048]{2,1,0:T(8,128)} custom-call(f32[2,8,2048]{2,1,0:T(8,128)S(1)} %get-tuple-element.41.kept_ref, f32[2,8,2048]{2,1,0:T(8,128)S(1)} %get-tuple-element.46.end_ref, f32[2,8,512]{2,1,0:T(8,128)S(1)} %get-tuple-element.47.ends_ref, bf16[128,512]{1,0:T(8,128)(2,1)S(1)} %get-tuple-element.48.spread_ref, ...), custom_call_target="tpu_custom_call" | custom-call | flops 1000000 | bytes 125000 | tf_op jit(solution)/shard_map/pallas_call | solution.py:343
  22.2 0.0 collective-permute-done.5.rest_2_
  22.2 0.0 collective-permute-done.6.rest_3_
  (2 shorter events, 0.0 us)
Async XLA Ops:
  0.0 5.2 %collective-permute-start = (f32[2,8,2048]{2,1,0:T(8,128)}, f32[2,8,2048]{2,1,0:T(8,128)S(1)}, u32[]{:S(2)}, u32[]{:S(2)}) collective-permute-start(f32[2,8,2048]{2,1,0:T(8,128)} %bitcast.3), channel_id=1, source_target_pairs={{0,1},{1,0},{2,3},{3,2},{4,5},{5,4},{6,7},{7,6},{8,9},{9,8},{10,11... | collective-permute-start | bytes 393224 | tf_op jit(solution)/shard_map/ppermute | solution.py:363
  0.5 7.5 %collective-permute-start.1 = (f32[2,8,2048]{2,1,0:T(8,128)}, f32[2,8,2048]{2,1,0:T(8,128)S(1)}, u32[]{:S(2)}, u32[]{:S(2)}) collective-permute-start(f32[2,8,2048]{2,1,0:T(8,128)} %bitcast.4), channel_id=1, source_target_pairs={{0,7},{1,2},{2,1},{3,4},{4,3},{5,6},{6,5},{7,0},{8,15},{9,10},{10,... | collective-permute-start | bytes 393224 | tf_op jit(solution)/shard_map/ppermute | solution.py:374
  4.0 7.1 %collective-permute-start.3 = (f32[2,8,2048]{2,1,0:T(8,128)}, f32[2,8,2048]{2,1,0:T(8,128)S(1)}, u32[]{:S(2)}, u32[]{:S(2)}) collective-permute-start(f32[2,8,2048]{2,1,0:T(8,128)} %bitcast.5), channel_id=1, source_target_pairs={{0,2},{1,7},{2,4},{3,1},{4,6},{5,3},{6,0},{7,5},{8,10},{9,15},{10,... | collective-permute-start | bytes 393224 | tf_op jit(solution)/shard_map/ppermute | solution.py:374
  4.0 1.0 %copy-start = (f32[1,2,8,2048]{3,2,1,0:T(8,128)S(1)}, f32[1,2,8,2048]{3,2,1,0:T(8,128)}, u32[]{:S(2)}) copy-start(f32[1,2,8,2048]{3,2,1,0:T(8,128)} %param.3) | copy-start | bytes 393220
  8.8 2.4 %collective-permute-start.4 = (f32[2,4,512]{2,1,0:T(4,128)S(1)}, f32[2,4,512]{2,1,0:T(4,128)S(1)}, u32[]{:S(2)}, u32[]{:S(2)}) collective-permute-start(f32[2,4,512]{2,1,0:T(4,128)S(1)} %get-tuple-element.49.rest_0_.sent_ref), channel_id=1, source_target_pairs={{0,1},{1,0},{2,3},{3,2},{4,5},{5,4},{6,7},{7,6},{8,9},{9,8},{10,11... | collective-permute-start | bytes 49160 | tf_op jit(solution)/shard_map/ppermute | solution.py:363
  11.9 10.4 %collective-permute-start.5 = (f32[2,8,512]{2,1,0:T(8,128)S(1)}, f32[2,8,512]{2,1,0:T(8,128)S(1)}, u32[]{:S(2)}, u32[]{:S(2)}) collective-permute-start(f32[2,8,512]{2,1,0:T(8,128)S(1)} %shard_map.21), channel_id=1, source_target_pairs={{0,16},{8,24},{16,8},{24,0},{1,17},{9,25},{17,9},{25,1},{2,18},{10... | collective-permute-start | bytes 98312 | tf_op jit(solution)/shard_map/ppermute | solution.py:450
  12.2 10.0 %collective-permute-start.6 = (f32[2,8,512]{2,1,0:T(8,128)S(1)}, f32[2,8,512]{2,1,0:T(8,128)S(1)}, u32[]{:S(2)}, u32[]{:S(2)}) collective-permute-start(f32[2,8,512]{2,1,0:T(8,128)S(1)} %shard_map.21), channel_id=1, source_target_pairs={{0,24},{8,0},{16,8},{24,16},{1,25},{9,1},{17,9},{25,17},{2,26},{10... | collective-permute-start | bytes 98312 | tf_op jit(solution)/shard_map/ppermute | solution.py:450
  15.8 5.5 %collective-permute-start.2 = (f32[2,4,512]{2,1,0:T(4,128)S(1)}, f32[2,4,512]{2,1,0:T(4,128)S(1)}, u32[]{:S(2)}, u32[]{:S(2)}) collective-permute-start(f32[2,4,512]{2,1,0:T(4,128)S(1)} %get-tuple-element.49.rest_0_.sent_ref), channel_id=1, source_target_pairs={{0,8},{8,16},{16,24},{24,0},{1,9},{9,17},{17,25},{25,1},{2,10},{10... | collective-permute-start | bytes 49160 | tf_op jit(solution)/shard_map/ppermute | solution.py:450

commit v9 on v8

--- a/solution.py
+++ b/solution.py
@@ -21,6 +21,7 @@
 ROWS = 8
 OUT_PIECES = 2
 HOLD_TURNS = 80
+BRANCHES = 4
 
 
 def shifted(field, amount, axis):
@@ -275,9 +276,12 @@
             term = jnp.concatenate([none, term, none], axis=0)
         return term
 
-    terms = [[placed(ref, q) for q in range(2)] for ref in held]
+    known = isinstance(group, int)
+    terms = [[placed(ref, q) for q in range(2)] for ref in held[: group + 1 if known else None]]
 
     def of(index):
+        if known:
+            return terms[group - index]
         if index == groups - 1:
             return terms[0]
         picked = terms[min(len(terms) - 1, groups - 1 - index)]
@@ -286,10 +290,11 @@
         return picked
 
     path = of(0)
-    for index in range(1, groups):
+    for index in range(1, group + 1 if known else groups):
         term = of(index)
         after = advance(path, COARSE_COURANT, COARSE_DIFFUSION, 1)
-        path = [jnp.where(index <= group, after[q] + term[q], path[q]) for q in range(2)]
+        after = [after[q] + term[q] for q in range(2)]
+        path = after if known else [jnp.where(index <= group, after[q], path[q]) for q in range(2)]
     first = (reach - 2) // 2
     odd = lax.axis_index("space") % 2 == 1
     moves, own = [], []
@@ -312,26 +317,24 @@
         copy.wait()
 
 
+def by_group(first, last, *refs):
+    group = lax.axis_index("tm")
+    if last <= BRANCHES:
+        for g in range(first, last):
+            pl.when(group == g)(functools.partial(corrected, g, last, *refs))
+    else:
+        inside = (group >= first) & (group < last)
+        pl.when(inside)(functools.partial(corrected, group, last, *refs))
+
+
 def early_kernel(among, kept_ref, end_ref, ends_ref, spread_ref, *rest):
     held, (out_hbm, stage_ref, sems) = rest[:-3], rest[-3:]
-    group = lax.axis_index("tm")
-
-    @pl.when(group < among)
-    def _():
-        corrected(
-            group, among, held, kept_ref, end_ref, ends_ref, spread_ref, out_hbm, stage_ref, sems
-        )
+    by_group(0, among, held, kept_ref, end_ref, ends_ref, spread_ref, out_hbm, stage_ref, sems)
 
 
 def late_kernel(groups, among, before_hbm, kept_ref, end_ref, ends_ref, spread_ref, *rest):
     held, (out_hbm, stage_ref, sems) = rest[:-3], rest[-3:]
-    group = lax.axis_index("tm")
-
-    @pl.when(group >= among)
-    def _():
-        corrected(
-            group, groups, held, kept_ref, end_ref, ends_ref, spread_ref, out_hbm, stage_ref, sems
-        )
+    by_group(among, groups, held, kept_ref, end_ref, ends_ref, spread_ref, out_hbm, stage_ref, sems)
 
 
 def call(kernel, shapes, operands, cost=0, hbm=(), smem=(), scratch=(), out=VMEM, alias=None):

time: 22.4 us -> 22.4 us (level)
  transfers between devices with their start and end apart: 7 -> 7, of which waited for: 3 -> 3; matrix products, arithmetic and copies ran while one was open for 0% -> 0% of each run, Pallas kernels for 14% -> 13%
where the time goes in v9:
time: 22.4 us; the launch traced here: 22.2 us
  waiting for transfers between devices  9.41 us (42%)
  starting transfers between devices  7.99 us (36%)
  Pallas kernels  3.77 us (17%)
  local copies, waits for them, and re-layouts  0.97 us (4%)
    ppermute x3, waiting for transfers between devices, step(): lax.ppermute(sent if k <= EXT else window, 'tm', forward(groups, k))  5.54 us
    ppermute x3, starting transfers between devices, step(): lax.ppermute(sent if k <= EXT else window, 'tm', forward(groups, k))  3.88 us
    ppermute x2, waiting for transfers between devices, from_far(): return lax.ppermute(block, ('tm', 'space'), pairs)  3.87 us
    pallas_call x6, Pallas kernels, call(): pl.pallas_call(kernel, out_shape=[jax.ShapeDtypeStruct(shape, dtype) for...  3.77 us
    ppermute x2, starting transfers between devices, from_far(): return lax.ppermute(block, ('tm', 'space'), pairs)  3.55 us
    unnamed x2, local copies, waits for them, and re-layouts  0.97 us
    ppermute x2, starting transfers between devices, from_near(): return lax.ppermute(block, 'space', pairs)  0.56 us
  transfers between devices with their start and end apart: 7, of which 3 were waited for; matrix products, arithmetic and copies ran while one was open for 0% of the time, Pallas kernels for 13%

profile of v9, /device:TPU:0, one launch (start us, length us, event | category | flops | bytes accessed | tf_op | source)
XLA Modules:
  0.0 22.2 jit_solution(6011497474031399432)
XLA Ops:
  0.0 0.5 %collective-permute-start = (f32[2,8,2048]{2,1,0:T(8,128)}, f32[2,8,2048]{2,1,0:T(8,128)S(1)}, u32[]{:S(2)}, u32[]{:S(2)}) collective-permute-start(f32[2,8,2048]{2,1,0:T(8,128)} %bitcast.3), channel_id=1, source_target_pairs={{0,1},{1,0},{2,3},{3,2},{4,5},{5,4},{6,7},{7,6},{8,9},{9,8},{10,11... | collective-permute-start | bytes 393224 | tf_op jit(solution)/shard_map/ppermute | solution.py:366
  0.5 3.5 %collective-permute-start.1 = (f32[2,8,2048]{2,1,0:T(8,128)}, f32[2,8,2048]{2,1,0:T(8,128)S(1)}, u32[]{:S(2)}, u32[]{:S(2)}) collective-permute-start(f32[2,8,2048]{2,1,0:T(8,128)} %bitcast.4), channel_id=1, source_target_pairs={{0,7},{1,2},{2,1},{3,4},{4,3},{5,6},{6,5},{7,0},{8,15},{9,10},{10,... | collective-permute-start | bytes 393224 | tf_op jit(solution)/shard_map/ppermute | solution.py:377
  4.0 0.0 collective-permute-start.3
  4.0 0.0 copy-start
  4.0 1.0 %copy-done = f32[1,2,8,2048]{3,2,1,0:T(8,128)S(1)} copy-done((f32[1,2,8,2048]{3,2,1,0:T(8,128)S(1)}, f32[1,2,8,2048]{3,2,1,0:T(8,128)}, u32[]{:S(2)}) %copy-start) | copy-done | bytes 131096
  5.0 0.2 %shard_map.17 = (f32[2,8,2048]{2,1,0:T(8,128)S(1)}, f32[8,2048]{1,0:T(8,128)S(1)}, bf16[512,128]{1,0:T(8,128)(2,1)S(1)}, bf16[128,512]{1,0:T(8,128)(2,1)S(1)}) custom-call(s32[1]{0:T(128)} %bitcast.1.held_ref, f32[2,8,2048]{2,1,0:T(8,128)S(1)} %bitcast.6), custom_call_target="tpu_custom_call" | custom-call | flops 4000000 | bytes 500000 | tf_op jit(solution)/shard_map/pallas_call | solution.py:346
  5.2 0.0 collective-permute-done.near_ref
  5.3 1.2 %shard_map.18 = (f32[4,2,8,2048]{3,2,1,0:T(8,128)S(1)}, f32[4,2,8,2048]{3,2,1,0:T(8,128)S(1)}, f32[2,8,2048]{2,1,0:T(8,128)S(1)}, f32[2,8,512]{2,1,0:T(8,128)S(1)}, f32[2,8,512]{2,1,0:T(8,128)S(1)}) custom-call(f32[2,8,2048]{2,1,0:T(8,128)S(1)} %collective-permute-done.near_ref, f32[2,8,2048]{2,1,0:T(8,128)S(1)} %get-tuple-element.38.own_ref, ...), custom_call_target="tpu_custom_call" | custom-call | flops 8000000 | bytes 1000000 | tf_op jit(solution)/shard_map/pallas_call | solution.py:346
  6.4 1.6 %collective-permute-done.1.far_ref = f32[2,8,2048]{2,1,0:T(8,128)S(1)} collective-permute-done((f32[2,8,2048]{2,1,0:T(8,128)}, f32[2,8,2048]{2,1,0:T(8,128)S(1)}, u32[]{:S(2)}, u32[]{:S(2)}) %collective-permute-start.1) | collective-permute-done | bytes 131104 | tf_op jit(solution)/shard_map/ppermute | solution.py:377
  8.0 0.7 %shard_map.19 = (f32[2,8,2048]{2,1,0:T(8,128)S(1)}, f32[2,4,512]{2,1,0:T(4,128)S(1)}, f32[2,8,512]{2,1,0:T(8,128)S(1)}, f32[3,2,8,2048]{3,2,1,0:T(8,128)S(1)}, f32[8,512]{1,0:T(8,128)S(1)}) custom-call(f32[2,8,2048]{2,1,0:T(8,128)S(1)} %collective-permute-done.1.far_ref, f32[4,2,8,2048]{3,2,1,0:T(8,128)S(1)} %get-tuple-element.42.first_ref, ...), custom_call_target="tpu_custom_call" | custom-call | flops 2000000 | bytes 250000 | tf_op jit(solution)/shard_map/pallas_call | solution.py:346
  8.8 0.1 collective-permute-start.4
  8.8 2.3 %collective-permute-done.3.farther_ref = f32[2,8,2048]{2,1,0:T(8,128)S(1)} collective-permute-done((f32[2,8,2048]{2,1,0:T(8,128)}, f32[2,8,2048]{2,1,0:T(8,128)S(1)}, u32[]{:S(2)}, u32[]{:S(2)}) %collective-permute-start.3) | collective-permute-done | bytes 131104 | tf_op jit(solution)/shard_map/ppermute | solution.py:377
  11.1 0.0 collective-permute-done.4.near_ref
  11.1 0.8 %shard_map.21 = f32[2,8,512]{2,1,0:T(8,128)S(1)} custom-call(f32[2,8,2048]{2,1,0:T(8,128)S(1)} %collective-permute-done.1.far_ref, f32[3,2,8,2048]{3,2,1,0:T(8,128)S(1)} %get-tuple-element.50.trail_ref, f32[2,8,2048]{2,1,0:T(8,128)S(1)} %collective-permute-done.3.farther_ref, f32[8,512]{1,0:T(8,128)S(1)} %get-tuple-element.51.far_means_ref, ...), custom_call_target="tpu_custom_call" | custom-call | flops 2000000 | bytes 250000 | tf_op jit(solution)/shard_map/pallas_call | solution.py:346
  11.9 0.4 %collective-permute-start.5 = (f32[2,8,512]{2,1,0:T(8,128)S(1)}, f32[2,8,512]{2,1,0:T(8,128)S(1)}, u32[]{:S(2)}, u32[]{:S(2)}) collective-permute-start(f32[2,8,512]{2,1,0:T(8,128)S(1)} %shard_map.21), channel_id=1, source_target_pairs={{0,16},{8,24},{16,8},{24,0},{1,17},{9,25},{17,9},{25,1},{2,18},{10... | collective-permute-start | bytes 98312 | tf_op jit(solution)/shard_map/ppermute | solution.py:453
  12.2 3.5 %collective-permute-start.6 = (f32[2,8,512]{2,1,0:T(8,128)S(1)}, f32[2,8,512]{2,1,0:T(8,128)S(1)}, u32[]{:S(2)}, u32[]{:S(2)}) collective-permute-start(f32[2,8,512]{2,1,0:T(8,128)S(1)} %shard_map.21), channel_id=1, source_target_pairs={{0,24},{8,0},{16,8},{24,16},{1,25},{9,1},{17,9},{25,17},{2,26},{10... | collective-permute-start | bytes 98312 | tf_op jit(solution)/shard_map/ppermute | solution.py:453
  15.8 0.0 collective-permute-start.2
  15.8 5.5 %collective-permute-done.2.rest_1_ = f32[2,4,512]{2,1,0:T(4,128)S(1)} collective-permute-done((f32[2,4,512]{2,1,0:T(4,128)S(1)}, f32[2,4,512]{2,1,0:T(4,128)S(1)}, u32[]{:S(2)}, u32[]{:S(2)}) %collective-permute-start.2) | collective-permute-done | bytes 16416 | tf_op jit(solution)/shard_map/ppermute | solution.py:453
  21.3 0.8 %shard_map.20.before_hbm = f32[2,8,2048]{2,1,0:T(8,128)} custom-call(f32[2,8,2048]{2,1,0:T(8,128)S(1)} %get-tuple-element.41.kept_ref, f32[2,8,2048]{2,1,0:T(8,128)S(1)} %get-tuple-element.46.end_ref, f32[2,8,512]{2,1,0:T(8,128)S(1)} %get-tuple-element.47.ends_ref, bf16[128,512]{1,0:T(8,128)(2,1)S(1)} %get-tuple-element.48.spread_ref, ...), custom_call_target="tpu_custom_call" | custom-call | flops 1000000 | bytes 125000 | tf_op jit(solution)/shard_map/pallas_call | solution.py:346
  22.1 0.0 collective-permute-done.5.rest_2_
  22.2 0.0 collective-permute-done.6.rest_3_
  (2 shorter events, 0.0 us)
Async XLA Ops:
  0.0 5.2 %collective-permute-start = (f32[2,8,2048]{2,1,0:T(8,128)}, f32[2,8,2048]{2,1,0:T(8,128)S(1)}, u32[]{:S(2)}, u32[]{:S(2)}) collective-permute-start(f32[2,8,2048]{2,1,0:T(8,128)} %bitcast.3), channel_id=1, source_target_pairs={{0,1},{1,0},{2,3},{3,2},{4,5},{5,4},{6,7},{7,6},{8,9},{9,8},{10,11... | collective-permute-start | bytes 393224 | tf_op jit(solution)/shard_map/ppermute | solution.py:366
  0.5 7.5 %collective-permute-start.1 = (f32[2,8,2048]{2,1,0:T(8,128)}, f32[2,8,2048]{2,1,0:T(8,128)S(1)}, u32[]{:S(2)}, u32[]{:S(2)}) collective-permute-start(f32[2,8,2048]{2,1,0:T(8,128)} %bitcast.4), channel_id=1, source_target_pairs={{0,7},{1,2},{2,1},{3,4},{4,3},{5,6},{6,5},{7,0},{8,15},{9,10},{10,... | collective-permute-start | bytes 393224 | tf_op jit(solution)/shard_map/ppermute | solution.py:377
  4.0 7.1 %collective-permute-start.3 = (f32[2,8,2048]{2,1,0:T(8,128)}, f32[2,8,2048]{2,1,0:T(8,128)S(1)}, u32[]{:S(2)}, u32[]{:S(2)}) collective-permute-start(f32[2,8,2048]{2,1,0:T(8,128)} %bitcast.5), channel_id=1, source_target_pairs={{0,2},{1,7},{2,4},{3,1},{4,6},{5,3},{6,0},{7,5},{8,10},{9,15},{10,... | collective-permute-start | bytes 393224 | tf_op jit(solution)/shard_map/ppermute | solution.py:377
  4.0 1.0 %copy-start = (f32[1,2,8,2048]{3,2,1,0:T(8,128)S(1)}, f32[1,2,8,2048]{3,2,1,0:T(8,128)}, u32[]{:S(2)}) copy-start(f32[1,2,8,2048]{3,2,1,0:T(8,128)} %param.3) | copy-start | bytes 393220
  8.8 2.4 %collective-permute-start.4 = (f32[2,4,512]{2,1,0:T(4,128)S(1)}, f32[2,4,512]{2,1,0:T(4,128)S(1)}, u32[]{:S(2)}, u32[]{:S(2)}) collective-permute-start(f32[2,4,512]{2,1,0:T(4,128)S(1)} %get-tuple-element.49.rest_0_.sent_ref), channel_id=1, source_target_pairs={{0,1},{1,0},{2,3},{3,2},{4,5},{5,4},{6,7},{7,6},{8,9},{9,8},{10,11... | collective-permute-start | bytes 49160 | tf_op jit(solution)/shard_map/ppermute | solution.py:366
  11.9 10.3 %collective-permute-start.5 = (f32[2,8,512]{2,1,0:T(8,128)S(1)}, f32[2,8,512]{2,1,0:T(8,128)S(1)}, u32[]{:S(2)}, u32[]{:S(2)}) collective-permute-start(f32[2,8,512]{2,1,0:T(8,128)S(1)} %shard_map.21), channel_id=1, source_target_pairs={{0,16},{8,24},{16,8},{24,0},{1,17},{9,25},{17,9},{25,1},{2,18},{10... | collective-permute-start | bytes 98312 | tf_op jit(solution)/shard_map/ppermute | solution.py:453
  12.2 9.9 %collective-permute-start.6 = (f32[2,8,512]{2,1,0:T(8,128)S(1)}, f32[2,8,512]{2,1,0:T(8,128)S(1)}, u32[]{:S(2)}, u32[]{:S(2)}) collective-permute-start(f32[2,8,512]{2,1,0:T(8,128)S(1)} %shard_map.21), channel_id=1, source_target_pairs={{0,24},{8,0},{16,8},{24,16},{1,25},{9,1},{17,9},{25,17},{2,26},{10... | collective-permute-start | bytes 98312 | tf_op jit(solution)/shard_map/ppermute | solution.py:453
  15.8 5.5 %collective-permute-start.2 = (f32[2,4,512]{2,1,0:T(4,128)S(1)}, f32[2,4,512]{2,1,0:T(4,128)S(1)}, u32[]{:S(2)}, u32[]{:S(2)}) collective-permute-start(f32[2,4,512]{2,1,0:T(4,128)S(1)} %get-tuple-element.49.rest_0_.sent_ref), channel_id=1, source_target_pairs={{0,8},{8,16},{16,24},{24,0},{1,9},{9,17},{17,25},{25,1},{2,10},{10... | collective-permute-start | bytes 49160 | tf_op jit(solution)/shard_map/ppermute | solution.py:453

commit v10 on v9

--- a/solution.py
+++ b/solution.py
@@ -355,6 +355,10 @@
     )(*operands)
 
 
+def moved(block, axis, pairs):
+    return lax.ppermute(block, axis, pairs)
+
+
 def hold():
     at = lax.axis_index("space") % 4
     turns = jnp.where((at == 1) | (at == 2), HOLD_TURNS, 0)
@@ -363,7 +367,7 @@
 
 def from_near(block):
     pairs = [(i, i ^ 1) for i in range(lax.axis_size("space"))]
-    return lax.ppermute(block, "space", pairs)
+    return moved(block, "space", pairs)
 
 
 def from_far(block, step, among):
@@ -374,14 +378,19 @@
             away = step if (i + step) % 2 == 0 else -step
             to = (i + away) % count if t < among else i ^ 1
             pairs.append((t * count + i, t * count + to))
-    return lax.ppermute(block, ("tm", "space"), pairs)
-
-
-def forward(groups, distance):
-    pairs = [(i, (i + distance) % groups) for i in range(groups)]
+    return moved(block, ("tm", "space"), pairs)
+
+
+def forward(groups, count, distance):
+    later = [(i + distance) % groups for i in range(groups)]
     if distance == 2 and groups > 2:
-        pairs[-2:] = [(groups - 2, 1), (groups - 1, 0)]
-    return pairs
+        later[-2:] = [1, 0]
+    aside = 1 if 2 < distance == groups - 1 else -1
+    return [
+        (i * count + s, later[i] * count + (s ^ 1 if i == aside else s))
+        for i in range(groups)
+        for s in range(count)
+    ]
 
 
 def step(c_state):
@@ -450,7 +459,7 @@
         (window,) = call(functools.partial(window_kernel, depth), [window], pieces)
     held = [sent]
     for k in range(1, groups):
-        held.append(lax.ppermute(sent if k <= EXT else window, "tm", forward(groups, k)))
+        held.append(moved(sent if k <= EXT else window, ("tm", "space"), forward(groups, count, k)))
     whole = (own.shape, full)
     scratch = [pltpu.VMEM(own.shape, full), pltpu.SemaphoreType.DMA((OUT_PIECES,))]
     early = min(groups, 1 + EXT)

time: 22.4 us -> 22.4 us (level)
  no operation moved by 1% of the time
where the time goes in v10:
time: 22.4 us; the launch traced here: 22.2 us
  waiting for transfers between devices  9.41 us (42%)
  starting transfers between devices  7.99 us (36%)
  Pallas kernels  3.77 us (17%)
  local copies, waits for them, and re-layouts  0.97 us (4%)
    ppermute x7, waiting for transfers between devices, moved(): return lax.ppermute(block, axis, pairs)  9.41 us
    ppermute x7, starting transfers between devices, moved(): return lax.ppermute(block, axis, pairs)  7.99 us
    pallas_call x6, Pallas kernels, call(): pl.pallas_call(kernel, out_shape=[jax.ShapeDtypeStruct(shape, dtype) for...  3.77 us
    unnamed x2, local copies, waits for them, and re-layouts  0.97 us
  transfers between devices with their start and end apart: 7, of which 3 were waited for; matrix products, arithmetic and copies ran while one was open for 0% of the time, Pallas kernels for 13%

profile of v10, /device:TPU:0, one launch (start us, length us, event | category | flops | bytes accessed | tf_op | source)
XLA Modules:
  0.0 22.2 jit_solution(13716318379152454650)
XLA Ops:
  0.0 0.5 %collective-permute-start = (f32[2,8,2048]{2,1,0:T(8,128)}, f32[2,8,2048]{2,1,0:T(8,128)S(1)}, u32[]{:S(2)}, u32[]{:S(2)}) collective-permute-start(f32[2,8,2048]{2,1,0:T(8,128)} %bitcast.3), channel_id=1, source_target_pairs={{0,1},{1,0},{2,3},{3,2},{4,5},{5,4},{6,7},{7,6},{8,9},{9,8},{10,11... | collective-permute-start | bytes 393224 | tf_op jit(solution)/shard_map/ppermute | solution.py:359
  0.5 3.5 %collective-permute-start.1 = (f32[2,8,2048]{2,1,0:T(8,128)}, f32[2,8,2048]{2,1,0:T(8,128)S(1)}, u32[]{:S(2)}, u32[]{:S(2)}) collective-permute-start(f32[2,8,2048]{2,1,0:T(8,128)} %bitcast.4), channel_id=1, source_target_pairs={{0,7},{1,2},{2,1},{3,4},{4,3},{5,6},{6,5},{7,0},{8,15},{9,10},{10,... | collective-permute-start | bytes 393224 | tf_op jit(solution)/shard_map/ppermute | solution.py:359
  4.0 0.0 collective-permute-start.3
  4.0 0.0 copy-start
  4.0 1.0 %copy-done = f32[1,2,8,2048]{3,2,1,0:T(8,128)S(1)} copy-done((f32[1,2,8,2048]{3,2,1,0:T(8,128)S(1)}, f32[1,2,8,2048]{3,2,1,0:T(8,128)}, u32[]{:S(2)}) %copy-start) | copy-done | bytes 131096
  5.0 0.2 %shard_map.17 = (f32[2,8,2048]{2,1,0:T(8,128)S(1)}, f32[8,2048]{1,0:T(8,128)S(1)}, bf16[512,128]{1,0:T(8,128)(2,1)S(1)}, bf16[128,512]{1,0:T(8,128)(2,1)S(1)}) custom-call(s32[1]{0:T(128)} %bitcast.1.held_ref, f32[2,8,2048]{2,1,0:T(8,128)S(1)} %bitcast.6), custom_call_target="tpu_custom_call" | custom-call | flops 4000000 | bytes 500000 | tf_op jit(solution)/shard_map/pallas_call | solution.py:346
  5.2 0.0 collective-permute-done.near_ref
  5.3 1.2 %shard_map.18 = (f32[4,2,8,2048]{3,2,1,0:T(8,128)S(1)}, f32[4,2,8,2048]{3,2,1,0:T(8,128)S(1)}, f32[2,8,2048]{2,1,0:T(8,128)S(1)}, f32[2,8,512]{2,1,0:T(8,128)S(1)}, f32[2,8,512]{2,1,0:T(8,128)S(1)}) custom-call(f32[2,8,2048]{2,1,0:T(8,128)S(1)} %collective-permute-done.near_ref, f32[2,8,2048]{2,1,0:T(8,128)S(1)} %get-tuple-element.38.own_ref, ...), custom_call_target="tpu_custom_call" | custom-call | flops 8000000 | bytes 1000000 | tf_op jit(solution)/shard_map/pallas_call | solution.py:346
  6.4 1.6 %collective-permute-done.1.far_ref = f32[2,8,2048]{2,1,0:T(8,128)S(1)} collective-permute-done((f32[2,8,2048]{2,1,0:T(8,128)}, f32[2,8,2048]{2,1,0:T(8,128)S(1)}, u32[]{:S(2)}, u32[]{:S(2)}) %collective-permute-start.1) | collective-permute-done | bytes 131104 | tf_op jit(solution)/shard_map/ppermute | solution.py:359
  8.0 0.7 %shard_map.19 = (f32[2,8,2048]{2,1,0:T(8,128)S(1)}, f32[2,4,512]{2,1,0:T(4,128)S(1)}, f32[2,8,512]{2,1,0:T(8,128)S(1)}, f32[3,2,8,2048]{3,2,1,0:T(8,128)S(1)}, f32[8,512]{1,0:T(8,128)S(1)}) custom-call(f32[2,8,2048]{2,1,0:T(8,128)S(1)} %collective-permute-done.1.far_ref, f32[4,2,8,2048]{3,2,1,0:T(8,128)S(1)} %get-tuple-element.42.first_ref, ...), custom_call_target="tpu_custom_call" | custom-call | flops 2000000 | bytes 250000 | tf_op jit(solution)/shard_map/pallas_call | solution.py:346
  8.8 0.1 collective-permute-start.4
  8.8 2.3 %collective-permute-done.3.farther_ref = f32[2,8,2048]{2,1,0:T(8,128)S(1)} collective-permute-done((f32[2,8,2048]{2,1,0:T(8,128)}, f32[2,8,2048]{2,1,0:T(8,128)S(1)}, u32[]{:S(2)}, u32[]{:S(2)}) %collective-permute-start.3) | collective-permute-done | bytes 131104 | tf_op jit(solution)/shard_map/ppermute | solution.py:359
  11.1 0.0 collective-permute-done.4.near_ref
  11.1 0.8 %shard_map.21 = f32[2,8,512]{2,1,0:T(8,128)S(1)} custom-call(f32[2,8,2048]{2,1,0:T(8,128)S(1)} %collective-permute-done.1.far_ref, f32[3,2,8,2048]{3,2,1,0:T(8,128)S(1)} %get-tuple-element.50.trail_ref, f32[2,8,2048]{2,1,0:T(8,128)S(1)} %collective-permute-done.3.farther_ref, f32[8,512]{1,0:T(8,128)S(1)} %get-tuple-element.51.far_means_ref, ...), custom_call_target="tpu_custom_call" | custom-call | flops 2000000 | bytes 250000 | tf_op jit(solution)/shard_map/pallas_call | solution.py:346
  11.9 0.4 %collective-permute-start.5 = (f32[2,8,512]{2,1,0:T(8,128)S(1)}, f32[2,8,512]{2,1,0:T(8,128)S(1)}, u32[]{:S(2)}, u32[]{:S(2)}) collective-permute-start(f32[2,8,512]{2,1,0:T(8,128)S(1)} %shard_map.21), channel_id=1, source_target_pairs={{0,16},{1,17},{2,18},{3,19},{4,20},{5,21},{6,22},{7,23},{8,24},{9,... | collective-permute-start | bytes 98312 | tf_op jit(solution)/shard_map/ppermute | solution.py:359
  12.2 3.5 %collective-permute-start.6 = (f32[2,8,512]{2,1,0:T(8,128)S(1)}, f32[2,8,512]{2,1,0:T(8,128)S(1)}, u32[]{:S(2)}, u32[]{:S(2)}) collective-permute-start(f32[2,8,512]{2,1,0:T(8,128)S(1)} %shard_map.21), channel_id=1, source_target_pairs={{0,24},{1,25},{2,26},{3,27},{4,28},{5,29},{6,30},{7,31},{8,1},{9,0... | collective-permute-start | bytes 98312 | tf_op jit(solution)/shard_map/ppermute | solution.py:359
  15.8 0.0 collective-permute-start.2
  15.8 5.5 %collective-permute-done.2.rest_1_ = f32[2,4,512]{2,1,0:T(4,128)S(1)} collective-permute-done((f32[2,4,512]{2,1,0:T(4,128)S(1)}, f32[2,4,512]{2,1,0:T(4,128)S(1)}, u32[]{:S(2)}, u32[]{:S(2)}) %collective-permute-start.2) | collective-permute-done | bytes 16416 | tf_op jit(solution)/shard_map/ppermute | solution.py:359
  21.3 0.8 %shard_map.20.before_hbm = f32[2,8,2048]{2,1,0:T(8,128)} custom-call(f32[2,8,2048]{2,1,0:T(8,128)S(1)} %get-tuple-element.41.kept_ref, f32[2,8,2048]{2,1,0:T(8,128)S(1)} %get-tuple-element.46.end_ref, f32[2,8,512]{2,1,0:T(8,128)S(1)} %get-tuple-element.47.ends_ref, bf16[128,512]{1,0:T(8,128)(2,1)S(1)} %get-tuple-element.48.spread_ref, ...), custom_call_target="tpu_custom_call" | custom-call | flops 1000000 | bytes 125000 | tf_op jit(solution)/shard_map/pallas_call | solution.py:346
  22.1 0.0 collective-permute-done.5.rest_2_
  22.2 0.0 collective-permute-done.6.rest_3_
  (2 shorter events, 0.0 us)
Async XLA Ops:
  0.0 5.2 %collective-permute-start = (f32[2,8,2048]{2,1,0:T(8,128)}, f32[2,8,2048]{2,1,0:T(8,128)S(1)}, u32[]{:S(2)}, u32[]{:S(2)}) collective-permute-start(f32[2,8,2048]{2,1,0:T(8,128)} %bitcast.3), channel_id=1, source_target_pairs={{0,1},{1,0},{2,3},{3,2},{4,5},{5,4},{6,7},{7,6},{8,9},{9,8},{10,11... | collective-permute-start | bytes 393224 | tf_op jit(solution)/shard_map/ppermute | solution.py:359
  0.5 7.5 %collective-permute-start.1 = (f32[2,8,2048]{2,1,0:T(8,128)}, f32[2,8,2048]{2,1,0:T(8,128)S(1)}, u32[]{:S(2)}, u32[]{:S(2)}) collective-permute-start(f32[2,8,2048]{2,1,0:T(8,128)} %bitcast.4), channel_id=1, source_target_pairs={{0,7},{1,2},{2,1},{3,4},{4,3},{5,6},{6,5},{7,0},{8,15},{9,10},{10,... | collective-permute-start | bytes 393224 | tf_op jit(solution)/shard_map/ppermute | solution.py:359
  4.0 7.1 %collective-permute-start.3 = (f32[2,8,2048]{2,1,0:T(8,128)}, f32[2,8,2048]{2,1,0:T(8,128)S(1)}, u32[]{:S(2)}, u32[]{:S(2)}) collective-permute-start(f32[2,8,2048]{2,1,0:T(8,128)} %bitcast.5), channel_id=1, source_target_pairs={{0,2},{1,7},{2,4},{3,1},{4,6},{5,3},{6,0},{7,5},{8,10},{9,15},{10,... | collective-permute-start | bytes 393224 | tf_op jit(solution)/shard_map/ppermute | solution.py:359
  4.0 1.0 %copy-start = (f32[1,2,8,2048]{3,2,1,0:T(8,128)S(1)}, f32[1,2,8,2048]{3,2,1,0:T(8,128)}, u32[]{:S(2)}) copy-start(f32[1,2,8,2048]{3,2,1,0:T(8,128)} %param.3) | copy-start | bytes 393220
  8.8 2.4 %collective-permute-start.4 = (f32[2,4,512]{2,1,0:T(4,128)S(1)}, f32[2,4,512]{2,1,0:T(4,128)S(1)}, u32[]{:S(2)}, u32[]{:S(2)}) collective-permute-start(f32[2,4,512]{2,1,0:T(4,128)S(1)} %get-tuple-element.49.rest_0_.sent_ref), channel_id=1, source_target_pairs={{0,1},{1,0},{2,3},{3,2},{4,5},{5,4},{6,7},{7,6},{8,9},{9,8},{10,11... | collective-permute-start | bytes 49160 | tf_op jit(solution)/shard_map/ppermute | solution.py:359
  11.9 10.3 %collective-permute-start.5 = (f32[2,8,512]{2,1,0:T(8,128)S(1)}, f32[2,8,512]{2,1,0:T(8,128)S(1)}, u32[]{:S(2)}, u32[]{:S(2)}) collective-permute-start(f32[2,8,512]{2,1,0:T(8,128)S(1)} %shard_map.21), channel_id=1, source_target_pairs={{0,16},{1,17},{2,18},{3,19},{4,20},{5,21},{6,22},{7,23},{8,24},{9,... | collective-permute-start | bytes 98312 | tf_op jit(solution)/shard_map/ppermute | solution.py:359
  12.2 9.9 %collective-permute-start.6 = (f32[2,8,512]{2,1,0:T(8,128)S(1)}, f32[2,8,512]{2,1,0:T(8,128)S(1)}, u32[]{:S(2)}, u32[]{:S(2)}) collective-permute-start(f32[2,8,512]{2,1,0:T(8,128)S(1)} %shard_map.21), channel_id=1, source_target_pairs={{0,24},{1,25},{2,26},{3,27},{4,28},{5,29},{6,30},{7,31},{8,1},{9,0... | collective-permute-start | bytes 98312 | tf_op jit(solution)/shard_map/ppermute | solution.py:359
  15.8 5.5 %collective-permute-start.2 = (f32[2,4,512]{2,1,0:T(4,128)S(1)}, f32[2,4,512]{2,1,0:T(4,128)S(1)}, u32[]{:S(2)}, u32[]{:S(2)}) collective-permute-start(f32[2,4,512]{2,1,0:T(4,128)S(1)} %get-tuple-element.49.rest_0_.sent_ref), channel_id=1, source_target_pairs={{0,8},{1,9},{2,10},{3,11},{4,12},{5,13},{6,14},{7,15},{8,16},{9,17... | collective-permute-start | bytes 49160 | tf_op jit(solution)/shard_map/ppermute | solution.py:359

commit v11 on v8

--- a/solution.py
+++ b/solution.py
@@ -19,7 +19,7 @@
 LANES = 128
 VMEM = pl.BlockSpec(memory_space=pltpu.VMEM)
 ROWS = 8
-OUT_PIECES = 2
+OUT_PIECES = 1
 HOLD_TURNS = 80
 
 
@@ -352,6 +352,10 @@
     )(*operands)
 
 
+def moved(block, axis, pairs):
+    return lax.ppermute(block, axis, pairs)
+
+
 def hold():
     at = lax.axis_index("space") % 4
     turns = jnp.where((at == 1) | (at == 2), HOLD_TURNS, 0)
@@ -360,7 +364,7 @@
 
 def from_near(block):
     pairs = [(i, i ^ 1) for i in range(lax.axis_size("space"))]
-    return lax.ppermute(block, "space", pairs)
+    return moved(block, "space", pairs)
 
 
 def from_far(block, step, among):
@@ -371,14 +375,19 @@
             away = step if (i + step) % 2 == 0 else -step
             to = (i + away) % count if t < among else i ^ 1
             pairs.append((t * count + i, t * count + to))
-    return lax.ppermute(block, ("tm", "space"), pairs)
-
-
-def forward(groups, distance):
-    pairs = [(i, (i + distance) % groups) for i in range(groups)]
+    return moved(block, ("tm", "space"), pairs)
+
+
+def forward(groups, count, distance):
+    later = [(i + distance) % groups for i in range(groups)]
     if distance == 2 and groups > 2:
-        pairs[-2:] = [(groups - 2, 1), (groups - 1, 0)]
-    return pairs
+        later[-2:] = [1, 0]
+    aside = 1 if 2 < distance == groups - 1 else -1
+    return [
+        (i * count + s, later[i] * count + (s ^ 1 if i == aside else s))
+        for i in range(groups)
+        for s in range(count)
+    ]
 
 
 def step(c_state):
@@ -447,7 +456,7 @@
         (window,) = call(functools.partial(window_kernel, depth), [window], pieces)
     held = [sent]
     for k in range(1, groups):
-        held.append(lax.ppermute(sent if k <= EXT else window, "tm", forward(groups, k)))
+        held.append(moved(sent if k <= EXT else window, ("tm", "space"), forward(groups, count, k)))
     whole = (own.shape, full)
     scratch = [pltpu.VMEM(own.shape, full), pltpu.SemaphoreType.DMA((OUT_PIECES,))]
     early = min(groups, 1 + EXT)

time: 22.4 us -> 22.4 us (level)
  no operation moved by 1% of the time
where the time goes in v11:
time: 22.4 us; the launch traced here: 22.3 us
  waiting for transfers between devices  9.41 us (42%)
  starting transfers between devices  7.99 us (36%)
  Pallas kernels  3.84 us (17%)
  local copies, waits for them, and re-layouts  0.97 us (4%)
    ppermute x7, waiting for transfers between devices, moved(): return lax.ppermute(block, axis, pairs)  9.41 us
    ppermute x7, starting transfers between devices, moved(): return lax.ppermute(block, axis, pairs)  7.99 us
    pallas_call x6, Pallas kernels, call(): pl.pallas_call(kernel, out_shape=[jax.ShapeDtypeStruct(shape, dtype) for...  3.84 us
    unnamed x2, local copies, waits for them, and re-layouts  0.97 us
  transfers between devices with their start and end apart: 7, of which 3 were waited for; matrix products, arithmetic and copies ran while one was open for 0% of the time, Pallas kernels for 14%

profile of v11, /device:TPU:0, one launch (start us, length us, event | category | flops | bytes accessed | tf_op | source)
XLA Modules:
  0.0 22.3 jit_solution(8250219688305428187)
XLA Ops:
  0.0 0.5 %collective-permute-start = (f32[2,8,2048]{2,1,0:T(8,128)}, f32[2,8,2048]{2,1,0:T(8,128)S(1)}, u32[]{:S(2)}, u32[]{:S(2)}) collective-permute-start(f32[2,8,2048]{2,1,0:T(8,128)} %bitcast.3), channel_id=1, source_target_pairs={{0,1},{1,0},{2,3},{3,2},{4,5},{5,4},{6,7},{7,6},{8,9},{9,8},{10,11... | collective-permute-start | bytes 393224 | tf_op jit(solution)/shard_map/ppermute | solution.py:356
  0.5 3.5 %collective-permute-start.1 = (f32[2,8,2048]{2,1,0:T(8,128)}, f32[2,8,2048]{2,1,0:T(8,128)S(1)}, u32[]{:S(2)}, u32[]{:S(2)}) collective-permute-start(f32[2,8,2048]{2,1,0:T(8,128)} %bitcast.4), channel_id=1, source_target_pairs={{0,7},{1,2},{2,1},{3,4},{4,3},{5,6},{6,5},{7,0},{8,15},{9,10},{10,... | collective-permute-start | bytes 393224 | tf_op jit(solution)/shard_map/ppermute | solution.py:356
  4.0 0.0 collective-permute-start.3
  4.0 0.0 copy-start
  4.0 1.0 %copy-done = f32[1,2,8,2048]{3,2,1,0:T(8,128)S(1)} copy-done((f32[1,2,8,2048]{3,2,1,0:T(8,128)S(1)}, f32[1,2,8,2048]{3,2,1,0:T(8,128)}, u32[]{:S(2)}) %copy-start) | copy-done | bytes 131096
  5.0 0.2 %shard_map.17 = (f32[2,8,2048]{2,1,0:T(8,128)S(1)}, f32[8,2048]{1,0:T(8,128)S(1)}, bf16[512,128]{1,0:T(8,128)(2,1)S(1)}, bf16[128,512]{1,0:T(8,128)(2,1)S(1)}) custom-call(s32[1]{0:T(128)} %bitcast.1.held_ref, f32[2,8,2048]{2,1,0:T(8,128)S(1)} %bitcast.6), custom_call_target="tpu_custom_call" | custom-call | flops 4000000 | bytes 500000 | tf_op jit(solution)/shard_map/pallas_call | solution.py:343
  5.2 0.0 collective-permute-done.near_ref
  5.3 1.2 %shard_map.18 = (f32[4,2,8,2048]{3,2,1,0:T(8,128)S(1)}, f32[4,2,8,2048]{3,2,1,0:T(8,128)S(1)}, f32[2,8,2048]{2,1,0:T(8,128)S(1)}, f32[2,8,512]{2,1,0:T(8,128)S(1)}, f32[2,8,512]{2,1,0:T(8,128)S(1)}) custom-call(f32[2,8,2048]{2,1,0:T(8,128)S(1)} %collective-permute-done.near_ref, f32[2,8,2048]{2,1,0:T(8,128)S(1)} %get-tuple-element.38.own_ref, ...), custom_call_target="tpu_custom_call" | custom-call | flops 8000000 | bytes 1000000 | tf_op jit(solution)/shard_map/pallas_call | solution.py:343
  6.4 1.6 %collective-permute-done.1.far_ref = f32[2,8,2048]{2,1,0:T(8,128)S(1)} collective-permute-done((f32[2,8,2048]{2,1,0:T(8,128)}, f32[2,8,2048]{2,1,0:T(8,128)S(1)}, u32[]{:S(2)}, u32[]{:S(2)}) %collective-permute-start.1) | collective-permute-done | bytes 131104 | tf_op jit(solution)/shard_map/ppermute | solution.py:356
  8.0 0.7 %shard_map.19 = (f32[2,8,2048]{2,1,0:T(8,128)S(1)}, f32[2,4,512]{2,1,0:T(4,128)S(1)}, f32[2,8,512]{2,1,0:T(8,128)S(1)}, f32[3,2,8,2048]{3,2,1,0:T(8,128)S(1)}, f32[8,512]{1,0:T(8,128)S(1)}) custom-call(f32[2,8,2048]{2,1,0:T(8,128)S(1)} %collective-permute-done.1.far_ref, f32[4,2,8,2048]{3,2,1,0:T(8,128)S(1)} %get-tuple-element.42.first_ref, ...), custom_call_target="tpu_custom_call" | custom-call | flops 2000000 | bytes 250000 | tf_op jit(solution)/shard_map/pallas_call | solution.py:343
  8.8 0.1 collective-permute-start.4
  8.8 2.3 %collective-permute-done.3.farther_ref = f32[2,8,2048]{2,1,0:T(8,128)S(1)} collective-permute-done((f32[2,8,2048]{2,1,0:T(8,128)}, f32[2,8,2048]{2,1,0:T(8,128)S(1)}, u32[]{:S(2)}, u32[]{:S(2)}) %collective-permute-start.3) | collective-permute-done | bytes 131104 | tf_op jit(solution)/shard_map/ppermute | solution.py:356
  11.1 0.0 collective-permute-done.4.near_ref
  11.1 0.8 %shard_map.21 = f32[2,8,512]{2,1,0:T(8,128)S(1)} custom-call(f32[2,8,2048]{2,1,0:T(8,128)S(1)} %collective-permute-done.1.far_ref, f32[3,2,8,2048]{3,2,1,0:T(8,128)S(1)} %get-tuple-element.50.trail_ref, f32[2,8,2048]{2,1,0:T(8,128)S(1)} %collective-permute-done.3.farther_ref, f32[8,512]{1,0:T(8,128)S(1)} %get-tuple-element.51.far_means_ref, ...), custom_call_target="tpu_custom_call" | custom-call | flops 2000000 | bytes 250000 | tf_op jit(solution)/shard_map/pallas_call | solution.py:343
  11.9 0.4 %collective-permute-start.5 = (f32[2,8,512]{2,1,0:T(8,128)S(1)}, f32[2,8,512]{2,1,0:T(8,128)S(1)}, u32[]{:S(2)}, u32[]{:S(2)}) collective-permute-start(f32[2,8,512]{2,1,0:T(8,128)S(1)} %shard_map.21), channel_id=1, source_target_pairs={{0,16},{1,17},{2,18},{3,19},{4,20},{5,21},{6,22},{7,23},{8,24},{9,... | collective-permute-start | bytes 98312 | tf_op jit(solution)/shard_map/ppermute | solution.py:356
  12.2 3.5 %collective-permute-start.6 = (f32[2,8,512]{2,1,0:T(8,128)S(1)}, f32[2,8,512]{2,1,0:T(8,128)S(1)}, u32[]{:S(2)}, u32[]{:S(2)}) collective-permute-start(f32[2,8,512]{2,1,0:T(8,128)S(1)} %shard_map.21), channel_id=1, source_target_pairs={{0,24},{1,25},{2,26},{3,27},{4,28},{5,29},{6,30},{7,31},{8,1},{9,0... | collective-permute-start | bytes 98312 | tf_op jit(solution)/shard_map/ppermute | solution.py:356
  15.8 0.0 collective-permute-start.2
  15.8 5.5 %collective-permute-done.2.rest_1_ = f32[2,4,512]{2,1,0:T(4,128)S(1)} collective-permute-done((f32[2,4,512]{2,1,0:T(4,128)S(1)}, f32[2,4,512]{2,1,0:T(4,128)S(1)}, u32[]{:S(2)}, u32[]{:S(2)}) %collective-permute-start.2) | collective-permute-done | bytes 16416 | tf_op jit(solution)/shard_map/ppermute | solution.py:356
  21.3 0.9 %shard_map.20.before_hbm = f32[2,8,2048]{2,1,0:T(8,128)} custom-call(f32[2,8,2048]{2,1,0:T(8,128)S(1)} %get-tuple-element.41.kept_ref, f32[2,8,2048]{2,1,0:T(8,128)S(1)} %get-tuple-element.46.end_ref, f32[2,8,512]{2,1,0:T(8,128)S(1)} %get-tuple-element.47.ends_ref, bf16[128,512]{1,0:T(8,128)(2,1)S(1)} %get-tuple-element.48.spread_ref, ...), custom_call_target="tpu_custom_call" | custom-call | flops 1000000 | bytes 125000 | tf_op jit(solution)/shard_map/pallas_call | solution.py:343
  22.2 0.0 collective-permute-done.5.rest_2_
  22.2 0.0 collective-permute-done.6.rest_3_
  (2 shorter events, 0.0 us)
Async XLA Ops:
  0.0 5.2 %collective-permute-start = (f32[2,8,2048]{2,1,0:T(8,128)}, f32[2,8,2048]{2,1,0:T(8,128)S(1)}, u32[]{:S(2)}, u32[]{:S(2)}) collective-permute-start(f32[2,8,2048]{2,1,0:T(8,128)} %bitcast.3), channel_id=1, source_target_pairs={{0,1},{1,0},{2,3},{3,2},{4,5},{5,4},{6,7},{7,6},{8,9},{9,8},{10,11... | collective-permute-start | bytes 393224 | tf_op jit(solution)/shard_map/ppermute | solution.py:356
  0.5 7.5 %collective-permute-start.1 = (f32[2,8,2048]{2,1,0:T(8,128)}, f32[2,8,2048]{2,1,0:T(8,128)S(1)}, u32[]{:S(2)}, u32[]{:S(2)}) collective-permute-start(f32[2,8,2048]{2,1,0:T(8,128)} %bitcast.4), channel_id=1, source_target_pairs={{0,7},{1,2},{2,1},{3,4},{4,3},{5,6},{6,5},{7,0},{8,15},{9,10},{10,... | collective-permute-start | bytes 393224 | tf_op jit(solution)/shard_map/ppermute | solution.py:356
  4.0 7.1 %collective-permute-start.3 = (f32[2,8,2048]{2,1,0:T(8,128)}, f32[2,8,2048]{2,1,0:T(8,128)S(1)}, u32[]{:S(2)}, u32[]{:S(2)}) collective-permute-start(f32[2,8,2048]{2,1,0:T(8,128)} %bitcast.5), channel_id=1, source_target_pairs={{0,2},{1,7},{2,4},{3,1},{4,6},{5,3},{6,0},{7,5},{8,10},{9,15},{10,... | collective-permute-start | bytes 393224 | tf_op jit(solution)/shard_map/ppermute | solution.py:356
  4.0 1.0 %copy-start = (f32[1,2,8,2048]{3,2,1,0:T(8,128)S(1)}, f32[1,2,8,2048]{3,2,1,0:T(8,128)}, u32[]{:S(2)}) copy-start(f32[1,2,8,2048]{3,2,1,0:T(8,128)} %param.3) | copy-start | bytes 393220
  8.8 2.4 %collective-permute-start.4 = (f32[2,4,512]{2,1,0:T(4,128)S(1)}, f32[2,4,512]{2,1,0:T(4,128)S(1)}, u32[]{:S(2)}, u32[]{:S(2)}) collective-permute-start(f32[2,4,512]{2,1,0:T(4,128)S(1)} %get-tuple-element.49.rest_0_.sent_ref), channel_id=1, source_target_pairs={{0,1},{1,0},{2,3},{3,2},{4,5},{5,4},{6,7},{7,6},{8,9},{9,8},{10,11... | collective-permute-start | bytes 49160 | tf_op jit(solution)/shard_map/ppermute | solution.py:356
  11.9 10.4 %collective-permute-start.5 = (f32[2,8,512]{2,1,0:T(8,128)S(1)}, f32[2,8,512]{2,1,0:T(8,128)S(1)}, u32[]{:S(2)}, u32[]{:S(2)}) collective-permute-start(f32[2,8,512]{2,1,0:T(8,128)S(1)} %shard_map.21), channel_id=1, source_target_pairs={{0,16},{1,17},{2,18},{3,19},{4,20},{5,21},{6,22},{7,23},{8,24},{9,... | collective-permute-start | bytes 98312 | tf_op jit(solution)/shard_map/ppermute | solution.py:356
  12.2 10.0 %collective-permute-start.6 = (f32[2,8,512]{2,1,0:T(8,128)S(1)}, f32[2,8,512]{2,1,0:T(8,128)S(1)}, u32[]{:S(2)}, u32[]{:S(2)}) collective-permute-start(f32[2,8,512]{2,1,0:T(8,128)S(1)} %shard_map.21), channel_id=1, source_target_pairs={{0,24},{1,25},{2,26},{3,27},{4,28},{5,29},{6,30},{7,31},{8,1},{9,0... | collective-permute-start | bytes 98312 | tf_op jit(solution)/shard_map/ppermute | solution.py:356
  15.8 5.5 %collective-permute-start.2 = (f32[2,4,512]{2,1,0:T(4,128)S(1)}, f32[2,4,512]{2,1,0:T(4,128)S(1)}, u32[]{:S(2)}, u32[]{:S(2)}) collective-permute-start(f32[2,4,512]{2,1,0:T(4,128)S(1)} %get-tuple-element.49.rest_0_.sent_ref), channel_id=1, source_target_pairs={{0,8},{1,9},{2,10},{3,11},{4,12},{5,13},{6,14},{7,15},{8,16},{9,17... | collective-permute-start | bytes 49160 | tf_op jit(solution)/shard_map/ppermute | solution.py:356
